TPU v7x, 128 devices: a whole 4x4x4 slice. The times are simulated.
128 devices in a mesh: gx: 16 (over x, z_lo, core), gy: 8 (over z_hi, y).
Axes of the slice: x: 4, y: 4, z: 4 (z_hi: 2, z_lo: 2; z = z_hi * 2 + z_lo), core: 2. Of those that a mesh axis runs over, the one named last changes fastest.
Arguments:
- fields: float32 [5, 256, 256, 128], P(None, 'gx', 'gy'), may hold values from -6 to 6
- patch_weight: bfloat16 [2560, 512], replicated, may hold values from -0.125 to 0.125
- trainer_of: int32 [8192, 1], P(('gx', 'gy')), may hold values from 0 to 127; in each aligned block of 64 rows (0 to 63, 64 to 127, ...) at most 2 rows name the same one
- lag_index: int32 [32, 32, 16], P('gx', 'gy'), may hold values from 0 to 1
- w_in: bfloat16 [128, 512, 2048], P(('gx', 'gy')), may hold values from -0.25 to 0.25
- b_in: float32 [128, 2048], P(('gx', 'gy')), may hold values from -3 to 3
- w_out: bfloat16 [128, 2048, 512], P(('gx', 'gy')), may hold values from -0.125 to 0.125
- b_out: float32 [128, 512], P(('gx', 'gy')), may hold values from -3 to 3
Outputs:
- new_fields: float32 [5, 256, 256, 128], P(None, 'gx', 'gy')
- patch_gradient: float32 [2560, 512], replicated
- w_in_gradient: float32 [128, 512, 2048], P(('gx', 'gy'))
- b_in_gradient: float32 [128, 2048], P(('gx', 'gy'))
- w_out_gradient: float32 [128, 2048, 512], P(('gx', 'gy'))
- b_out_gradient: float32 [128, 512], P(('gx', 'gy'))
Inputs may be any that keep to these rules, and one draw needn't show every extreme that they name: `trainer_of`: among the 64 rows of one brick, no trainer is named more than 2 times.
All inputs are finite; a program needn't handle non-finite values.
Results may differ from a plain program's by a relative error of at most 0.0062.
Values may be sent and summed in bfloat16 or wider, within the bound.
No kernel may reach another device: no remote copies, remote signals or barrier semaphores. Data moves between devices by JAX's collectives and lax.ppermute only.
A program may use at most 128 MiB of HBM per device.

v0:
```python
import jax
import jax.numpy as jnp
from jax import lax
from jax.sharding import PartitionSpec as P

FIELDS = 5
PATCH = 8
STEPS = 3
EMBED = 512
BLOCK_ROWS = 2


time_step = 0.2
viscosity = 0.5
drift_x = 0.6
drift_y = -0.4
drift_z = 0.3
error_weight = 0.0625


def with_halo(x, sides, width):
    edges = {}
    for axis, dim in sides:
        count, length = (lax.axis_size(axis), x.shape[dim])
        up = [(i, (i + 1) % count) for i in range(count - 1)]
        last = lax.slice_in_dim(x, length - width, length, axis=dim)
        initial = lax.slice_in_dim(x, 0, width, axis=dim)
        edges[dim] = (
            lax.ppermute(last, axis, up),
            lax.ppermute(initial, axis, [(b, a) for a, b in up]),
        )
    done = []
    for _, dim in sides:
        low, high = edges[dim]
        around = [(width, width) if d in done else (0, 0) for d in range(x.ndim)]
        x = jnp.concatenate([jnp.pad(low, around), x, jnp.pad(high, around)], axis=dim)
        done.append(dim)
    return x


def sent_together(arrays, axis, split_dim, concat_dim, along):
    columns = [a.reshape(*a.shape[:along], -1) for a in arrays]
    both = jnp.concatenate(columns, axis=along)
    result, at, finished = (
        lax.all_to_all(both, axis, split_axis=split_dim, concat_axis=concat_dim, tiled=True),
        0,
        [],
    )
    for a, column in zip(arrays, columns):
        piece = result[..., at : at + column.shape[along]]
        finished.append(piece.reshape(*piece.shape[:along], *a.shape[along:]))
        at += column.shape[along]
    return tuple(finished)


def shifted(padded, dimension, offset):
    window = [slice(None)]
    for other in (1, 2, 3):
        window.append(slice(2, padded.shape[other] - 2))
    window[dimension] = slice(2 + offset, padded.shape[dimension] - 2 + offset)
    return padded[tuple(window)]


def tendency(padded):
    gradients = []
    laplacian = 0.0
    for dimension in (1, 2, 3):
        back_two = shifted(padded, dimension, -2)
        back_one = shifted(padded, dimension, -1)
        middle = shifted(padded, dimension, 0)
        ahead_one = shifted(padded, dimension, 1)
        ahead_two = shifted(padded, dimension, 2)
        gradients.append((back_two - 8.0 * back_one + 8.0 * ahead_one - ahead_two) / 12.0)
        laplacian = (
            laplacian
            + (-back_two + 16.0 * back_one - 30.0 * middle + 16.0 * ahead_one - ahead_two) / 12.0
        )
    carried = drift_x * gradients[0] + drift_y * gradients[1] + drift_z * gradients[2]
    divergence = gradients[0][1] + gradients[1][2] + gradients[2][3]
    acoustic = jnp.stack(
        [divergence, gradients[0][4], gradients[1][4], gradients[2][4], divergence]
    )
    return viscosity * laplacian - carried - acoustic


def contract_rows(left, right):
    return lax.dot_general(
        left, right, (((0,), (0,)), ((), ())), preferred_element_type=jnp.float32
    )


def contract_cols(left, right):
    return lax.dot_general(
        left, right, (((1,), (1,)), ((), ())), preferred_element_type=jnp.float32
    )


def trainer_step(source, target, valid, w_first, b_first, w_second, b_second):
    pre = jnp.dot(source, w_first, preferred_element_type=jnp.float32) + b_first
    hidden = jax.nn.silu(pre).astype(jnp.bfloat16)
    predict = jnp.dot(hidden, w_second, preferred_element_type=jnp.float32) + b_second
    error = (error_weight * (predict - target.astype(jnp.float32)) * valid).astype(jnp.bfloat16)
    b_second_grad = jnp.sum(error.astype(jnp.float32), axis=0)
    w_second_grad = contract_rows(hidden, error)
    back = contract_cols(error, w_second)
    sigma = jax.nn.sigmoid(pre)
    pre_grad = (back * sigma * (1.0 + pre * (1.0 - sigma))).astype(jnp.bfloat16)
    b_first_grad = jnp.sum(pre_grad.astype(jnp.float32), axis=0)
    w_first_grad = contract_rows(source, pre_grad)
    source_grad = contract_cols(pre_grad, w_first).astype(jnp.bfloat16)
    return (source_grad, w_first_grad, b_first_grad, w_second_grad, b_second_grad)


def patchify(state):
    width_x, width_y, width_z = (state.shape[1], state.shape[2], state.shape[3])
    shaped = state.reshape(
        FIELDS, width_x // PATCH, PATCH, width_y // PATCH, PATCH, width_z // PATCH, PATCH
    )
    return shaped.transpose(1, 3, 5, 0, 2, 4, 6).reshape(-1, FIELDS * PATCH**3)


def pad_third(current):
    return jnp.pad(current, ((0, 0), (0, 0), (0, 0), (2, 2)))


def advance(fields):
    states = []
    current = fields
    for counter in range(STEPS):
        padded = with_halo(current, (("gx", 1), ("gy", 2)), 2)
        current = current + time_step * tendency(pad_third(padded))
        states.append(current)
    return states


def per_device(fields, patch_weight, trainer_of, lag_index, w_in, b_in, w_out, b_out):
    states = advance(fields)
    devices = lax.axis_size("gx") * lax.axis_size("gy")
    lag_rows = lag_index.reshape(-1, 1)
    picked = patchify(states[0].astype(jnp.bfloat16))
    picked = jnp.where(lag_rows == 1, patchify(states[1].astype(jnp.bfloat16)), picked)
    target = jnp.dot(
        patchify(states[-1].astype(jnp.bfloat16)), patch_weight, preferred_element_type=jnp.float32
    ).astype(jnp.bfloat16)
    patch_count = picked.shape[0]
    block_count = patch_count // BLOCK_ROWS
    slot_count = max(2, 2 * block_count // devices)
    owners = trainer_of[:, 0]
    onehot = (owners[:, None] == jnp.arange(devices, dtype=jnp.int32)[None, :]).astype(jnp.int32)
    within_rank = jnp.sum((jnp.cumsum(onehot, axis=0) - onehot) * onehot, axis=1)
    block_slot = owners * slot_count + within_rank

    def into_slots(rows):
        width = rows.shape[1]
        blocks = rows.reshape(block_count, BLOCK_ROWS, width)
        buffer = (
            jnp.zeros((devices * slot_count, BLOCK_ROWS, width), rows.dtype)
            .at[block_slot]
            .set(blocks)
        )
        return buffer.reshape(devices, slot_count, BLOCK_ROWS, width)

    valid_send = jnp.zeros((devices * slot_count,), jnp.bfloat16).at[block_slot].set(1.0)
    valid_send = valid_send.reshape(devices, slot_count)
    source = jnp.dot(picked, patch_weight, preferred_element_type=jnp.float32).astype(jnp.bfloat16)
    got_source, got_target, got_valid = sent_together(
        (into_slots(source), into_slots(target), valid_send), ("gx", "gy"), 0, 0, 2
    )
    valid_rows = jnp.repeat(got_valid.astype(jnp.float32).reshape(-1), BLOCK_ROWS)[:, None]
    results = trainer_step(
        got_source.reshape(-1, EMBED),
        got_target.reshape(-1, EMBED),
        valid_rows,
        w_in[0],
        b_in[0],
        w_out[0],
        b_out[0],
    )
    returned = lax.all_to_all(
        results[0].reshape(devices, slot_count, BLOCK_ROWS, EMBED),
        ("gx", "gy"),
        split_axis=0,
        concat_axis=0,
        tiled=True,
    )
    source_grad = returned.reshape(devices * slot_count, BLOCK_ROWS, EMBED)[block_slot]
    partial_value = contract_rows(picked, source_grad.reshape(patch_count, EMBED))
    patch_gradient = lax.psum(partial_value, ("gx", "gy"))
    return (
        states[-1],
        patch_gradient,
        results[1][None],
        results[2][None],
        results[3][None],
        results[4][None],
    )


def solution(mesh):
    in_specs = (
        P(None, "gx", "gy", None),
        P(),
        P(("gx", "gy"), None),
        P("gx", "gy", None),
        P(("gx", "gy"), None, None),
        P(("gx", "gy"), None),
        P(("gx", "gy"), None, None),
        P(("gx", "gy"), None),
    )
    out_specs = (
        P(None, "gx", "gy", None),
        P(),
        P(("gx", "gy"), None, None),
        P(("gx", "gy"), None),
        P(("gx", "gy"), None, None),
        P(("gx", "gy"), None),
    )
    return jax.shard_map(
        per_device, mesh=mesh, in_specs=in_specs, out_specs=out_specs, check_vma=False
    )
```

profile of v0, /device:TPU:1, one launch (start us, length us, event | category | flops | bytes accessed | tf_op | source)
XLA Modules:
  0.0 482.0 jit_solution(16049055990114909716)
XLA Ops:
  8.5 4.7 collective-permute-start.2
  18.3 3.4 collective-permute-start
  33.7 4.0 fusion.57
  38.8 4.9 %collective-permute-start.6 = (f32[5,16,2,128]{3,2,1,0:T(2,128)S(1)}, f32[5,16,2,128]{3,2,1,0:T(2,128)}, u32[]{:S(2)}, u32[]{:S(2)}) collective-permute-start(f32[5,16,2,128]{3,2,1,0:T(2,128)S(1)} %get-tuple-element.34), channel_id=1, source_target_pairs={{0,1},{1,2},{2,3},{3,4},{4,5},{5,6},{6,7},{8,9},{9,10},{10,11},{11... | collective-permute-start | bytes 245768 | tf_op jit(solution)/shard_map/ppermute | solution.py:29
  51.3 14.5 %reshape.74 = bf16[5,2,8,4,8,16,8]{6,5,4,3,2,1,0:T(8,128)(2,1)} reshape(bf16[5,16,32,128]{3,2,1,0:T(8,128)(2,1)} %get-tuple-element.10) | data formatting | bytes 1310720 | tf_op jit(solution)/shard_map/reshape | solution.py:116
  65.7 13.3 %copy.21 = bf16[2,4,16,5,8,8,8]{2,1,0,6,5,4,3:T(4,128)(2,1)} copy(bf16[2,4,16,5,8,8,8]{6,2,5,1,4,0,3:T(8,128)(2,1)} %bitcast.73) | data formatting | bytes 1310720 | tf_op jit(solution)/shard_map/transpose | solution.py:119
  79.1 8.1 %reshape.76 = bf16[128,2560]{0,1:T(8,128)(2,1)} reshape(bf16[2,4,16,5,8,8,8]{2,1,0,6,5,4,3:T(4,128)(2,1)} %copy.21) | data formatting | bytes 1310720 | tf_op jit(solution)/shard_map/reshape | solution.py:119
  89.0 4.6 select_maximum_fusion.4
  96.3 3.9 fusion.55
  102.1 4.9 %collective-permute-start.10 = (f32[5,16,2,128]{3,2,1,0:T(2,128)}, f32[5,16,2,128]{3,2,1,0:T(2,128)}, u32[]{:S(2)}, u32[]{:S(2)}) collective-permute-start(f32[5,16,2,128]{3,2,1,0:T(2,128)} %get-tuple-element.30), channel_id=1, source_target_pairs={{0,1},{1,2},{2,3},{3,4},{4,5},{5,6},{6,7},{8,9},{9,10},{10,11},{11... | collective-permute-start | bytes 245768 | tf_op jit(solution)/shard_map/ppermute | solution.py:29
  108.3 3.9 collective-permute-start.8
  114.5 14.4 %reshape.73 = bf16[5,2,8,4,8,16,8]{6,5,4,3,2,1,0:T(8,128)(2,1)} reshape(bf16[5,16,32,128]{3,2,1,0:T(8,128)(2,1)} %get-tuple-element.8) | data formatting | bytes 1310720 | tf_op jit(solution)/shard_map/reshape | solution.py:116
  129.0 13.3 %copy.20 = bf16[2,4,16,5,8,8,8]{2,1,0,6,5,4,3:T(4,128)(2,1)} copy(bf16[2,4,16,5,8,8,8]{6,2,5,1,4,0,3:T(8,128)(2,1)} %bitcast.74) | data formatting | bytes 1310720 | tf_op jit(solution)/shard_map/transpose | solution.py:119
  142.3 8.1 %reshape.75 = bf16[128,2560]{0,1:T(8,128)(2,1)} reshape(bf16[2,4,16,5,8,8,8]{2,1,0,6,5,4,3:T(4,128)(2,1)} %copy.20) | data formatting | bytes 1310720 | tf_op jit(solution)/shard_map/reshape | solution.py:119
  153.2 5.4 %scatter_fusion = bf16[256,2,512]{2,1,0:T(2,128)(2,1)S(1)} fusion(bf16[256,2,512]{2,1,0:T(2,128)(2,1)S(1)} %broadcast.110.clone.1, s32[64]{0:T(128)S(1)} %fusion.50, bf16[64,2,512]{2,1,0:T(2,128)(2,1)} %reshape.97), kind=kCustom, calls=%fused_computation.1 | custom fusion | bytes 393472 | tf_op jit(solution)/shard_map/scatter | solution.py:159
  161.6 4.6 select_maximum_fusion
  169.0 4.1 fusion.53
  173.1 14.4 %reshape.78 = bf16[5,2,8,4,8,16,8]{6,5,4,3,2,1,0:T(8,128)(2,1)} reshape(bf16[5,16,32,128]{3,2,1,0:T(8,128)(2,1)} %get-tuple-element.6) | data formatting | bytes 1310720 | tf_op jit(solution)/shard_map/reshape | solution.py:116
  187.5 13.3 %copy.22 = bf16[2,4,16,5,8,8,8]{2,1,0,6,5,4,3:T(4,128)(2,1)} copy(bf16[2,4,16,5,8,8,8]{6,2,5,1,4,0,3:T(8,128)(2,1)} %bitcast.75) | data formatting | bytes 1310720 | tf_op jit(solution)/shard_map/transpose | solution.py:119
  200.8 7.5 %reshape.79 = bf16[128,2560]{0,1:T(8,128)(2,1)S(1)} reshape(bf16[2,4,16,5,8,8,8]{2,1,0,6,5,4,3:T(4,128)(2,1)} %copy.22) | data formatting | bytes 1310720 | tf_op jit(solution)/shard_map/reshape | solution.py:119
  213.9 20.5 %all-to-all-start = ((bf16[128,2,2049]{2,1,0:T(2,128)(2,1)}), bf16[128,2,2049]{2,1,0:T(2,128)(2,1)S(1)}, u32[]{:S(2)}, u32[]{:S(2)}) async-start(bf16[128,2,2049]{2,1,0:T(2,128)(2,1)} %pad_maximum_fusion.8), calls=%async_computation | async-start | bytes 2228224 | tf_op jit(solution)/shard_map/all_to_all | solution.py:45
  234.4 19.8 %all-to-all-done = bf16[128,2,2049]{2,1,0:T(2,128)(2,1)S(1)} async-done(((bf16[128,2,2049]{2,1,0:T(2,128)(2,1)}), bf16[128,2,2049]{2,1,0:T(2,128)(2,1)S(1)}, u32[]{:S(2)}, u32[]{:S(2)}) %all-to-all-start) | async-done | bytes 1049120 | tf_op jit(solution)/shard_map/all_to_all | solution.py:45
  262.7 3.0 convert_reduce_fusion
  269.4 5.0 %all-to-all-start.1 = ((bf16[128,2,2,512]{3,2,1,0:T(2,128)(2,1)}), bf16[128,2,2,512]{3,2,1,0:T(2,128)(2,1)S(1)}, u32[]{:S(2)}, u32[]{:S(2)}) async-start(bf16[128,2,2,512]{3,2,1,0:T(2,128)(2,1)} %reshape.81), calls=%async_computation.1 | async-start | bytes 1048576 | tf_op jit(solution)/shard_map/all_to_all | solution.py:179
  274.4 12.3 %broadcast_select_fusion = bf16[2,4,16,5,8,8,8]{6,2,5,1,4,0,3:T(8,128)(2,1)} fusion(pred[2,4,16]{2,1,0:T(4,128)(4,1)S(1)} %broadcast_compare_fusion, bf16[5,2,8,4,8,16,8]{6,5,4,3,2,1,0:T(8,128)(2,1)} %reshape.74, bf16[5,2,8,4,8,16,8]{6,5,4,3,2,1,0:T(8,128)(2,1)} %reshape.73), kind=kLoop, calls=%fused_computation.4 | loop fusion | flops 327680 | bytes 1966208 | tf_op jit(solution)/shard_map/jit(_where)/select_n | solution.py:141
  286.7 13.3 %copy.19 = bf16[2,4,16,5,8,8,8]{2,1,0,6,5,4,3:T(4,128)(2,1)} copy(bf16[2,4,16,5,8,8,8]{6,2,5,1,4,0,3:T(8,128)(2,1)} %broadcast_select_fusion) | data formatting | bytes 1310720 | tf_op jit(solution)/shard_map/jit(_where)/select_n | solution.py:141
  300.0 7.3 %select_n.17 = bf16[128,2560]{0,1:T(8,128)(2,1)S(1)} reshape(bf16[2,4,16,5,8,8,8]{2,1,0,6,5,4,3:T(4,128)(2,1)} %copy.19) | data formatting | bytes 1310720 | tf_op jit(solution)/shard_map/jit(_where)/select_n | solution.py:141
  308.3 3.2 fusion.65
  311.5 5.0 %convolution_bitcast_fusion.1 = f32[1,512,2048]{2,1,0:T(8,128)} fusion(bf16[512,512]{1,0:T(8,128)(2,1)S(1)} %reshape_reshape.16, bf16[512,2048]{1,0:T(8,128)(2,1)} %copy-done.11), kind=kOutput, calls=%fused_computation.23 | convolution fusion | flops 1073741824 | bytes 6815744 | tf_op jit(solution)/shard_map/dot_general | solution.py:87
  316.6 3.5 convolution_bitcast_fusion
  320.0 149.3 %all-reduce.11.cloned.1.call-done = f32[2560,512]{1,0:T(8,128)} async-done(((f32[2560,512]{1,0:T(8,128)}), f32[2560,512]{1,0:T(8,128)}) %all-reduce.11.cloned.1.call-update) | async-done | bytes 5242896 | tf_op jit(solution)/shard_map/psum | solution.py:188
  469.3 5.6 %copy.44 = f32[2560,512]{1,0:T(8,128)} copy(f32[2560,512]{1,0:T(8,128)} %all-reduce.11.cloned.1.call-done) | data formatting | bytes 10485760
  (130 shorter events, 63.8 us)
Async XLA Ops:
  7.2 143.2 %copy-start = (bf16[2560,512]{1,0:T(8,128)(2,1)S(1)}, bf16[2560,512]{1,0:T(8,128)(2,1)}, u32[]{:S(2)}) copy-start(bf16[2560,512]{1,0:T(8,128)(2,1)} %param.9) | copy-start | bytes 7864324
  8.5 15.7 %collective-permute-start.2 = (f32[5,16,2,128]{3,2,1,0:T(2,128)S(1)}, f32[5,16,2,128]{3,2,1,0:T(2,128)}, u32[]{:S(2)}, u32[]{:S(2)}) collective-permute-start(f32[5,16,2,128]{3,2,1,0:T(2,128)S(1)} %get-tuple-element.39), channel_id=1, source_target_pairs={{0,1},{1,2},{2,3},{3,4},{4,5},{5,6},{6,7},{8,9},{9,10},{10,11},{11... | collective-permute-start | bytes 245768 | tf_op jit(solution)/shard_map/ppermute | solution.py:29
  13.1 11.9 %collective-permute-start.3 = (f32[5,16,2,128]{3,2,1,0:T(2,128)S(1)}, f32[5,16,2,128]{3,2,1,0:T(2,128)}, u32[]{:S(2)}, u32[]{:S(2)}) collective-permute-start(f32[5,16,2,128]{3,2,1,0:T(2,128)S(1)} %get-tuple-element.40), channel_id=1, source_target_pairs={{1,0},{2,1},{3,2},{4,3},{5,4},{6,5},{7,6},{9,8},{10,9},{11,10},{12... | collective-permute-start | bytes 245768 | tf_op jit(solution)/shard_map/ppermute | solution.py:30
  15.5 12.4 %collective-permute-start.1 = (f32[5,2,32,128]{3,2,1,0:T(8,128)S(1)}, f32[5,2,32,128]{3,2,1,0:T(8,128)S(1)}, u32[]{:S(2)}, u32[]{:S(2)}) collective-permute-start(f32[5,2,32,128]{3,2,1,0:T(8,128)S(1)} %get-tuple-element.41), channel_id=1, source_target_pairs={{8,0},{16,8},{24,16},{32,24},{40,32},{48,40},{56,48},{64,56},{72,6... | collective-permute-start | bytes 491528 | tf_op jit(solution)/shard_map/ppermute | solution.py:30
  18.3 7.7 %collective-permute-start = (f32[5,2,32,128]{3,2,1,0:T(8,128)S(1)}, f32[5,2,32,128]{3,2,1,0:T(8,128)S(1)}, u32[]{:S(2)}, u32[]{:S(2)}) collective-permute-start(f32[5,2,32,128]{3,2,1,0:T(8,128)S(1)} %get-tuple-element.42), channel_id=1, source_target_pairs={{0,8},{8,16},{16,24},{24,32},{32,40},{40,48},{48,56},{56,64},{64,7... | collective-permute-start | bytes 491528 | tf_op jit(solution)/shard_map/ppermute | solution.py:29
  32.4 1.3 copy-start.6
  33.7 16.1 %copy-start.13 = (s32[64,1]{0,1:T(1,128)S(1)}, s32[64,1]{0,1:T(1,128)}, u32[]{:S(2)}) copy-start(s32[64,1]{0,1:T(1,128)} %param.10) | copy-start | bytes 772
  37.7 1.1 copy-start.4
  38.8 48.4 %collective-permute-start.6 = (f32[5,16,2,128]{3,2,1,0:T(2,128)S(1)}, f32[5,16,2,128]{3,2,1,0:T(2,128)}, u32[]{:S(2)}, u32[]{:S(2)}) collective-permute-start(f32[5,16,2,128]{3,2,1,0:T(2,128)S(1)} %get-tuple-element.34), channel_id=1, source_target_pairs={{0,1},{1,2},{2,3},{3,4},{4,5},{5,6},{6,7},{8,9},{9,10},{10,11},{11... | collective-permute-start | bytes 245768 | tf_op jit(solution)/shard_map/ppermute | solution.py:29
  43.7 44.4 %collective-permute-start.7 = (f32[5,16,2,128]{3,2,1,0:T(2,128)S(1)}, f32[5,16,2,128]{3,2,1,0:T(2,128)}, u32[]{:S(2)}, u32[]{:S(2)}) collective-permute-start(f32[5,16,2,128]{3,2,1,0:T(2,128)S(1)} %get-tuple-element.35), channel_id=1, source_target_pairs={{1,0},{2,1},{3,2},{4,3},{5,4},{6,5},{7,6},{9,8},{10,9},{11,10},{12... | collective-permute-start | bytes 245768 | tf_op jit(solution)/shard_map/ppermute | solution.py:30
  45.0 44.0 %collective-permute-start.4 = (f32[5,2,32,128]{3,2,1,0:T(8,128)S(1)}, f32[5,2,32,128]{3,2,1,0:T(8,128)S(1)}, u32[]{:S(2)}, u32[]{:S(2)}) collective-permute-start(f32[5,2,32,128]{3,2,1,0:T(8,128)S(1)} %get-tuple-element.32), channel_id=1, source_target_pairs={{0,8},{8,16},{16,24},{24,32},{32,40},{40,48},{48,56},{56,64},{64,7... | collective-permute-start | bytes 491528 | tf_op jit(solution)/shard_map/ppermute | solution.py:29
  47.8 41.2 %collective-permute-start.5 = (f32[5,2,32,128]{3,2,1,0:T(8,128)S(1)}, f32[5,2,32,128]{3,2,1,0:T(8,128)S(1)}, u32[]{:S(2)}, u32[]{:S(2)}) collective-permute-start(f32[5,2,32,128]{3,2,1,0:T(8,128)S(1)} %get-tuple-element.33), channel_id=1, source_target_pairs={{8,0},{16,8},{24,16},{32,24},{40,32},{48,40},{56,48},{64,56},{72,6... | collective-permute-start | bytes 491528 | tf_op jit(solution)/shard_map/ppermute | solution.py:30
  93.7 1.3 copy-start.5
  100.2 1.1 copy-start.2
  102.1 57.7 %collective-permute-start.10 = (f32[5,16,2,128]{3,2,1,0:T(2,128)}, f32[5,16,2,128]{3,2,1,0:T(2,128)}, u32[]{:S(2)}, u32[]{:S(2)}) collective-permute-start(f32[5,16,2,128]{3,2,1,0:T(2,128)} %get-tuple-element.30), channel_id=1, source_target_pairs={{0,1},{1,2},{2,3},{3,4},{4,5},{5,6},{6,7},{8,9},{9,10},{10,11},{11... | collective-permute-start | bytes 245768 | tf_op jit(solution)/shard_map/ppermute | solution.py:29
  107.0 53.7 %collective-permute-start.11 = (f32[5,16,2,128]{3,2,1,0:T(2,128)}, f32[5,16,2,128]{3,2,1,0:T(2,128)}, u32[]{:S(2)}, u32[]{:S(2)}) collective-permute-start(f32[5,16,2,128]{3,2,1,0:T(2,128)} %get-tuple-element.31), channel_id=1, source_target_pairs={{1,0},{2,1},{3,2},{4,3},{5,4},{6,5},{7,6},{9,8},{10,9},{11,10},{12... | collective-permute-start | bytes 245768 | tf_op jit(solution)/shard_map/ppermute | solution.py:30
  108.3 53.4 %collective-permute-start.8 = (f32[5,2,32,128]{3,2,1,0:T(8,128)}, f32[5,2,32,128]{3,2,1,0:T(8,128)S(1)}, u32[]{:S(2)}, u32[]{:S(2)}) collective-permute-start(f32[5,2,32,128]{3,2,1,0:T(8,128)} %get-tuple-element.28), channel_id=1, source_target_pairs={{0,8},{8,16},{16,24},{24,32},{32,40},{40,48},{48,56},{56,64},{64,7... | collective-permute-start | bytes 491528 | tf_op jit(solution)/shard_map/ppermute | solution.py:29
  112.2 49.4 %collective-permute-start.9 = (f32[5,2,32,128]{3,2,1,0:T(8,128)}, f32[5,2,32,128]{3,2,1,0:T(8,128)S(1)}, u32[]{:S(2)}, u32[]{:S(2)}) collective-permute-start(f32[5,2,32,128]{3,2,1,0:T(8,128)} %get-tuple-element.29), channel_id=1, source_target_pairs={{8,0},{16,8},{24,16},{32,24},{40,32},{48,40},{56,48},{64,56},{72,6... | collective-permute-start | bytes 491528 | tf_op jit(solution)/shard_map/ppermute | solution.py:30
  166.3 1.3 copy-start.3
  208.9 3.2 copy-start.9
  213.9 40.3 %all-to-all-start = ((bf16[128,2,2049]{2,1,0:T(2,128)(2,1)}), bf16[128,2,2049]{2,1,0:T(2,128)(2,1)S(1)}, u32[]{:S(2)}, u32[]{:S(2)}) async-start(bf16[128,2,2049]{2,1,0:T(2,128)(2,1)} %pad_maximum_fusion.8), calls=%async_computation | async-start | bytes 2228224 | tf_op jit(solution)/shard_map/all_to_all | solution.py:45
  257.7 3.1 copy-start.12
  257.7 3.1 copy-start.14
  257.7 3.1 copy-start.15
  257.7 3.1 copy-start.16
  260.7 2.0 copy-start.7
  262.7 4.4 copy-start.10
  265.8 1.4 copy-start.11
  269.4 38.0 %all-to-all-start.1 = ((bf16[128,2,2,512]{3,2,1,0:T(2,128)(2,1)}), bf16[128,2,2,512]{3,2,1,0:T(2,128)(2,1)S(1)}, u32[]{:S(2)}, u32[]{:S(2)}) async-start(bf16[128,2,2,512]{3,2,1,0:T(2,128)(2,1)} %reshape.81), calls=%async_computation.1 | async-start | bytes 1048576 | tf_op jit(solution)/shard_map/all_to_all | solution.py:179
  274.4 194.9 %all-reduce.11.cloned.1.call-start = ((), (), s32[]{:S(2)}) async-start(), calls=%async_computation.2 | async-start | bytes 10485760 | tf_op jit(solution)/shard_map/psum | solution.py:188
  311.5 5.0 %copy-start.8 = (f32[512,2048]{1,0:T(8,128)S(1)}, f32[512,2048]{1,0:T(8,128)}, u32[]{:S(2)}) copy-start(f32[512,2048]{1,0:T(8,128)} %copy-done.7) | copy-start | bytes 12582916
  469.3 5.6 %copy-start.1 = (bf16[2560,512]{1,0:T(8,128)(2,1)S(1)}, bf16[2560,512]{1,0:T(8,128)(2,1)}, u32[]{:S(2)}) copy-start(bf16[2560,512]{1,0:T(8,128)(2,1)} %param.9) | copy-start | bytes 7864324
Sparse Core Ops, SparseCore 0:
  311.6 157.6 all-reduce.10
where the time goes:
time: 490 us; the launch traced here: 482 us
  waiting for transfers between devices  169 us (34%)
  local copies, waits for them, and re-layouts  166 us (34%)
  starting transfers between devices  61.1 us (12%)
  other arithmetic  47.8 us (10%)
  matrix products  23.2 us (5%)
  between operations  15 us (3%)
    psum x1, waiting for transfers between devices, per_device(): patch_gradient = lax.psum(partial_value, ('gx', 'gy'))  149 us
    reshape x3, local copies, waits for them, and re-layouts, patchify(): state.reshape(FIELDS, width_x // PATCH, PATCH, width_y // PATCH, PATCH, w...  43.3 us
    transpose x3, local copies, waits for them, and re-layouts, patchify(): shaped.transpose(1, 3, 5, 0, 2, 4, 6).reshape(-1, FIELDS * PATCH ** 3)  40 us
    ppermute x6, starting transfers between devices, with_halo(): lax.ppermute(last, axis, up)  24.7 us
    reshape x3, local copies, waits for them, and re-layouts, patchify(): shaped.transpose(1, 3, 5, 0, 2, 4, 6).reshape(-1, FIELDS * PATCH ** 3)  23.7 us
    select_n x2, local copies, waits for them, and re-layouts, per_device(): jnp.where(lag_rows == 1, patchify(states[1].astype(jnp.bfloat16)), picked)  20.7 us
    all_to_all x1, starting transfers between devices, sent_together(): lax.all_to_all(both, axis, split_axis=split_dim, concat_axis=concat_dim,...  20.5 us
    all_to_all x1, waiting for transfers between devices, sent_together(): lax.all_to_all(both, axis, split_axis=split_dim, concat_axis=concat_dim,...  19.8 us
  transfers between devices with their start and end apart: 15, of which 2 were waited for; matrix products, arithmetic and copies ran while one was open for 28% of the time, Pallas kernels for 0%

commit v1 on v0

v1 whole, which is shorter than its diff:
```python
import functools

import jax
import jax.numpy as jnp
from jax import lax
from jax.experimental import pallas as pl
from jax.experimental.pallas import tpu as pltpu
from jax.sharding import PartitionSpec as P

FIELDS = 5
PATCH = 8
STEPS = 3
EMBED = 512
BLOCK_ROWS = 2
REACH = 2 * STEPS
LIFT = 8

time_step = 0.2
viscosity = 0.5
drift_x = 0.6
drift_y = -0.4
drift_z = 0.3
error_weight = 0.0625

SLOPE = {-2: 1.0 / 12.0, -1: -8.0 / 12.0, 1: 8.0 / 12.0, 2: -1.0 / 12.0}
BEND = {-2: -1.0 / 12.0, -1: 16.0 / 12.0, 1: 16.0 / 12.0, 2: -1.0 / 12.0}
OFFSETS = (-2, -1, 1, 2)


def own_weights(drift):
    return {k: time_step * (viscosity * BEND[k] - drift * SLOPE[k]) for k in OFFSETS}


OWN_X, OWN_Y, OWN_Z = own_weights(drift_x), own_weights(drift_y), own_weights(drift_z)
MIDDLE = 1.0 - time_step * viscosity * 3.0 * 30.0 / 12.0
PUSH = {k: -time_step * SLOPE[k] for k in OFFSETS}


def rolled(value, offset, axis):
    size = value.shape[axis]
    return pltpu.roll(value, (-offset) % size, axis)


def weighted(pieces, weights):
    total = None
    for k in OFFSETS:
        term = pieces[k] * weights[k]
        total = term if total is None else total + term
    return total


def slope_of(pieces):
    return (pieces[-1] - pieces[1]) * PUSH[-1] + (pieces[2] - pieces[-2]) * PUSH[2]


def one_row(src, row, own_z, push_z, window):
    def along(field):
        middle = src[field, row]
        xs = {k: src[field, row + k] for k in OFFSETS}
        ys = {k: rolled(middle, k, 0) for k in OFFSETS}
        zs = {k: rolled(middle, k, 1) for k in OFFSETS}
        return middle, xs, ys, zs

    def own(middle, xs, ys, zs):
        return (
            middle * MIDDLE + weighted(xs, OWN_X) + weighted(ys, OWN_Y) + weighted(zs, own_z)
        )

    cut = (lambda v: v) if window is None else (lambda v: v[window[0] : window[1]])
    parts = along(4)
    pressure = cut(own(*parts))
    px, py, pz = cut(slope_of(parts[1])), cut(slope_of(parts[2])), cut(weighted(parts[3], push_z))
    parts = along(1)
    first = cut(own(*parts)) + px
    spread = cut(slope_of(parts[1]))
    parts = along(2)
    second = cut(own(*parts)) + py
    spread = spread + cut(slope_of(parts[2]))
    parts = along(3)
    third = cut(own(*parts)) + pz
    spread = spread + cut(weighted(parts[3], push_z))
    parts = along(0)
    density = cut(own(*parts)) + spread
    return density, first, second, third, pressure + spread


def slot_rows(owner_row, owner_col, patches):
    earlier_r = lax.broadcasted_iota(jnp.int32, (patches, patches), 0)
    earlier_c = lax.broadcasted_iota(jnp.int32, (patches, patches), 1)
    same = owner_row == owner_col
    half_r, half_c = earlier_r // BLOCK_ROWS, earlier_c // BLOCK_ROWS
    return same, earlier_r, earlier_c, half_r, half_c


def target_rows(owner_row, owner_col, patches, slots, along_lanes):
    same, at_r, at_c, half_r, half_c = slot_rows(owner_row, owner_col, patches)
    if along_lanes:
        hit = same & (half_r < half_c) & (at_r % BLOCK_ROWS == 0)
        rank = jnp.sum(jnp.where(hit, 1.0, 0.0), axis=0, keepdims=True).astype(jnp.int32)
        place = lax.broadcasted_iota(jnp.int32, (1, patches), 1) % BLOCK_ROWS
        owner = owner_row
    else:
        hit = same & (half_c < half_r) & (at_c % BLOCK_ROWS == 0)
        rank = jnp.sum(jnp.where(hit, 1.0, 0.0), axis=1, keepdims=True).astype(jnp.int32)
        place = lax.broadcasted_iota(jnp.int32, (patches, 1), 0) % BLOCK_ROWS
        owner = owner_col
    return (owner * slots + rank) * BLOCK_ROWS + place


def window_kernel(
    shape,
    rows,
    slots,
    edge_ref,
    f_ref,
    xlo_ref,
    xhi_ref,
    ylo_ref,
    yhi_ref,
    lag_ref,
    own_row_ref,
    own_col_ref,
    w_ref,
    new_ref,
    picked_ref,
    send_ref,
    first_ref,
    second_ref,
    shuffle_ref,
    natural_ref,
    both_ref,
):
    wide_x, wide_y, wide_z = shape
    patches = (wide_x // PATCH) * (wide_y // PATCH) * (wide_z // PATCH)
    top_x, top_y = REACH + wide_x, LIFT + wide_y
    full_x, full_y = top_x + REACH, top_y + LIFT
    lane = lax.broadcasted_iota(jnp.int32, (1, wide_z), 1)
    inside = {k: (lane + k >= 0) & (lane + k < wide_z) for k in OFFSETS}
    own_z = {k: jnp.where(inside[k], OWN_Z[k], 0.0) for k in OFFSETS}
    push_z = {k: jnp.where(inside[k], PUSH[k], 0.0) for k in OFFSETS}

    first_ref[:, :, 0:LIFT, :] = jnp.zeros((FIELDS, full_x, LIFT, wide_z), jnp.float32)
    first_ref[:, :, top_y:full_y, :] = jnp.zeros((FIELDS, full_x, LIFT, wide_z), jnp.float32)
    first_ref[:, REACH:top_x, LIFT:top_y, :] = f_ref[...]
    first_ref[:, 0:REACH, LIFT:top_y, :] = xlo_ref[...].astype(jnp.float32)
    first_ref[:, top_x:full_x, LIFT:top_y, :] = xhi_ref[...].astype(jnp.float32)
    first_ref[:, :, LIFT - REACH : LIFT, :] = ylo_ref[...].astype(jnp.float32)
    first_ref[:, :, top_y : top_y + REACH, :] = yhi_ref[...].astype(jnp.float32)

    def clear(ref, least):
        @pl.when(edge_ref[0] == 1)
        def _():
            ref[:, least:REACH] = jnp.zeros((FIELDS, REACH - least, full_y, wide_z), jnp.float32)

        @pl.when(edge_ref[1] == 1)
        def _():
            ref[:, top_x : full_x - least] = jnp.zeros(
                (FIELDS, REACH - least, full_y, wide_z), jnp.float32
            )

        @pl.when(edge_ref[2] == 1)
        def _():
            ref[:, :, 0:LIFT] = jnp.zeros((FIELDS, full_x, LIFT, wide_z), jnp.float32)

        @pl.when(edge_ref[3] == 1)
        def _():
            ref[:, :, top_y:full_y] = jnp.zeros((FIELDS, full_x, LIFT, wide_z), jnp.float32)

    def step(src, dst, least):
        def body(row, carry):
            done = one_row(src, row, own_z, push_z, None)
            for field in range(FIELDS):
                dst[field, row] = done[field]
            return carry

        lax.fori_loop(least, full_x - least, body, 0)
        clear(dst, least)

    def last_step(src):
        def body(row, carry):
            done = one_row(src, row, own_z, push_z, (LIFT, top_y))
            for field in range(FIELDS):
                new_ref[field, row - REACH] = done[field]
            return carry

        lax.fori_loop(REACH, top_x, body, 0)

    z_count = wide_z // PATCH
    lane_r = lax.broadcasted_iota(jnp.int32, (wide_z, wide_z), 0)
    lane_c = lax.broadcasted_iota(jnp.int32, (wide_z, wide_z), 1)
    swap = jnp.where(
        (lane_r // PATCH == lane_c % z_count) & (lane_r % PATCH == lane_c // z_count), 1.0, 0.0
    ).astype(jnp.bfloat16)
    group = lax.broadcasted_iota(jnp.int32, (PATCH, wide_z), 1) // z_count

    def into_patches(load, store):
        for field in range(FIELDS):
            flat = load(field).reshape(wide_x * wide_y, wide_z)
            shuffle_ref[field] = jnp.dot(
                flat.astype(jnp.bfloat16), swap, preferred_element_type=jnp.float32
            ).reshape(wide_x, wide_y, wide_z)

        def body(at, carry):
            field, inner = at // PATCH, at % PATCH
            tiles = [
                shuffle_ref[field, px * PATCH + inner, py * PATCH : (py + 1) * PATCH]
                for px in range(wide_x // PATCH)
                for py in range(wide_y // PATCH)
            ]
            for bit in (4, 2, 1):
                low = (group & bit) == 0
                fresh = list(tiles)
                for i in range(PATCH):
                    if i & bit:
                        continue
                    a, b = tiles[i], tiles[i | bit]
                    fresh[i] = jnp.where(low, a, pltpu.roll(b, bit * z_count, 1))
                    fresh[i | bit] = jnp.where(
                        low, pltpu.roll(a, wide_z - bit * z_count, 1), b
                    )
                tiles = fresh
            for inner_z in range(PATCH):
                natural_ref[at, pl.ds(inner_z, PATCH, stride=PATCH), :] = tiles[inner_z]
            return carry

        lax.fori_loop(0, FIELDS * PATCH, body, 0, unroll=2)
        for field in range(FIELDS):
            block = natural_ref[field * PATCH : (field + 1) * PATCH]
            block = block.reshape(PATCH**3, patches).astype(jnp.bfloat16)
            store(field * PATCH**3, block)

    def keep_picked(at, block):
        picked_ref[at : at + PATCH**3, :] = block
        both_ref[at : at + PATCH**3, 0:patches] = block

    def keep_target(at, block):
        both_ref[at : at + PATCH**3, patches : 2 * patches] = block

    def chosen(field):
        one = second_ref[field, REACH:top_x, LIFT:top_y]
        two = first_ref[field, REACH:top_x, LIFT:top_y]
        one = one.reshape(wide_x // PATCH, PATCH, wide_y, wide_z)
        two = two.reshape(wide_x // PATCH, PATCH, wide_y, wide_z)
        return jnp.where(lag_ref[...][:, None] == 1.0, two, one)

    step(first_ref, second_ref, 2)
    step(second_ref, first_ref, 4)
    last_step(first_ref)
    into_patches(chosen, keep_picked)
    into_patches(lambda field: new_ref[field], keep_target)

    embedded = lax.dot_general(
        both_ref[...], w_ref[...], (((0,), (0,)), ((), ())), preferred_element_type=jnp.float32
    ).astype(jnp.bfloat16)
    at = target_rows(own_row_ref[...], own_col_ref[...], patches, slots, True)
    chosen_rows = lax.broadcasted_iota(jnp.int32, (rows, patches), 0) == at
    select = jnp.where(chosen_rows, 1.0, 0.0).astype(jnp.bfloat16)
    for half in range(2):
        send_ref[:, half * EMBED : (half + 1) * EMBED] = jnp.dot(
            select,
            embedded[half * patches : (half + 1) * patches],
            preferred_element_type=jnp.float32,
        ).astype(jnp.bfloat16)


def closing_kernel(rows, slots, own_row_ref, own_col_ref, picked_ref, back_ref, part_ref):
    patches = picked_ref.shape[1]
    at = target_rows(own_row_ref[...], own_col_ref[...], patches, slots, False)
    chosen_rows = lax.broadcasted_iota(jnp.int32, (patches, rows), 1) == at
    select = jnp.where(chosen_rows, 1.0, 0.0).astype(jnp.bfloat16)
    gradient = jnp.dot(select, back_ref[...], preferred_element_type=jnp.float32)
    part_ref[...] = jnp.dot(
        picked_ref[...], gradient.astype(jnp.bfloat16), preferred_element_type=jnp.float32
    ).astype(part_ref.dtype)


def neighbours(low_piece, high_piece, axis):
    count = lax.axis_size(axis)
    up = [(i, i + 1) for i in range(count - 1)]
    down = [(b, a) for a, b in up]
    return lax.ppermute(high_piece, axis, up), lax.ppermute(low_piece, axis, down)


def contract_rows(left, right):
    return lax.dot_general(
        left, right, (((0,), (0,)), ((), ())), preferred_element_type=jnp.float32
    )


def contract_cols(left, right):
    return lax.dot_general(
        left, right, (((1,), (1,)), ((), ())), preferred_element_type=jnp.float32
    )


def trainer_step(source, target, valid, w_first, b_first, w_second, b_second):
    pre = jnp.dot(source, w_first, preferred_element_type=jnp.float32) + b_first
    hidden = jax.nn.silu(pre).astype(jnp.bfloat16)
    predict = jnp.dot(hidden, w_second, preferred_element_type=jnp.float32) + b_second
    error = (error_weight * (predict - target.astype(jnp.float32)) * valid).astype(jnp.bfloat16)
    b_second_grad = jnp.sum(error.astype(jnp.float32), axis=0)
    w_second_grad = contract_rows(hidden, error)
    back = contract_cols(error, w_second)
    sigma = jax.nn.sigmoid(pre)
    pre_grad = (back * sigma * (1.0 + pre * (1.0 - sigma))).astype(jnp.bfloat16)
    b_first_grad = jnp.sum(pre_grad.astype(jnp.float32), axis=0)
    w_first_grad = contract_rows(source, pre_grad)
    source_grad = contract_cols(pre_grad, w_first).astype(jnp.bfloat16)
    return (source_grad, w_first_grad, b_first_grad, w_second_grad, b_second_grad)


def per_device(fields, patch_weight, trainer_of, lag_index, w_in, b_in, w_out, b_out):
    axes = ("gx", "gy")
    n_x, n_y = lax.axis_size("gx"), lax.axis_size("gy")
    devices = n_x * n_y
    _, wide_x, wide_y, wide_z = fields.shape
    patches = (wide_x // PATCH) * (wide_y // PATCH) * (wide_z // PATCH)
    blocks = patches // BLOCK_ROWS
    slots = max(2, 2 * blocks // devices)
    rows = devices * slots * BLOCK_ROWS

    everyone = lax.all_gather(trainer_of[:, 0], axes)
    xlo, xhi = neighbours(fields[:, :REACH], fields[:, wide_x - REACH :], "gx")
    y_first = jnp.concatenate([p[:, :, :REACH] for p in (xlo, fields, xhi)], axis=1)
    y_last = jnp.concatenate([p[:, :, wide_y - REACH :] for p in (xlo, fields, xhi)], axis=1)
    ylo, yhi = neighbours(y_first, y_last, "gy")

    at_x, at_y = lax.axis_index("gx"), lax.axis_index("gy")
    edges = jnp.stack([at_x == 0, at_x == n_x - 1, at_y == 0, at_y == n_y - 1]).astype(jnp.int32)
    lag = jnp.repeat(jnp.repeat(lag_index.astype(jnp.float32), PATCH, axis=1), PATCH, axis=2)
    own_patch = jnp.repeat(trainer_of[:, 0], BLOCK_ROWS)
    own_row, own_col = own_patch[None, :], own_patch[:, None]

    vmem = pl.BlockSpec(memory_space=pltpu.VMEM)
    full = (FIELDS, wide_x + 2 * REACH, wide_y + 2 * LIFT, wide_z)
    new_fields, picked, send = pl.pallas_call(
        functools.partial(window_kernel, (wide_x, wide_y, wide_z), rows, slots),
        out_shape=(
            jax.ShapeDtypeStruct(fields.shape, jnp.float32),
            jax.ShapeDtypeStruct((FIELDS * PATCH**3, patches), jnp.bfloat16),
            jax.ShapeDtypeStruct((rows, 2 * EMBED), jnp.bfloat16),
        ),
        in_specs=[pl.BlockSpec(memory_space=pltpu.SMEM)] + [vmem] * 9,
        out_specs=(vmem, vmem, vmem),
        scratch_shapes=[
            pltpu.VMEM(full, jnp.float32),
            pltpu.VMEM(full, jnp.float32),
            pltpu.VMEM((FIELDS, wide_x, wide_y, wide_z), jnp.float32),
            pltpu.VMEM((FIELDS * PATCH, PATCH * PATCH, patches), jnp.float32),
            pltpu.VMEM((FIELDS * PATCH**3, 2 * patches), jnp.bfloat16),
        ],
        compiler_params=pltpu.CompilerParams(vmem_limit_bytes=48 * 1024 * 1024),
        name="window",
    )(edges, fields, xlo, xhi, ylo, yhi, lag, own_row, own_col, patch_weight)

    got = lax.all_to_all(send.reshape(devices, -1), axes, 0, 0, tiled=True)
    got = got.reshape(rows, 2 * EMBED)
    me = at_x * n_y + at_y
    counts = jnp.sum((everyone == me).astype(jnp.int32), axis=1)
    place = lax.broadcasted_iota(jnp.int32, (devices, slots * BLOCK_ROWS), 1) // BLOCK_ROWS
    valid = (place < counts[:, None]).astype(jnp.float32).reshape(rows, 1)
    source_grad, w_in_grad, b_in_grad, w_out_grad, b_out_grad = trainer_step(
        got[:, :EMBED], got[:, EMBED:], valid, w_in[0], b_in[0], w_out[0], b_out[0]
    )
    back = lax.all_to_all(source_grad.reshape(devices, -1), axes, 0, 0, tiled=True)
    part = pl.pallas_call(
        functools.partial(closing_kernel, rows, slots),
        out_shape=jax.ShapeDtypeStruct((FIELDS * PATCH**3, EMBED), jnp.float32),
        in_specs=[vmem] * 4,
        out_specs=vmem,
        compiler_params=pltpu.CompilerParams(vmem_limit_bytes=32 * 1024 * 1024),
        name="closing",
    )(own_row, own_col, picked, back.reshape(rows, EMBED))
    patch_gradient = lax.psum(part, axes)
    return (
        new_fields,
        patch_gradient,
        w_in_grad[None],
        b_in_grad[None],
        w_out_grad[None],
        b_out_grad[None],
    )


def solution(mesh):
    in_specs = (
        P(None, "gx", "gy", None),
        P(),
        P(("gx", "gy"), None),
        P("gx", "gy", None),
        P(("gx", "gy"), None, None),
        P(("gx", "gy"), None),
        P(("gx", "gy"), None, None),
        P(("gx", "gy"), None),
    )
    out_specs = (
        P(None, "gx", "gy", None),
        P(),
        P(("gx", "gy"), None, None),
        P(("gx", "gy"), None),
        P(("gx", "gy"), None, None),
        P(("gx", "gy"), None),
    )
    return jax.shard_map(
        per_device, mesh=mesh, in_specs=in_specs, out_specs=out_specs, check_vma=False
    )
```

time: 490 us -> 407 us (0.83)
  local copies, waits for them, and re-layouts: 166 us -> 42 us
  blocking collectives: 0 us -> 90.1 us
  starting transfers between devices: 61.1 us -> 28.1 us
  Pallas kernels: 0 us -> 26.7 us
  other arithmetic: 47.8 us -> 27.8 us
  waiting for transfers between devices: 169 us -> 156 us
  matrix products: 23.2 us -> 17.9 us
    unnamed x0 -> x1, blocking collectives: none -> 70.7 us
    reshape x10 -> x6, local copies, waits for them, and re-layouts: 68.8 us -> 4.53 us  [the longest x2 1.64 us: per_device(): jnp.repeat(jnp.repeat(lag_index.astype(jnp.float32), PATCH, axis=1), PATC...]
    transpose x3 -> x0, local copies, waits for them, and re-layouts: 40 us -> none  [patchify(): shaped.transpose(1, 3, 5, 0, 2, 4, 6).reshape(-1, FIELDS * PATCH ** 3)]
    pallas_call x0 -> x2, Pallas kernels: none -> 26.7 us  [the longest x1 25.5 us: per_device(): pl.pallas_call(functools.partial(window_kernel, (wide_x, wide_y, wide_z),...]
    all_to_all x0 -> x4, other arithmetic: none -> 25.8 us  [the longest x2 16.1 us: per_device(): got = lax.all_to_all(send.reshape(devices, -1), axes, 0, 0, tiled=True)]
    ppermute x12 -> x4, starting transfers between devices: 35.6 us -> 12.1 us  [the longest x2 7.51 us: neighbours(): lax.ppermute(high_piece, axis, up)]
    select_n x2 -> x0, local copies, waits for them, and re-layouts: 20.7 us -> none  [per_device(): jnp.where(lag_rows == 1, patchify(states[1].astype(jnp.bfloat16)), picked)]
    all_to_all x2 -> x1, waiting for transfers between devices: 19.8 us -> 0.01 us  [per_device(): got = lax.all_to_all(send.reshape(devices, -1), axes, 0, 0, tiled=True)]
  transfers between devices with their start and end apart: 15 -> 6, of which waited for: 2 -> 5; matrix products, arithmetic and copies ran while one was open for 28% -> 4% of each run, Pallas kernels for 0% -> 0%
where the time goes in v1:
time: 407 us; the launch traced here: 403 us
  waiting for transfers between devices  156 us (38%)
  blocking collectives  90.1 us (22%)
  local copies, waits for them, and re-layouts  42 us (10%)
  starting transfers between devices  28.1 us (7%)
  other arithmetic  27.8 us (7%)
  Pallas kernels  26.7 us (7%)
  matrix products  17.9 us (4%)
  between operations  14.9 us (4%)
    psum x1, waiting for transfers between devices, per_device(): patch_gradient = lax.psum(part, axes)  143 us
    unnamed x1, blocking collectives  70.7 us
    pallas_call x1, Pallas kernels, per_device(): pl.pallas_call(functools.partial(window_kernel, (wide_x, wide_y, wide_z),...  25.5 us
    unnamed x53, local copies, waits for them, and re-layouts  23.9 us
    all_to_all x1, blocking collectives, per_device(): lax.all_to_all(source_grad.reshape(devices, -1), axes, 0, 0, tiled=True)  19.4 us
    all_to_all x2, other arithmetic, per_device(): got = lax.all_to_all(send.reshape(devices, -1), axes, 0, 0, tiled=True)  16.1 us
    all_to_all x1, starting transfers between devices, per_device(): got = lax.all_to_all(send.reshape(devices, -1), axes, 0, 0, tiled=True)  16 us
    all_to_all x2, other arithmetic, per_device(): lax.all_to_all(source_grad.reshape(devices, -1), axes, 0, 0, tiled=True)  9.72 us
  transfers between devices with their start and end apart: 6, of which 5 were waited for; matrix products, arithmetic and copies ran while one was open for 4% of the time, Pallas kernels for 0%

profile of v1, /device:TPU:1, one launch (start us, length us, event | category | flops | bytes accessed | tf_op | source)
XLA Modules:
  0.0 403.2 jit_solution(8242068311694449583)
XLA Ops:
  7.2 1.4 fusion.26
  8.6 3.3 collective-permute-start.1
  11.9 3.5 collective-permute-start
  16.7 3.3 collective-permute-done.1.xhi_ref
  20.9 4.6 %collective-permute-done.xlo_ref = f32[5,6,32,128]{3,2,1,0:T(8,128)S(1)} collective-permute-done((f32[5,6,32,128]{3,2,1,0:T(8,128)S(1)}, f32[5,6,32,128]{3,2,1,0:T(8,128)S(1)}, u32[]{:S(2)}, u32[]{:S(2)}) %collective-permute-start) | collective-permute-done | bytes 491552 | tf_op jit(solution)/shard_map/ppermute | solution.py:281
  27.2 4.0 collective-permute-start.2
  37.7 4.2 %collective-permute-done.3 = f32[5,28,6,128]{3,1,2,0:T(8,128)} collective-permute-done((f32[5,28,6,128]{3,1,2,0:T(8,128)}, f32[5,28,6,128]{3,1,2,0:T(8,128)}, u32[]{:S(2)}, u32[]{:S(2)}) %collective-permute-start.3) | collective-permute-done | bytes 430112 | tf_op jit(solution)/shard_map/ppermute | solution.py:281
  41.9 1.3 copy.46.yhi_ref
  45.3 25.5 %window.1 = (f32[5,16,32,128]{3,2,1,0:T(8,128)}, bf16[2560,128]{1,0:T(8,128)(2,1)S(1)}, bf16[512,1024]{1,0:T(8,128)(2,1)S(1)}) custom-call(s32[4]{0:T(128)S(1)} %add_convert_fusion.edge_ref, f32[5,16,32,128]{3,2,1,0:T(8,128)S(1)} %copy-done.2, f32[5,6,32,128]{3,2,1,0:T(8,128)S(1)} %copy-done.6, f32[5,6,32,128]{3,2,1,0:T(8,128)S(1)} %copy-done.4, ...), custom_call_target="tpu_custom_call" | custom-call | tf_op jit(solution)/shard_map/window/pallas_call | solution.py:336
  72.6 5.7 %all_to_all.16 = bf16[128,1,4096]{2,1,0:T(2,128)(2,1)} reshape(bf16[512,1024]{1,0:T(8,128)(2,1)} %copy-done.7) | data formatting | bytes 2097152 | tf_op jit(solution)/shard_map/all_to_all | solution.py:356
  78.9 8.4 %reduce.2 = bf16[128,4096]{1,0:T(8,128)(2,1)S(1)} reduce(bf16[128,1,4096]{2,1,0:T(2,128)(2,1)} %all_to_all.16, bf16[]{:T(256)} %broadcast.62), dimensions={1}, to_apply=%all_to_all.16.reduce_sub_computation | reduce | bytes 2097154 | tf_op jit(solution)/shard_map/all_to_all | solution.py:356
  87.2 1.6 reshape.95
  88.8 16.0 %all-to-all-start = ((bf16[128,2,2048]{2,1,0:T(2,128)(2,1)}), bf16[128,2,2048]{2,1,0:T(2,128)(2,1)S(1)}, u32[]{:S(2)}, u32[]{:S(2)}) async-start(bf16[128,2,2048]{2,1,0:T(2,128)(2,1)} %reshape.95), calls=%async_computation | async-start | bytes 2097152 | tf_op jit(solution)/shard_map/all_to_all | solution.py:356
  105.0 70.7 %all-reduce = s32[8192]{0:T(1024)S(1)} all-reduce(s32[8192]{0:T(1024)S(1)} %bitcast_dynamic-update-slice_fusion), channel_id=2, replica_groups=mesh['gx'=16,'gy'=8] {'gx','gy'}, use_global_device_ids=true, to_apply=%add | all-reduce | flops 8192 | bytes 65536
  176.1 3.4 reshape.96
  179.5 7.7 %reduce = bf16[128,4096]{1,0:T(8,128)(2,1)S(1)} reduce(bf16[128,1,4096]{2,1,0:T(2,128)(2,1)} %reshape.96, bf16[]{:T(256)} %constant.53), dimensions={1}, to_apply=%all_to_all.13.reduce_sub_computation | reduce | bytes 2097154 | tf_op jit(solution)/shard_map/all_to_all | solution.py:356
  187.3 1.5 reshape.78
  188.7 3.1 fusion.5
  191.9 2.0 convert_reduce_fusion.1
  193.9 3.0 convert_reduce_fusion
  196.9 1.4 copy-done.15
  199.6 1.6 all_to_all.17
  201.2 4.8 %reduce.3 = bf16[128,2048]{1,0:T(8,128)(2,1)S(1)} reduce(bf16[128,1,2048]{2,1,0:T(2,128)(2,1)} %all_to_all.17, bf16[]{:T(256)} %broadcast.62), dimensions={1}, to_apply=%all_to_all.17.reduce_sub_computation | reduce | bytes 1048578 | tf_op jit(solution)/shard_map/all_to_all | solution.py:365
  207.2 19.4 %all_to_all.20 = bf16[128,2,1024]{2,1,0:T(2,128)(2,1)S(1)} all-to-all(bf16[128,2,1024]{2,1,0:T(2,128)(2,1)} %reshape.97), channel_id=1, replica_groups=mesh['gx'=16,'gy'=8] {'gx','gy'}, dimensions={0} | all-to-all | bytes 1048576 | tf_op jit(solution)/shard_map/all_to_all | solution.py:365
  226.6 1.7 reshape.98
  228.3 4.9 %reduce.1 = bf16[128,2048]{1,0:T(8,128)(2,1)} reduce(bf16[128,1,2048]{2,1,0:T(2,128)(2,1)} %reshape.98, bf16[]{:T(256)} %constant.53), dimensions={1}, to_apply=%all_to_all.15.reduce_sub_computation | reduce | bytes 1048578 | tf_op jit(solution)/shard_map/all_to_all | solution.py:365
  233.2 1.4 reshape.79.back_ref
  235.8 2.3 copy-done.1
  239.4 5.1 %convolution_bitcast_fusion.1 = f32[1,512,2048]{2,1,0:T(8,128)} fusion(bf16[512,2048]{1,0:T(8,128)(2,1)} %copy-done.15, bf16[512,1024]{1,0:T(8,128)(2,1)S(1)} %copy-done.13), kind=kOutput, calls=%fused_computation.5 | convolution fusion | flops 1073741824 | bytes 6815744 | tf_op jit(solution)/shard_map/dot_general | solution.py:285
  244.5 3.5 convolution_bitcast_fusion
  247.9 142.6 %all-reduce.3.cloned.1.call-done = f32[2560,512]{1,0:T(8,128)} async-done(((f32[2560,512]{1,0:T(8,128)}), f32[2560,512]{1,0:T(8,128)}) %all-reduce.3.cloned.1.call-update) | async-done | bytes 5242896 | tf_op jit(solution)/shard_map/psum | solution.py:374
  390.5 5.4 %copy.56 = f32[2560,512]{1,0:T(8,128)} copy(f32[2560,512]{1,0:T(8,128)} %all-reduce.3.cloned.1.call-done) | data formatting | bytes 10485760
  (81 shorter events, 20.2 us)
Async XLA Ops:
  7.2 184.7 %copy-start = (bf16[1,2048,512]{2,1,0:T(8,128)(2,1)S(1)}, bf16[1,2048,512]{2,1,0:T(8,128)(2,1)}, u32[]{:S(2)}) copy-start(bf16[1,2048,512]{2,1,0:T(8,128)(2,1)} %param.14) | copy-start | bytes 6291460
  7.2 9.5 %copy-start.16 = (s32[2,4,16]{2,1,0:T(4,128)S(1)}, s32[2,4,16]{2,1,0:T(4,128)}, u32[]{:S(2)}) copy-start(s32[2,4,16]{2,1,0:T(4,128)} %param.11) | copy-start | bytes 1540
  7.2 26.2 %copy-start.17 = (s32[64,1]{0,1:T(1,128)S(1)}, s32[64,1]{0,1:T(1,128)}, u32[]{:S(2)}) copy-start(s32[64,1]{0,1:T(1,128)} %param.10) | copy-start | bytes 772
  8.6 11.4 %collective-permute-start.1 = (f32[5,6,32,128]{3,2,1,0:T(8,128)S(1)}, f32[5,6,32,128]{3,2,1,0:T(8,128)S(1)}, u32[]{:S(2)}, u32[]{:S(2)}) collective-permute-start(f32[5,6,32,128]{3,2,1,0:T(8,128)S(1)} %get-tuple-element.14), channel_id=1, source_target_pairs={{8,0},{16,8},{24,16},{32,24},{40,32},{48,40},{56,48},{64,56},{72,6... | collective-permute-start | bytes 1474568 | tf_op jit(solution)/shard_map/ppermute | solution.py:281
  11.9 13.5 %collective-permute-start = (f32[5,6,32,128]{3,2,1,0:T(8,128)S(1)}, f32[5,6,32,128]{3,2,1,0:T(8,128)S(1)}, u32[]{:S(2)}, u32[]{:S(2)}) collective-permute-start(f32[5,6,32,128]{3,2,1,0:T(8,128)S(1)} %get-tuple-element.15), channel_id=1, source_target_pairs={{0,8},{8,16},{16,24},{24,32},{32,40},{40,48},{48,56},{56,64},{64,7... | collective-permute-start | bytes 1474568 | tf_op jit(solution)/shard_map/ppermute | solution.py:281
  16.6 26.6 %copy-start.2 = (f32[5,16,32,128]{3,2,1,0:T(8,128)S(1)}, f32[5,16,32,128]{3,2,1,0:T(8,128)}, u32[]{:S(2)}) copy-start(f32[5,16,32,128]{3,2,1,0:T(8,128)} %f_ref.1) | copy-start | bytes 3932164
  20.1 0.8 copy-start.3
  25.5 0.8 copy-start.5
  27.2 9.3 %collective-permute-start.2 = (f32[5,28,6,128]{3,1,2,0:T(8,128)}, f32[5,28,6,128]{3,1,2,0:T(8,128)}, u32[]{:S(2)}, u32[]{:S(2)}) collective-permute-start(f32[5,28,6,128]{3,1,2,0:T(8,128)} %pad_maximum_fusion), channel_id=1, source_target_pairs={{0,1},{1,2},{2,3},{3,4},{4,5},{5,6},{6,7},{8,9},{9,10},{10,11},{11... | collective-permute-start | bytes 1290248 | tf_op jit(solution)/shard_map/ppermute | solution.py:281
  32.1 9.9 %collective-permute-start.3 = (f32[5,28,6,128]{3,1,2,0:T(8,128)}, f32[5,28,6,128]{3,1,2,0:T(8,128)}, u32[]{:S(2)}, u32[]{:S(2)}) collective-permute-start(f32[5,28,6,128]{3,1,2,0:T(8,128)} %pad_maximum_fusion.1), channel_id=1, source_target_pairs={{1,0},{2,1},{3,2},{4,3},{5,4},{6,5},{7,6},{9,8},{10,9},{11,10},{12... | collective-permute-start | bytes 1290248 | tf_op jit(solution)/shard_map/ppermute | solution.py:281
  43.2 1.0 copy-start.4
  44.3 1.0 copy-start.6
  70.8 1.0 copy-start.7
  71.8 0.8 copy-start.8
  88.8 87.3 %all-to-all-start = ((bf16[128,2,2048]{2,1,0:T(2,128)(2,1)}), bf16[128,2,2048]{2,1,0:T(2,128)(2,1)S(1)}, u32[]{:S(2)}, u32[]{:S(2)}) async-start(bf16[128,2,2048]{2,1,0:T(2,128)(2,1)} %reshape.95), calls=%async_computation | async-start | bytes 2097152 | tf_op jit(solution)/shard_map/all_to_all | solution.py:356
  104.8 285.8 %all-reduce.3.cloned.1.call-start = ((), (), s32[]{:S(2)}) async-start(), calls=%async_computation.2 | async-start | bytes 10485760 | tf_op jit(solution)/shard_map/psum | solution.py:374
  187.3 4.6 %copy-start.18 = (f32[1,2048]{1,0:T(1,128)S(1)}, f32[1,2048]{1,0:T(1,128)}, u32[]{:S(2)}) copy-start(f32[1,2048]{1,0:T(1,128)} %param.13) | copy-start | bytes 24580
  187.3 4.6 %copy-start.19 = (f32[1,512]{1,0:T(1,128)S(1)}, f32[1,512]{1,0:T(1,128)}, u32[]{:S(2)}) copy-start(f32[1,512]{1,0:T(1,128)} %param.15) | copy-start | bytes 6148
  188.7 3.1 copy-start.12
  191.8 2.0 copy-start.10
  193.9 3.0 copy-start.20
  193.9 4.4 %copy-start.14 = (bf16[1,512,2048]{2,1,0:T(8,128)(2,1)S(1)}, bf16[1,512,2048]{2,1,0:T(8,128)(2,1)}, u32[]{:S(2)}) copy-start(bf16[1,512,2048]{2,1,0:T(8,128)(2,1)} %param.12) | copy-start | bytes 6291460
  196.9 1.4 copy-start.15
  201.2 33.4 %copy-start.9 = (bf16[2560,128]{1,0:T(8,128)(2,1)S(1)}, bf16[2560,128]{1,0:T(8,128)(2,1)}, u32[]{:S(2)}) copy-start(bf16[2560,128]{1,0:T(8,128)(2,1)} %copy-done.8) | copy-start | bytes 1966084
  235.8 2.4 copy-start.1
  238.2 1.2 copy-start.13
  239.4 5.1 %copy-start.11 = (f32[512,2048]{1,0:T(8,128)S(1)}, f32[512,2048]{1,0:T(8,128)}, u32[]{:S(2)}) copy-start(f32[512,2048]{1,0:T(8,128)} %copy-done.10) | copy-start | bytes 12582916
  239.4 5.1 %copy-start.21 = (bf16[512,512]{1,0:T(8,128)(2,1)S(1)}, bf16[512,512]{1,0:T(8,128)(2,1)}, u32[]{:S(2)}) copy-start(bf16[512,512]{1,0:T(8,128)(2,1)} %copy-done.20) | copy-start | bytes 1572868
Sparse Core Ops, SparseCore 0:
  238.3 152.1 all-reduce.2

commit v2 on v1

--- a/solution.py
+++ b/solution.py
@@ -14,6 +14,8 @@
 BLOCK_ROWS = 2
 REACH = 2 * STEPS
 LIFT = 8
+EMPTY = 1.0e30
+FULL_BELOW = 1.0e29
 
 time_step = 0.2
 viscosity = 0.5
@@ -104,7 +106,7 @@
         rank = jnp.sum(jnp.where(hit, 1.0, 0.0), axis=1, keepdims=True).astype(jnp.int32)
         place = lax.broadcasted_iota(jnp.int32, (patches, 1), 0) % BLOCK_ROWS
         owner = owner_col
-    return (owner * slots + rank) * BLOCK_ROWS + place
+    return owner, rank * BLOCK_ROWS + place
 
 
 def window_kernel(
@@ -122,7 +124,8 @@
     own_col_ref,
     w_ref,
     new_ref,
-    picked_ref,
+    keep_ref,
+    give_ref,
     send_ref,
     first_ref,
     second_ref,
@@ -139,13 +142,11 @@
     own_z = {k: jnp.where(inside[k], OWN_Z[k], 0.0) for k in OFFSETS}
     push_z = {k: jnp.where(inside[k], PUSH[k], 0.0) for k in OFFSETS}
 
-    first_ref[:, :, 0:LIFT, :] = jnp.zeros((FIELDS, full_x, LIFT, wide_z), jnp.float32)
-    first_ref[:, :, top_y:full_y, :] = jnp.zeros((FIELDS, full_x, LIFT, wide_z), jnp.float32)
     first_ref[:, REACH:top_x, LIFT:top_y, :] = f_ref[...]
     first_ref[:, 0:REACH, LIFT:top_y, :] = xlo_ref[...].astype(jnp.float32)
     first_ref[:, top_x:full_x, LIFT:top_y, :] = xhi_ref[...].astype(jnp.float32)
-    first_ref[:, :, LIFT - REACH : LIFT, :] = ylo_ref[...].astype(jnp.float32)
-    first_ref[:, :, top_y : top_y + REACH, :] = yhi_ref[...].astype(jnp.float32)
+    first_ref[:, :, 0:LIFT, :] = ylo_ref[...].astype(jnp.float32)
+    first_ref[:, :, top_y:full_y, :] = yhi_ref[...].astype(jnp.float32)
 
     def clear(ref, least):
         @pl.when(edge_ref[0] == 1)
@@ -230,7 +231,6 @@
             store(field * PATCH**3, block)
 
     def keep_picked(at, block):
-        picked_ref[at : at + PATCH**3, :] = block
         both_ref[at : at + PATCH**3, 0:patches] = block
 
     def keep_target(at, block):
@@ -252,26 +252,67 @@
     embedded = lax.dot_general(
         both_ref[...], w_ref[...], (((0,), (0,)), ((), ())), preferred_element_type=jnp.float32
     ).astype(jnp.bfloat16)
-    at = target_rows(own_row_ref[...], own_col_ref[...], patches, slots, True)
-    chosen_rows = lax.broadcasted_iota(jnp.int32, (rows, patches), 0) == at
-    select = jnp.where(chosen_rows, 1.0, 0.0).astype(jnp.bfloat16)
-    for half in range(2):
-        send_ref[:, half * EMBED : (half + 1) * EMBED] = jnp.dot(
-            select,
-            embedded[half * patches : (half + 1) * patches],
-            preferred_element_type=jnp.float32,
-        ).astype(jnp.bfloat16)
-
-
-def closing_kernel(rows, slots, own_row_ref, own_col_ref, picked_ref, back_ref, part_ref):
-    patches = picked_ref.shape[1]
-    at = target_rows(own_row_ref[...], own_col_ref[...], patches, slots, False)
+    half = both_ref.shape[0] // 2
+    mine = pl.multiple_of(edge_ref[4] * half, half)
+    keep_ref[...] = both_ref[pl.ds(mine, half), 0:patches]
+    give_ref[...] = both_ref[pl.ds(half - mine, half), 0:patches]
+    owner, slot = target_rows(own_row_ref[...], own_col_ref[...], patches, slots, True)
+    per = slots * BLOCK_ROWS
+    row = lax.broadcasted_iota(jnp.int32, (rows, patches), 0)
+    source_at = owner * (2 * per) + slot
+    is_source = row == source_at
+    is_target = row == source_at + per
+    source_pick = jnp.where(is_source, 1.0, 0.0).astype(jnp.bfloat16)
+    target_pick = jnp.where(is_target, 1.0, 0.0)
+    filled = jnp.sum(target_pick, axis=1, keepdims=True)
+    target_half = (lax.broadcasted_iota(jnp.int32, (rows, 1), 0) // per) % 2 == 1
+    marker = jnp.where(target_half & (filled == 0.0), EMPTY, 0.0)
+    placed = jnp.dot(source_pick, embedded[0:patches], preferred_element_type=jnp.float32)
+    placed = placed + jnp.dot(
+        target_pick.astype(jnp.bfloat16),
+        embedded[patches : 2 * patches],
+        preferred_element_type=jnp.float32,
+    )
+    send_ref[...] = (placed + marker).astype(jnp.bfloat16)
+
+
+def gather_kernel(rows, slots, own_row_ref, own_col_ref, back_ref, out_ref):
+    patches = own_row_ref.shape[1]
+    owner, slot = target_rows(own_row_ref[...], own_col_ref[...], patches, slots, False)
+    at = owner * (slots * BLOCK_ROWS) + slot
     chosen_rows = lax.broadcasted_iota(jnp.int32, (patches, rows), 1) == at
     select = jnp.where(chosen_rows, 1.0, 0.0).astype(jnp.bfloat16)
-    gradient = jnp.dot(select, back_ref[...], preferred_element_type=jnp.float32)
-    part_ref[...] = jnp.dot(
-        picked_ref[...], gradient.astype(jnp.bfloat16), preferred_element_type=jnp.float32
-    ).astype(part_ref.dtype)
+    out_ref[...] = jnp.dot(
+        select, back_ref[...], preferred_element_type=jnp.float32
+    ).astype(jnp.bfloat16)
+
+
+def part_kernel(keep_ref, got_ref, own_grad_ref, other_grad_ref, part_ref):
+    half = keep_ref.shape[0]
+    width = part_ref.shape[1]
+    total = jnp.dot(keep_ref[...], own_grad_ref[...], preferred_element_type=jnp.float32)
+    total = total + jnp.dot(
+        got_ref[...], other_grad_ref[...], preferred_element_type=jnp.float32
+    )
+    for side in range(EMBED // width):
+        part_ref[side * half : (side + 1) * half, :] = total[
+            :, side * width : (side + 1) * width
+        ].astype(jnp.bfloat16)
+
+
+def sum_kernel(parts_ref, copies_ref):
+    total = jnp.sum(parts_ref[...].astype(jnp.float32), axis=0).astype(jnp.bfloat16)
+    copies_ref[...] = jnp.broadcast_to(total[None], copies_ref.shape)
+
+
+def spread_kernel(core_ref, own_ref, other_ref, out_ref):
+    half, width = out_ref.shape[0] // 2, own_ref.shape[1]
+    mine = pl.multiple_of(core_ref[0] * half, half)
+    for side in range(EMBED // width):
+        lanes = slice(side * width, (side + 1) * width)
+        rows = slice(side * half, (side + 1) * half)
+        out_ref[pl.ds(mine, half), lanes] = own_ref[rows].astype(jnp.float32)
+        out_ref[pl.ds(half - mine, half), lanes] = other_ref[rows].astype(jnp.float32)
 
 
 def neighbours(low_piece, high_piece, axis):
@@ -293,11 +334,13 @@
     )
 
 
-def trainer_step(source, target, valid, w_first, b_first, w_second, b_second):
+def trainer_step(source, target, w_first, b_first, w_second, b_second):
     pre = jnp.dot(source, w_first, preferred_element_type=jnp.float32) + b_first
     hidden = jax.nn.silu(pre).astype(jnp.bfloat16)
     predict = jnp.dot(hidden, w_second, preferred_element_type=jnp.float32) + b_second
-    error = (error_weight * (predict - target.astype(jnp.float32)) * valid).astype(jnp.bfloat16)
+    wanted = target.astype(jnp.float32)
+    error = jnp.where(wanted < FULL_BELOW, error_weight * (predict - wanted), 0.0)
+    error = error.astype(jnp.bfloat16)
     b_second_grad = jnp.sum(error.astype(jnp.float32), axis=0)
     w_second_grad = contract_rows(hidden, error)
     back = contract_cols(error, w_second)
@@ -317,61 +360,105 @@
     patches = (wide_x // PATCH) * (wide_y // PATCH) * (wide_z // PATCH)
     blocks = patches // BLOCK_ROWS
     slots = max(2, 2 * blocks // devices)
-    rows = devices * slots * BLOCK_ROWS
-
-    everyone = lax.all_gather(trainer_of[:, 0], axes)
-    xlo, xhi = neighbours(fields[:, :REACH], fields[:, wide_x - REACH :], "gx")
-    y_first = jnp.concatenate([p[:, :, :REACH] for p in (xlo, fields, xhi)], axis=1)
-    y_last = jnp.concatenate([p[:, :, wide_y - REACH :] for p in (xlo, fields, xhi)], axis=1)
+    per = slots * BLOCK_ROWS
+    features = FIELDS * PATCH**3
+
+    narrow = fields.astype(jnp.bfloat16)
+    xlo, xhi = neighbours(narrow[:, :REACH], narrow[:, wide_x - REACH :], "gx")
+    y_first = jnp.concatenate([p[:, :, :LIFT] for p in (xlo, narrow, xhi)], axis=1)
+    y_last = jnp.concatenate([p[:, :, wide_y - LIFT :] for p in (xlo, narrow, xhi)], axis=1)
     ylo, yhi = neighbours(y_first, y_last, "gy")
 
     at_x, at_y = lax.axis_index("gx"), lax.axis_index("gy")
-    edges = jnp.stack([at_x == 0, at_x == n_x - 1, at_y == 0, at_y == n_y - 1]).astype(jnp.int32)
+    core = at_x % 2
+    edges = jnp.stack(
+        [at_x == 0, at_x == n_x - 1, at_y == 0, at_y == n_y - 1, core == 1]
+    ).astype(jnp.int32)
     lag = jnp.repeat(jnp.repeat(lag_index.astype(jnp.float32), PATCH, axis=1), PATCH, axis=2)
     own_patch = jnp.repeat(trainer_of[:, 0], BLOCK_ROWS)
     own_row, own_col = own_patch[None, :], own_patch[:, None]
 
     vmem = pl.BlockSpec(memory_space=pltpu.VMEM)
+    smem = pl.BlockSpec(memory_space=pltpu.SMEM)
+    grant = pltpu.CompilerParams(vmem_limit_bytes=32 * 1024 * 1024)
     full = (FIELDS, wide_x + 2 * REACH, wide_y + 2 * LIFT, wide_z)
-    new_fields, picked, send = pl.pallas_call(
-        functools.partial(window_kernel, (wide_x, wide_y, wide_z), rows, slots),
+    new_fields, keep, give, send = pl.pallas_call(
+        functools.partial(window_kernel, (wide_x, wide_y, wide_z), 2 * devices * per, slots),
         out_shape=(
             jax.ShapeDtypeStruct(fields.shape, jnp.float32),
-            jax.ShapeDtypeStruct((FIELDS * PATCH**3, patches), jnp.bfloat16),
-            jax.ShapeDtypeStruct((rows, 2 * EMBED), jnp.bfloat16),
+            jax.ShapeDtypeStruct((features // 2, patches), jnp.bfloat16),
+            jax.ShapeDtypeStruct((features // 2, patches), jnp.bfloat16),
+            jax.ShapeDtypeStruct((2 * devices * per, EMBED), jnp.bfloat16),
         ),
-        in_specs=[pl.BlockSpec(memory_space=pltpu.SMEM)] + [vmem] * 9,
-        out_specs=(vmem, vmem, vmem),
+        in_specs=[smem] + [vmem] * 9,
+        out_specs=(vmem, vmem, vmem, vmem),
         scratch_shapes=[
             pltpu.VMEM(full, jnp.float32),
             pltpu.VMEM(full, jnp.float32),
             pltpu.VMEM((FIELDS, wide_x, wide_y, wide_z), jnp.float32),
             pltpu.VMEM((FIELDS * PATCH, PATCH * PATCH, patches), jnp.float32),
-            pltpu.VMEM((FIELDS * PATCH**3, 2 * patches), jnp.bfloat16),
+            pltpu.VMEM((features, 2 * patches), jnp.bfloat16),
         ],
         compiler_params=pltpu.CompilerParams(vmem_limit_bytes=48 * 1024 * 1024),
         name="window",
     )(edges, fields, xlo, xhi, ylo, yhi, lag, own_row, own_col, patch_weight)
 
-    got = lax.all_to_all(send.reshape(devices, -1), axes, 0, 0, tiled=True)
-    got = got.reshape(rows, 2 * EMBED)
-    me = at_x * n_y + at_y
-    counts = jnp.sum((everyone == me).astype(jnp.int32), axis=1)
-    place = lax.broadcasted_iota(jnp.int32, (devices, slots * BLOCK_ROWS), 1) // BLOCK_ROWS
-    valid = (place < counts[:, None]).astype(jnp.float32).reshape(rows, 1)
+    pairs = [(i, i ^ 1) for i in range(n_x)]
+    groups = [
+        [x * n_y + y for x in range(n_x) for y in range(n_y) if x % 2 == c] for c in range(2)
+    ]
+    members = devices // 2
+    got_picked = lax.ppermute(give, "gx", pairs)
+    got = lax.all_to_all(send.reshape(devices, 2 * per, EMBED), axes, 0, 0, tiled=True)
     source_grad, w_in_grad, b_in_grad, w_out_grad, b_out_grad = trainer_step(
-        got[:, :EMBED], got[:, EMBED:], valid, w_in[0], b_in[0], w_out[0], b_out[0]
-    )
-    back = lax.all_to_all(source_grad.reshape(devices, -1), axes, 0, 0, tiled=True)
-    part = pl.pallas_call(
-        functools.partial(closing_kernel, rows, slots),
-        out_shape=jax.ShapeDtypeStruct((FIELDS * PATCH**3, EMBED), jnp.float32),
+        got[:, :per].reshape(devices * per, EMBED),
+        got[:, per:].reshape(devices * per, EMBED),
+        w_in[0],
+        b_in[0],
+        w_out[0],
+        b_out[0],
+    )
+    back = lax.all_to_all(source_grad.reshape(devices, per, EMBED), axes, 0, 0, tiled=True)
+    own_grad = pl.pallas_call(
+        functools.partial(gather_kernel, devices * per, slots),
+        out_shape=jax.ShapeDtypeStruct((patches, EMBED), jnp.bfloat16),
+        in_specs=[vmem] * 3,
+        out_specs=vmem,
+        name="gather",
+    )(own_row, own_col, back.reshape(devices * per, EMBED))
+    other_grad = lax.ppermute(own_grad, "gx", pairs)
+    width = EMBED // 2
+    piece = features // members
+    parts = pl.pallas_call(
+        part_kernel,
+        out_shape=jax.ShapeDtypeStruct((features, width), jnp.bfloat16),
         in_specs=[vmem] * 4,
         out_specs=vmem,
-        compiler_params=pltpu.CompilerParams(vmem_limit_bytes=32 * 1024 * 1024),
-        name="closing",
-    )(own_row, own_col, picked, back.reshape(rows, EMBED))
-    patch_gradient = lax.psum(part, axes)
+        compiler_params=grant,
+        name="part",
+    )(keep, got_picked, own_grad, other_grad)
+    parts = lax.all_to_all(
+        parts.reshape(members, piece, width), axes, 0, 0, axis_index_groups=groups, tiled=True
+    )
+    copies = pl.pallas_call(
+        sum_kernel,
+        out_shape=jax.ShapeDtypeStruct((members, piece, width), jnp.bfloat16),
+        in_specs=[vmem],
+        out_specs=vmem,
+        compiler_params=grant,
+        name="total",
+    )(parts)
+    own_half = lax.all_to_all(copies, axes, 0, 0, axis_index_groups=groups, tiled=True)
+    own_half = own_half.reshape(features, width)
+    other_half = lax.ppermute(own_half, "gx", pairs)
+    patch_gradient = pl.pallas_call(
+        spread_kernel,
+        out_shape=jax.ShapeDtypeStruct((features, EMBED), jnp.float32),
+        in_specs=[smem, vmem, vmem],
+        out_specs=vmem,
+        compiler_params=grant,
+        name="spread",
+    )(edges[4:5], own_half, other_half)
     return (
         new_fields,
         patch_gradient,

time: 407 us -> 197 us (0.48)
  waiting for transfers between devices: 156 us -> 20.6 us
  local copies, waits for them, and re-layouts: 42 us -> 16.7 us
  other arithmetic: 27.8 us -> 5.25 us
  between operations: 14.9 us -> 0.96 us
  blocking collectives: 90.1 us -> 81.8 us
  starting transfers between devices: 28.1 us -> 22.5 us
  Pallas kernels: 26.7 us -> 32.2 us
    psum x1 -> x0, waiting for transfers between devices: 143 us -> none  [per_device(): patch_gradient = lax.psum(part, axes)]
    unnamed x1 -> x0, blocking collectives: 70.7 us -> none
    all_to_all x1 -> x3, blocking collectives: 19.4 us -> 81.8 us  [the longest x1 33.6 us: per_device(): lax.all_to_all(send.reshape(devices, 2 * per, EMBED), axes, 0, 0, tiled=T...]
    all_to_all x4 -> x0, other arithmetic: 25.8 us -> none  [the longest x2 16.1 us: per_device(): got = lax.all_to_all(send.reshape(devices, -1), axes, 0, 0, tiled=True)]
    unnamed x53 -> x56, local copies, waits for them, and re-layouts: 23.9 us -> 8.25 us
    all_to_all x1, waiting for transfers between devices: 0.01 us -> 12.7 us  [per_device(): lax.all_to_all(source_grad.reshape(devices, per, EMBED), axes, 0, 0, tile...]
    all_to_all x1, starting transfers between devices: 16 us -> 4.74 us  [per_device(): lax.all_to_all(source_grad.reshape(devices, per, EMBED), axes, 0, 0, tile...]
    all_to_all x3 -> x0, local copies, waits for them, and re-layouts: 7.87 us -> none  [the longest x2 6.23 us: per_device(): got = lax.all_to_all(send.reshape(devices, -1), axes, 0, 0, tiled=True)]
  transfers between devices with their start and end apart: 6 -> 8, of which waited for: 5 -> 5; matrix products, arithmetic and copies ran while one was open for 4% -> 6% of each run, Pallas kernels for 0% -> 1%
where the time goes in v2:
time: 197 us; the launch traced here: 196 us
  blocking collectives  81.8 us (42%)
  Pallas kernels  32.2 us (16%)
  starting transfers between devices  22.5 us (11%)
  waiting for transfers between devices  20.6 us (10%)
  local copies, waits for them, and re-layouts  16.7 us (8%)
  matrix products  16.1 us (8%)
  other arithmetic  5.25 us (3%)
    all_to_all x1, blocking collectives, per_device(): lax.all_to_all(send.reshape(devices, 2 * per, EMBED), axes, 0, 0, tiled=T...  33.6 us
    pallas_call x1, Pallas kernels, per_device(): pl.pallas_call(functools.partial(window_kernel, (wide_x, wide_y, wide_z),...  25.6 us
    all_to_all x1, blocking collectives, per_device(): lax.all_to_all(copies, axes, 0, 0, axis_index_groups=groups, tiled=True)  24.5 us
    all_to_all x1, blocking collectives, per_device(): lax.all_to_all(parts.reshape(members, piece, width), axes, 0, 0, axis_ind...  23.7 us
    all_to_all x1, waiting for transfers between devices, per_device(): lax.all_to_all(source_grad.reshape(devices, per, EMBED), axes, 0, 0, tile...  12.7 us
    unnamed x56, local copies, waits for them, and re-layouts  8.25 us
    ppermute x2, starting transfers between devices, neighbours(): lax.ppermute(high_piece, axis, up)  7.44 us
    dot_general x2, matrix products, contract_rows(): lax.dot_general(left, right, (((0,), (0,)), ((), ())), preferred_element_...  6.76 us
  transfers between devices with their start and end apart: 8, of which 5 were waited for; matrix products, arithmetic and copies ran while one was open for 6% of the time, Pallas kernels for 1%

profile of v2, /device:TPU:1, one launch (start us, length us, event | category | flops | bytes accessed | tf_op | source)
XLA Modules:
  0.0 196.1 jit_solution(7179282998679271245)
XLA Ops:
  0.7 1.6 convert_element_type.34
  2.3 3.3 %collective-permute-start.1 = (bf16[5,6,32,128]{3,2,1,0:T(8,128)(2,1)S(1)}, bf16[5,6,32,128]{3,2,1,0:T(8,128)(2,1)S(1)}, u32[]{:S(2)}, u32[]{:S(2)}) collective-permute-start(bf16[5,6,32,128]{3,2,1,0:T(8,128)(2,1)S(1)} %get-tuple-element.18), channel_id=1, source_target_pairs={{8,0},{16,8},{24,16},{32,24},{40,32},{48,40},{56,48},{64,56},{72,6... | collective-permute-start | bytes 737288 | tf_op jit(solution)/shard_map/ppermute | solution.py:322
  5.7 3.5 %collective-permute-start = (bf16[5,6,32,128]{3,2,1,0:T(8,128)(2,1)S(1)}, bf16[5,6,32,128]{3,2,1,0:T(8,128)(2,1)S(1)}, u32[]{:S(2)}, u32[]{:S(2)}) collective-permute-start(bf16[5,6,32,128]{3,2,1,0:T(8,128)(2,1)S(1)} %get-tuple-element.19), channel_id=1, source_target_pairs={{0,8},{8,16},{16,24},{24,32},{32,40},{40,48},{48,56},{56,64},{64,7... | collective-permute-start | bytes 737288 | tf_op jit(solution)/shard_map/ppermute | solution.py:322
  10.0 1.2 collective-permute-done.1.xhi_ref
  11.8 2.1 %collective-permute-done.xlo_ref = bf16[5,6,32,128]{3,2,1,0:T(8,128)(2,1)S(1)} collective-permute-done((bf16[5,6,32,128]{3,2,1,0:T(8,128)(2,1)S(1)}, bf16[5,6,32,128]{3,2,1,0:T(8,128)(2,1)S(1)}, u32[]{:S(2)}, u32[]{:S(2)}) %collective-permute-start) | collective-permute-done | bytes 245792 | tf_op jit(solution)/shard_map/ppermute | solution.py:322
  15.4 3.9 %collective-permute-start.2 = (bf16[5,28,8,128]{3,2,1,0:T(8,128)(2,1)}, bf16[5,28,8,128]{3,2,1,0:T(8,128)(2,1)}, u32[]{:S(2)}, u32[]{:S(2)}) collective-permute-start(bf16[5,28,8,128]{3,2,1,0:T(8,128)(2,1)} %pad_maximum_fusion), channel_id=1, source_target_pairs={{0,1},{1,2},{2,3},{3,4},{4,5},{5,6},{6,7},{8,9},{9,10},{10,11},{11... | collective-permute-start | bytes 860168 | tf_op jit(solution)/shard_map/ppermute | solution.py:322
  20.0 1.3 collective-permute-start.3
  22.5 1.0 copy.21.lag_ref
  23.5 4.2 %collective-permute-done.3.yhi_ref = bf16[5,28,8,128]{3,2,1,0:T(8,128)(2,1)} collective-permute-done((bf16[5,28,8,128]{3,2,1,0:T(8,128)(2,1)}, bf16[5,28,8,128]{3,2,1,0:T(8,128)(2,1)}, u32[]{:S(2)}, u32[]{:S(2)}) %collective-permute-start.3) | collective-permute-done | bytes 286752 | tf_op jit(solution)/shard_map/ppermute | solution.py:322
  29.6 25.6 %window.1 = (f32[5,16,32,128]{3,2,1,0:T(8,128)}, bf16[1280,128]{1,0:T(8,128)(2,1)S(1)}, bf16[1280,128]{1,0:T(8,128)(2,1)S(1)}, bf16[1024,512]{1,0:T(8,128)(2,1)S(1)}) custom-call(s32[5]{0:T(128)S(1)} %convert_element_type.33.edge_ref, f32[5,16,32,128]{3,2,1,0:T(8,128)S(1)} %copy-done.1, bf16[5,6,32,128]{3,2,1,0:T(8,128)(2,1)S(1)} %copy-done.6, ...), custom_call_target="tpu_custom_call" | custom-call | tf_op jit(solution)/shard_map/window/pallas_call | solution.py:385
  55.3 33.6 %all_to_all.20 = bf16[128,8,512]{2,1,0:T(8,128)(2,1)S(1)} all-to-all(bf16[128,8,512]{2,1,0:T(8,128)(2,1)S(1)} %bitcast.56), channel_id=1, replica_groups=mesh['gx'=16,'gy'=8] {'gx','gy'}, dimensions={0} | all-to-all | bytes 2097152 | tf_op jit(solution)/shard_map/all_to_all | solution.py:412
  88.8 1.5 slice_convert_fusion
  90.3 2.6 %reshape.47 = f32[512,512]{1,0:T(8,128)} reshape(f32[128,4,512]{2,1,0:T(4,128)} %get-tuple-element.14) | data formatting | bytes 2097152 | tf_op jit(solution)/shard_map/convert_element_type | solution.py:341
  92.9 1.2 reshape.42
  94.1 3.1 %fusion.5 = f32[512,2048]{1,0:T(8,128)S(1)} fusion(bf16[512,512]{1,0:T(8,128)(2,1)S(1)} %reshape.42, bf16[1,512,2048]{2,1,0:T(8,128)(2,1)} %param.12), kind=kOutput, calls=%fused_computation.11 | convolution fusion | flops 1073741824 | bytes 6815744 | tf_op jit(solution)/shard_map/dot_general | solution.py:338
  97.2 2.0 %convert_reduce_fusion.1 = (f32[512]{0:T(512)}, bf16[512,512]{1,0:T(8,128)(2,1)S(1)}) fusion(f32[512,512]{1,0:T(8,128)S(1)} %copy-done.22, f32[512]{0:T(512)S(1)} %bitcast.61, bf16[1,2048,512]{2,1,0:T(8,128)(2,1)S(1)} %copy-done, f32[512,2048]{1,0:T(8,128)S(1)} %fusion.5, f32[2048]{0:T(1024)S(1)} %bitcast.58), kind=kOutput, calls=%fused_computation.19 | convolution fusion | flops 1082129920 | bytes 7876608 | tf_op jit(solution)/shard_map/dot_general | solution.py:340
  99.2 3.1 %convert_reduce_fusion = (f32[2048]{0:T(1024)}, bf16[512,2048]{1,0:T(8,128)(2,1)S(1)}) fusion(f32[512,2048]{1,0:T(8,128)S(1)} %fusion.5, f32[2048]{0:T(1024)S(1)} %bitcast.59, bf16[512,512]{1,0:T(8,128)(2,1)S(1)} %get-tuple-element.27, bf16[1,2048,512]{2,1,0:T(8,128)(2,1)S(1)} %copy-done), kind=kOutput, calls=%fused_computation | convolution fusion | flops 1086322688 | bytes 8929280 | tf_op jit(solution)/shard_map/dot_general | solution.py:332
  102.3 1.3 copy-done.20
  103.6 1.3 fusion.19
  105.8 4.7 %all-to-all-start.1 = ((bf16[128,4,512]{2,1,0:T(4,128)(2,1)}), bf16[128,4,512]{2,1,0:T(4,128)(2,1)S(1)}, u32[]{:S(2)}, u32[]{:S(2)}) async-start(bf16[128,4,512]{2,1,0:T(4,128)(2,1)} %reshape.43), calls=%async_computation.1 | async-start | bytes 1048576 | tf_op jit(solution)/shard_map/all_to_all | solution.py:421
  110.5 1.3 collective-permute-start.4
  111.8 12.7 %all-to-all-done.1 = bf16[128,4,512]{2,1,0:T(4,128)(2,1)S(1)} async-done(((bf16[128,4,512]{2,1,0:T(4,128)(2,1)}), bf16[128,4,512]{2,1,0:T(4,128)(2,1)S(1)}, u32[]{:S(2)}, u32[]{:S(2)}) %all-to-all-start.1) | async-done | bytes 524320 | tf_op jit(solution)/shard_map/all_to_all | solution.py:421
  125.4 2.2 %gather.1.own_grad_ref = bf16[128,512]{1,0:T(8,128)(2,1)} custom-call(s32[1,128]{1,0:T(1,128)} %copy-done.12, s32[128,1]{1,0:T(8,128)} %copy-done.2, bf16[512,512]{1,0:T(8,128)(2,1)} %reshape.44.back_ref), custom_call_target="tpu_custom_call" | custom-call | tf_op jit(solution)/shard_map/gather/pallas_call | solution.py:422
  127.6 1.0 collective-permute-start.5
  130.7 1.0 copy-done.9
  131.6 1.0 copy-done.11
  133.5 23.7 %all_to_all.21.parts_ref = bf16[64,40,256]{2,1,0:T(8,128)(2,1)S(1)} all-to-all(bf16[64,40,256]{2,1,0:T(8,128)(2,1)S(1)} %bitcast.53), channel_id=1, replica_groups={{0,1,2,3,4,5,6,7,16,17,18,19,20,21,22,23,32,33,34,35,36,37,38,39,48,49,..., dimensions={0} | all-to-all | bytes 2621440 | tf_op jit(solution)/shard_map/all_to_all | solution.py:440
  157.4 24.5 %all_to_all.22 = bf16[64,40,256]{2,1,0:T(8,128)(2,1)S(1)} all-to-all(bf16[64,40,256]{2,1,0:T(8,128)(2,1)S(1)} %total.1), channel_id=1, replica_groups={{0,1,2,3,4,5,6,7,16,17,18,19,20,21,22,23,32,33,34,35,36,37,38,39,48,49,..., dimensions={0} | all-to-all | bytes 2621440 | tf_op jit(solution)/shard_map/all_to_all | solution.py:451
  181.9 3.4 %collective-permute-start.6 = (bf16[2560,256]{1,0:T(8,128)(2,1)S(1)}, bf16[2560,256]{1,0:T(8,128)(2,1)S(1)}, u32[]{:S(2)}, u32[]{:S(2)}) collective-permute-start(bf16[2560,256]{1,0:T(8,128)(2,1)S(1)} %bitcast.54), channel_id=1, source_target_pairs={{0,8},{8,0},{16,24},{24,16},{32,40},{40,32},{48,56},{56,48},{64,72... | collective-permute-start | bytes 3932168 | tf_op jit(solution)/shard_map/ppermute | solution.py:453
  186.0 3.3 %convolution_bitcast_fusion.1 = f32[1,512,2048]{2,1,0:T(8,128)} fusion(bf16[512,512]{1,0:T(8,128)(2,1)S(1)} %copy-done.16, bf16[512,2048]{1,0:T(8,128)(2,1)S(1)} %copy-done.21), kind=kOutput, calls=%fused_computation.5 | convolution fusion | flops 1073741824 | bytes 6815744 | tf_op jit(solution)/shard_map/dot_general | solution.py:326
  189.3 3.5 %convolution_bitcast_fusion = f32[1,2048,512]{2,1,0:T(8,128)} fusion(bf16[512,512]{1,0:T(8,128)(2,1)S(1)} %copy-done.27, f32[512,2048]{1,0:T(8,128)S(1)} %copy-done.18, f32[2048]{0:T(1024)S(1)} %bitcast.60), kind=kOutput, calls=%fused_computation.4 | convolution fusion | flops 1080033280 | bytes 8921088 | tf_op jit(solution)/shard_map/dot_general | solution.py:326
  192.7 3.4 %spread.1 = f32[2560,512]{1,0:T(8,128)} custom-call(s32[1]{0:T(128)} %slice.41.core_ref, bf16[2560,256]{1,0:T(8,128)(2,1)S(1)} %bitcast.55, bf16[2560,256]{1,0:T(8,128)(2,1)S(1)} %collective-permute-done.6.other_ref), custom_call_target="tpu_custom_call" | custom-call | tf_op jit(solution)/shard_map/spread/pallas_call | solution.py:454
  (77 shorter events, 12.4 us)
Async XLA Ops:
  0.6 96.5 %copy-start = (bf16[1,2048,512]{2,1,0:T(8,128)(2,1)S(1)}, bf16[1,2048,512]{2,1,0:T(8,128)(2,1)}, u32[]{:S(2)}) copy-start(bf16[1,2048,512]{2,1,0:T(8,128)(2,1)} %param.14) | copy-start | bytes 6291460
  0.6 27.1 %copy-start.1 = (f32[5,16,32,128]{3,2,1,0:T(8,128)S(1)}, f32[5,16,32,128]{3,2,1,0:T(8,128)}, u32[]{:S(2)}) copy-start(f32[5,16,32,128]{3,2,1,0:T(8,128)} %f_ref.1) | copy-start | bytes 3932164
  0.7 20.7 %copy-start.23 = (s32[64,1]{0,1:T(1,128)S(1)}, s32[64,1]{0,1:T(1,128)}, u32[]{:S(2)}) copy-start(s32[64,1]{0,1:T(1,128)} %param.10) | copy-start | bytes 772
  2.3 8.8 %collective-permute-start.1 = (bf16[5,6,32,128]{3,2,1,0:T(8,128)(2,1)S(1)}, bf16[5,6,32,128]{3,2,1,0:T(8,128)(2,1)S(1)}, u32[]{:S(2)}, u32[]{:S(2)}) collective-permute-start(bf16[5,6,32,128]{3,2,1,0:T(8,128)(2,1)S(1)} %get-tuple-element.18), channel_id=1, source_target_pairs={{8,0},{16,8},{24,16},{32,24},{40,32},{48,40},{56,48},{64,56},{72,6... | collective-permute-start | bytes 737288 | tf_op jit(solution)/shard_map/ppermute | solution.py:322
  5.7 8.3 %collective-permute-start = (bf16[5,6,32,128]{3,2,1,0:T(8,128)(2,1)S(1)}, bf16[5,6,32,128]{3,2,1,0:T(8,128)(2,1)S(1)}, u32[]{:S(2)}, u32[]{:S(2)}) collective-permute-start(bf16[5,6,32,128]{3,2,1,0:T(8,128)(2,1)S(1)} %get-tuple-element.19), channel_id=1, source_target_pairs={{0,8},{8,16},{16,24},{24,32},{32,40},{40,48},{48,56},{56,64},{64,7... | collective-permute-start | bytes 737288 | tf_op jit(solution)/shard_map/ppermute | solution.py:322
  15.4 8.1 %collective-permute-start.2 = (bf16[5,28,8,128]{3,2,1,0:T(8,128)(2,1)}, bf16[5,28,8,128]{3,2,1,0:T(8,128)(2,1)}, u32[]{:S(2)}, u32[]{:S(2)}) collective-permute-start(bf16[5,28,8,128]{3,2,1,0:T(8,128)(2,1)} %pad_maximum_fusion), channel_id=1, source_target_pairs={{0,1},{1,2},{2,3},{3,4},{4,5},{5,6},{6,7},{8,9},{9,10},{10,11},{11... | collective-permute-start | bytes 860168 | tf_op jit(solution)/shard_map/ppermute | solution.py:322
  20.0 7.7 %collective-permute-start.3 = (bf16[5,28,8,128]{3,2,1,0:T(8,128)(2,1)}, bf16[5,28,8,128]{3,2,1,0:T(8,128)(2,1)}, u32[]{:S(2)}, u32[]{:S(2)}) collective-permute-start(bf16[5,28,8,128]{3,2,1,0:T(8,128)(2,1)} %pad_maximum_fusion.1), channel_id=1, source_target_pairs={{1,0},{2,1},{3,2},{4,3},{5,4},{6,5},{7,6},{9,8},{10,9},{11,10},{12... | collective-permute-start | bytes 860168 | tf_op jit(solution)/shard_map/ppermute | solution.py:322
  21.6 68.7 %copy-start.12 = (s32[1,128]{1,0:T(1,128)}, s32[1,128]{1,0:T(1,128)S(1)}, u32[]{:S(2)}) copy-start(s32[1,128]{1,0:T(1,128)S(1)} %broadcast_in_dim_reshape.6.own_row_ref) | copy-start | bytes 1540
  21.7 68.6 %copy-start.2 = (s32[128,1]{1,0:T(8,128)}, s32[128,1]{1,0:T(8,128)S(1)}, u32[]{:S(2)}) copy-start(s32[128,1]{1,0:T(8,128)S(1)} %broadcast_in_dim_reshape.8.own_col_ref) | copy-start | bytes 1540
  27.7 0.9 copy-start.4
  28.7 0.9 copy-start.6
  55.3 33.6 %copy-start.8 = (bf16[1280,128]{1,0:T(8,128)(2,1)}, bf16[1280,128]{1,0:T(8,128)(2,1)S(1)}, u32[]{:S(2)}) copy-start(bf16[1280,128]{1,0:T(8,128)(2,1)S(1)} %get-tuple-element.11.keep_ref) | copy-start | bytes 983044
  55.3 35.0 %copy-start.13 = (bf16[1280,128]{1,0:T(8,128)(2,1)}, bf16[1280,128]{1,0:T(8,128)(2,1)S(1)}, u32[]{:S(2)}) copy-start(bf16[1280,128]{1,0:T(8,128)(2,1)S(1)} %get-tuple-element.12) | copy-start | bytes 983044
  92.9 4.3 %copy-start.24 = (f32[1,2048]{1,0:T(1,128)S(1)}, f32[1,2048]{1,0:T(1,128)}, u32[]{:S(2)}) copy-start(f32[1,2048]{1,0:T(1,128)} %param.13) | copy-start | bytes 24580
  92.9 4.3 %copy-start.25 = (f32[1,512]{1,0:T(1,128)S(1)}, f32[1,512]{1,0:T(1,128)}, u32[]{:S(2)}) copy-start(f32[1,512]{1,0:T(1,128)} %param.15) | copy-start | bytes 6148
  94.1 5.1 %copy-start.15 = (bf16[512,512]{1,0:T(8,128)(2,1)}, bf16[512,512]{1,0:T(8,128)(2,1)S(1)}, u32[]{:S(2)}) copy-start(bf16[512,512]{1,0:T(8,128)(2,1)S(1)} %reshape.42) | copy-start | bytes 1572868
  94.1 3.1 %copy-start.22 = (f32[512,512]{1,0:T(8,128)S(1)}, f32[512,512]{1,0:T(8,128)}, u32[]{:S(2)}) copy-start(f32[512,512]{1,0:T(8,128)} %reshape.47) | copy-start | bytes 3145732
  97.1 2.0 %copy-start.17 = (f32[512,2048]{1,0:T(8,128)}, f32[512,2048]{1,0:T(8,128)S(1)}, u32[]{:S(2)}) copy-start(f32[512,2048]{1,0:T(8,128)S(1)} %fusion.5) | copy-start | bytes 12582916
  99.2 3.1 %copy-start.26 = (bf16[512,512]{1,0:T(8,128)(2,1)}, bf16[512,512]{1,0:T(8,128)(2,1)S(1)}, u32[]{:S(2)}) copy-start(bf16[512,512]{1,0:T(8,128)(2,1)S(1)} %get-tuple-element.27) | copy-start | bytes 1572868
  99.2 4.4 %copy-start.19 = (bf16[1,512,2048]{2,1,0:T(8,128)(2,1)S(1)}, bf16[1,512,2048]{2,1,0:T(8,128)(2,1)}, u32[]{:S(2)}) copy-start(bf16[1,512,2048]{2,1,0:T(8,128)(2,1)} %param.12) | copy-start | bytes 6291460
  102.3 1.3 copy-start.20
  103.6 7.0 %copy-start.14 = (bf16[1280,128]{1,0:T(8,128)(2,1)S(1)}, bf16[1280,128]{1,0:T(8,128)(2,1)}, u32[]{:S(2)}) copy-start(bf16[1280,128]{1,0:T(8,128)(2,1)} %copy-done.13) | copy-start | bytes 983044
  105.8 18.7 %all-to-all-start.1 = ((bf16[128,4,512]{2,1,0:T(4,128)(2,1)}), bf16[128,4,512]{2,1,0:T(4,128)(2,1)S(1)}, u32[]{:S(2)}, u32[]{:S(2)}) async-start(bf16[128,4,512]{2,1,0:T(4,128)(2,1)} %reshape.43), calls=%async_computation.1 | async-start | bytes 1048576 | tf_op jit(solution)/shard_map/all_to_all | solution.py:421
  110.5 18.0 %collective-permute-start.4 = (bf16[1280,128]{1,0:T(8,128)(2,1)S(1)}, bf16[1280,128]{1,0:T(8,128)(2,1)S(1)}, u32[]{:S(2)}, u32[]{:S(2)}) collective-permute-start(bf16[1280,128]{1,0:T(8,128)(2,1)S(1)} %copy-done.14), channel_id=1, source_target_pairs={{0,8},{8,0},{16,24},{24,16},{32,40},{40,32},{48,56},{56,48},{64,72... | collective-permute-start | bytes 983048 | tf_op jit(solution)/shard_map/ppermute | solution.py:411
  127.6 2.2 %collective-permute-start.5 = (bf16[128,512]{1,0:T(8,128)(2,1)}, bf16[128,512]{1,0:T(8,128)(2,1)S(1)}, u32[]{:S(2)}, u32[]{:S(2)}) collective-permute-start(bf16[128,512]{1,0:T(8,128)(2,1)} %gather.1.own_grad_ref), channel_id=1, source_target_pairs={{0,8},{8,0},{16,24},{24,16},{32,40},{40,32},{48,56},{56,48},{64,72... | collective-permute-start | bytes 393224 | tf_op jit(solution)/shard_map/ppermute | solution.py:429
  130.7 1.0 copy-start.9
  131.6 1.0 copy-start.11
  133.4 52.5 %copy-start.16 = (bf16[512,512]{1,0:T(8,128)(2,1)S(1)}, bf16[512,512]{1,0:T(8,128)(2,1)}, u32[]{:S(2)}) copy-start(bf16[512,512]{1,0:T(8,128)(2,1)} %copy-done.15) | copy-start | bytes 1572868
  133.5 52.5 %copy-start.21 = (bf16[512,2048]{1,0:T(8,128)(2,1)S(1)}, bf16[512,2048]{1,0:T(8,128)(2,1)}, u32[]{:S(2)}) copy-start(bf16[512,2048]{1,0:T(8,128)(2,1)} %copy-done.20) | copy-start | bytes 6291460
  157.4 31.9 %copy-start.18 = (f32[512,2048]{1,0:T(8,128)S(1)}, f32[512,2048]{1,0:T(8,128)}, u32[]{:S(2)}) copy-start(f32[512,2048]{1,0:T(8,128)} %copy-done.17) | copy-start | bytes 12582916
  157.4 31.9 %copy-start.27 = (bf16[512,512]{1,0:T(8,128)(2,1)S(1)}, bf16[512,512]{1,0:T(8,128)(2,1)}, u32[]{:S(2)}) copy-start(bf16[512,512]{1,0:T(8,128)(2,1)} %copy-done.26) | copy-start | bytes 1572868
  181.9 10.8 %collective-permute-start.6 = (bf16[2560,256]{1,0:T(8,128)(2,1)S(1)}, bf16[2560,256]{1,0:T(8,128)(2,1)S(1)}, u32[]{:S(2)}, u32[]{:S(2)}) collective-permute-start(bf16[2560,256]{1,0:T(8,128)(2,1)S(1)} %bitcast.54), channel_id=1, source_target_pairs={{0,8},{8,0},{16,24},{24,16},{32,40},{40,32},{48,56},{56,48},{64,72... | collective-permute-start | bytes 3932168 | tf_op jit(solution)/shard_map/ppermute | solution.py:453
  (4 other events, 3.0 us)

commit v3 on v2

--- a/solution.py
+++ b/solution.py
@@ -86,42 +86,47 @@
     return density, first, second, third, pressure + spread
 
 
-def slot_rows(owner_row, owner_col, patches):
-    earlier_r = lax.broadcasted_iota(jnp.int32, (patches, patches), 0)
-    earlier_c = lax.broadcasted_iota(jnp.int32, (patches, patches), 1)
-    same = owner_row == owner_col
-    half_r, half_c = earlier_r // BLOCK_ROWS, earlier_c // BLOCK_ROWS
-    return same, earlier_r, earlier_c, half_r, half_c
-
-
-def target_rows(owner_row, owner_col, patches, slots, along_lanes):
-    same, at_r, at_c, half_r, half_c = slot_rows(owner_row, owner_col, patches)
-    if along_lanes:
-        hit = same & (half_r < half_c) & (at_r % BLOCK_ROWS == 0)
-        rank = jnp.sum(jnp.where(hit, 1.0, 0.0), axis=0, keepdims=True).astype(jnp.int32)
-        place = lax.broadcasted_iota(jnp.int32, (1, patches), 1) % BLOCK_ROWS
-        owner = owner_row
-    else:
-        hit = same & (half_c < half_r) & (at_c % BLOCK_ROWS == 0)
-        rank = jnp.sum(jnp.where(hit, 1.0, 0.0), axis=1, keepdims=True).astype(jnp.int32)
-        place = lax.broadcasted_iota(jnp.int32, (patches, 1), 0) % BLOCK_ROWS
-        owner = owner_col
-    return owner, rank * BLOCK_ROWS + place
+def slots_kernel(slots, own_row_ref, own_col_ref, lag_ref, source_ref, target_ref, chosen_ref):
+    rows, patches = source_ref.shape
+    per = slots * BLOCK_ROWS
+    at_r = lax.broadcasted_iota(jnp.int32, (patches, patches), 0)
+    at_c = lax.broadcasted_iota(jnp.int32, (patches, patches), 1)
+    earlier = (at_r // BLOCK_ROWS < at_c // BLOCK_ROWS) & (at_r % BLOCK_ROWS == 0)
+    hit = (own_row_ref[...] == own_col_ref[...]) & earlier
+    rank = jnp.sum(jnp.where(hit, 1.0, 0.0), axis=0, keepdims=True).astype(jnp.int32)
+    place = lax.broadcasted_iota(jnp.int32, (1, patches), 1) % BLOCK_ROWS
+    at = own_row_ref[...] * (2 * per) + rank * BLOCK_ROWS + place
+    row = lax.broadcasted_iota(jnp.int32, (rows, patches), 0)
+    source_ref[...] = jnp.where(row == at, 1.0, 0.0).astype(jnp.bfloat16)
+    target_ref[...] = jnp.where(row == at + per, 1.0, 0.0).astype(jnp.bfloat16)
+    tall, wide = chosen_ref.shape
+    bricks, deep = lag_ref.shape
+    along = lax.broadcasted_iota(jnp.int32, (deep, wide), 0)
+    cells = lax.broadcasted_iota(jnp.int32, (deep, wide), 1)
+    spread = jnp.where(along == cells // PATCH, 1.0, 0.0).astype(jnp.bfloat16)
+    lanes = jnp.dot(
+        lag_ref[...].astype(jnp.bfloat16), spread, preferred_element_type=jnp.float32
+    )
+    line = lax.broadcasted_iota(jnp.int32, (tall, bricks), 0)
+    brick = lax.broadcasted_iota(jnp.int32, (tall, bricks), 1)
+    lift = jnp.where(line // PATCH == brick, 1.0, 0.0).astype(jnp.bfloat16)
+    chosen_ref[...] = jnp.dot(
+        lift, lanes.astype(jnp.bfloat16), preferred_element_type=jnp.float32
+    )
 
 
 def window_kernel(
     shape,
-    rows,
-    slots,
+    per,
     edge_ref,
     f_ref,
     xlo_ref,
     xhi_ref,
     ylo_ref,
     yhi_ref,
-    lag_ref,
-    own_row_ref,
-    own_col_ref,
+    chosen_ref,
+    source_pick_ref,
+    target_pick_ref,
     w_ref,
     new_ref,
     keep_ref,
@@ -174,7 +179,7 @@
                 dst[field, row] = done[field]
             return carry
 
-        lax.fori_loop(least, full_x - least, body, 0)
+        lax.fori_loop(least, full_x - least, body, 0, unroll=2)
         clear(dst, least)
 
     def last_step(src):
@@ -184,7 +189,7 @@
                 new_ref[field, row - REACH] = done[field]
             return carry
 
-        lax.fori_loop(REACH, top_x, body, 0)
+        lax.fori_loop(REACH, top_x, body, 0, unroll=2)
 
     z_count = wide_z // PATCH
     lane_r = lax.broadcasted_iota(jnp.int32, (wide_z, wide_z), 0)
@@ -201,30 +206,31 @@
                 flat.astype(jnp.bfloat16), swap, preferred_element_type=jnp.float32
             ).reshape(wide_x, wide_y, wide_z)
 
-        def body(at, carry):
-            field, inner = at // PATCH, at % PATCH
+        for field in range(FIELDS):
             tiles = [
-                shuffle_ref[field, px * PATCH + inner, py * PATCH : (py + 1) * PATCH]
+                shuffle_ref[
+                    field, px * PATCH : (px + 1) * PATCH, py * PATCH : (py + 1) * PATCH
+                ]
                 for px in range(wide_x // PATCH)
                 for py in range(wide_y // PATCH)
             ]
             for bit in (4, 2, 1):
-                low = (group & bit) == 0
+                low = ((group & bit) == 0)[None]
                 fresh = list(tiles)
                 for i in range(PATCH):
                     if i & bit:
                         continue
                     a, b = tiles[i], tiles[i | bit]
-                    fresh[i] = jnp.where(low, a, pltpu.roll(b, bit * z_count, 1))
+                    fresh[i] = jnp.where(low, a, pltpu.roll(b, bit * z_count, 2))
                     fresh[i | bit] = jnp.where(
-                        low, pltpu.roll(a, wide_z - bit * z_count, 1), b
+                        low, pltpu.roll(a, wide_z - bit * z_count, 2), b
                     )
                 tiles = fresh
             for inner_z in range(PATCH):
-                natural_ref[at, pl.ds(inner_z, PATCH, stride=PATCH), :] = tiles[inner_z]
-            return carry
-
-        lax.fori_loop(0, FIELDS * PATCH, body, 0, unroll=2)
+                natural_ref[
+                    field * PATCH : (field + 1) * PATCH, pl.ds(inner_z, PATCH, stride=PATCH), :
+                ] = tiles[inner_z]
+
         for field in range(FIELDS):
             block = natural_ref[field * PATCH : (field + 1) * PATCH]
             block = block.reshape(PATCH**3, patches).astype(jnp.bfloat16)
@@ -241,7 +247,8 @@
         two = first_ref[field, REACH:top_x, LIFT:top_y]
         one = one.reshape(wide_x // PATCH, PATCH, wide_y, wide_z)
         two = two.reshape(wide_x // PATCH, PATCH, wide_y, wide_z)
-        return jnp.where(lag_ref[...][:, None] == 1.0, two, one)
+        later = chosen_ref[...].reshape(wide_x // PATCH, 1, wide_y, wide_z)
+        return jnp.where(later == 1.0, two, one)
 
     step(first_ref, second_ref, 2)
     step(second_ref, first_ref, 4)
@@ -256,35 +263,108 @@
     mine = pl.multiple_of(edge_ref[4] * half, half)
     keep_ref[...] = both_ref[pl.ds(mine, half), 0:patches]
     give_ref[...] = both_ref[pl.ds(half - mine, half), 0:patches]
-    owner, slot = target_rows(own_row_ref[...], own_col_ref[...], patches, slots, True)
-    per = slots * BLOCK_ROWS
-    row = lax.broadcasted_iota(jnp.int32, (rows, patches), 0)
-    source_at = owner * (2 * per) + slot
-    is_source = row == source_at
-    is_target = row == source_at + per
-    source_pick = jnp.where(is_source, 1.0, 0.0).astype(jnp.bfloat16)
-    target_pick = jnp.where(is_target, 1.0, 0.0)
-    filled = jnp.sum(target_pick, axis=1, keepdims=True)
+    rows = send_ref.shape[0]
+    filled = jnp.sum(target_pick_ref[...].astype(jnp.float32), axis=1, keepdims=True)
     target_half = (lax.broadcasted_iota(jnp.int32, (rows, 1), 0) // per) % 2 == 1
     marker = jnp.where(target_half & (filled == 0.0), EMPTY, 0.0)
-    placed = jnp.dot(source_pick, embedded[0:patches], preferred_element_type=jnp.float32)
+    placed = jnp.dot(
+        source_pick_ref[...], embedded[0:patches], preferred_element_type=jnp.float32
+    )
     placed = placed + jnp.dot(
-        target_pick.astype(jnp.bfloat16),
+        target_pick_ref[...],
         embedded[patches : 2 * patches],
         preferred_element_type=jnp.float32,
     )
     send_ref[...] = (placed + marker).astype(jnp.bfloat16)
 
 
-def gather_kernel(rows, slots, own_row_ref, own_col_ref, back_ref, out_ref):
-    patches = own_row_ref.shape[1]
-    owner, slot = target_rows(own_row_ref[...], own_col_ref[...], patches, slots, False)
-    at = owner * (slots * BLOCK_ROWS) + slot
-    chosen_rows = lax.broadcasted_iota(jnp.int32, (patches, rows), 1) == at
-    select = jnp.where(chosen_rows, 1.0, 0.0).astype(jnp.bfloat16)
-    out_ref[...] = jnp.dot(
-        select, back_ref[...], preferred_element_type=jnp.float32
-    ).astype(jnp.bfloat16)
+def trainer_kernel(
+    per,
+    got_ref,
+    w_in_ref,
+    b_in_ref,
+    w_out_ref,
+    b_out_ref,
+    source_ref,
+    hidden_ref,
+    error_ref,
+    pre_grad_ref,
+    b_in_grad_ref,
+    b_out_grad_ref,
+    back_ref,
+    target_ref,
+    slope_ref,
+):
+    rows = source_ref.shape[0]
+    width = back_ref.shape[1]
+    small, large = 32 * per, 64 * per
+    line = lax.broadcasted_iota(jnp.int32, (small, large), 0)
+    taken = lax.broadcasted_iota(jnp.int32, (small, large), 1)
+    first = line // per * (2 * per) + line % per
+    source_pick = jnp.where(taken == first, 1.0, 0.0).astype(jnp.bfloat16)
+    target_pick = jnp.where(taken == first + per, 1.0, 0.0).astype(jnp.bfloat16)
+    for at in range(rows // small):
+        block = got_ref[at * large : (at + 1) * large]
+        lines = slice(at * small, (at + 1) * small)
+        source_ref[lines] = jnp.dot(
+            source_pick, block, preferred_element_type=jnp.float32
+        ).astype(jnp.bfloat16)
+        target_ref[lines] = jnp.dot(target_pick, block, preferred_element_type=jnp.float32)
+
+    chunk = 512
+    hidden_size = hidden_ref.shape[1]
+    source = source_ref[...]
+    predict = jnp.broadcast_to(b_out_ref[...], target_ref.shape)
+    for start in range(0, hidden_size, chunk):
+        lanes = slice(start, start + chunk)
+        pre = jnp.dot(source, w_in_ref[:, lanes], preferred_element_type=jnp.float32)
+        pre = pre + b_in_ref[:, lanes]
+        sigma = jax.nn.sigmoid(pre)
+        hidden = (pre * sigma).astype(jnp.bfloat16)
+        hidden_ref[:, lanes] = hidden
+        slope_ref[:, lanes] = sigma * (1.0 + pre * (1.0 - sigma))
+        predict = predict + jnp.dot(
+            hidden, w_out_ref[lanes], preferred_element_type=jnp.float32
+        )
+    wanted = target_ref[...]
+    error = jnp.where(wanted < FULL_BELOW, error_weight * (predict - wanted), 0.0)
+    error = error.astype(jnp.bfloat16)
+    error_ref[...] = error
+    b_out_grad_ref[...] = jnp.sum(error.astype(jnp.float32), axis=0, keepdims=True)
+    total = jnp.zeros(target_ref.shape, jnp.float32)
+    for start in range(0, hidden_size, chunk):
+        lanes = slice(start, start + chunk)
+        upstream = contract_cols(error, w_out_ref[lanes])
+        pre_grad = (upstream * slope_ref[:, lanes]).astype(jnp.bfloat16)
+        pre_grad_ref[:, lanes] = pre_grad
+        b_in_grad_ref[:, lanes] = jnp.sum(
+            pre_grad.astype(jnp.float32), axis=0, keepdims=True
+        )
+        total = total + contract_cols(pre_grad, w_in_ref[:, lanes])
+    gradient = total.astype(jnp.bfloat16)
+    out = lax.broadcasted_iota(jnp.int32, (large, small), 0)
+    origin = lax.broadcasted_iota(jnp.int32, (large, small), 1)
+    fits = origin == out // (2 * per) * per + out % per
+    side = out // per % 2
+    for at in range(rows // small):
+        lines = slice(at * small, (at + 1) * small)
+        block = jnp.zeros((large, width), jnp.float32)
+        for half in range(2):
+            move = jnp.where(fits & (side == half), 1.0, 0.0).astype(jnp.bfloat16)
+            block = block + jnp.dot(
+                move,
+                gradient[lines, half * width : (half + 1) * width],
+                preferred_element_type=jnp.float32,
+            )
+        back_ref[at * large : (at + 1) * large] = block.astype(jnp.bfloat16)
+
+
+def gather_kernel(source_pick_ref, target_pick_ref, back_ref, out_ref):
+    width = back_ref.shape[1]
+    for half, pick_ref in enumerate((source_pick_ref, target_pick_ref)):
+        out_ref[:, half * width : (half + 1) * width] = contract_rows(
+            pick_ref[...], back_ref[...]
+        ).astype(jnp.bfloat16)
 
 
 def part_kernel(keep_ref, got_ref, own_grad_ref, other_grad_ref, part_ref):
@@ -332,24 +412,6 @@
     return lax.dot_general(
         left, right, (((1,), (1,)), ((), ())), preferred_element_type=jnp.float32
     )
-
-
-def trainer_step(source, target, w_first, b_first, w_second, b_second):
-    pre = jnp.dot(source, w_first, preferred_element_type=jnp.float32) + b_first
-    hidden = jax.nn.silu(pre).astype(jnp.bfloat16)
-    predict = jnp.dot(hidden, w_second, preferred_element_type=jnp.float32) + b_second
-    wanted = target.astype(jnp.float32)
-    error = jnp.where(wanted < FULL_BELOW, error_weight * (predict - wanted), 0.0)
-    error = error.astype(jnp.bfloat16)
-    b_second_grad = jnp.sum(error.astype(jnp.float32), axis=0)
-    w_second_grad = contract_rows(hidden, error)
-    back = contract_cols(error, w_second)
-    sigma = jax.nn.sigmoid(pre)
-    pre_grad = (back * sigma * (1.0 + pre * (1.0 - sigma))).astype(jnp.bfloat16)
-    b_first_grad = jnp.sum(pre_grad.astype(jnp.float32), axis=0)
-    w_first_grad = contract_rows(source, pre_grad)
-    source_grad = contract_cols(pre_grad, w_first).astype(jnp.bfloat16)
-    return (source_grad, w_first_grad, b_first_grad, w_second_grad, b_second_grad)
 
 
 def per_device(fields, patch_weight, trainer_of, lag_index, w_in, b_in, w_out, b_out):
@@ -363,10 +425,17 @@
     per = slots * BLOCK_ROWS
     features = FIELDS * PATCH**3
 
-    narrow = fields.astype(jnp.bfloat16)
-    xlo, xhi = neighbours(narrow[:, :REACH], narrow[:, wide_x - REACH :], "gx")
-    y_first = jnp.concatenate([p[:, :, :LIFT] for p in (xlo, narrow, xhi)], axis=1)
-    y_last = jnp.concatenate([p[:, :, wide_y - LIFT :] for p in (xlo, narrow, xhi)], axis=1)
+    def narrow(piece):
+        return piece.astype(jnp.bfloat16)
+
+    xlo, xhi = neighbours(narrow(fields[:, :REACH]), narrow(fields[:, wide_x - REACH :]), "gx")
+    y_first = jnp.concatenate(
+        [xlo[:, :, :LIFT], narrow(fields[:, :, :LIFT]), xhi[:, :, :LIFT]], axis=1
+    )
+    at = wide_y - LIFT
+    y_last = jnp.concatenate(
+        [xlo[:, :, at:], narrow(fields[:, :, at:]), xhi[:, :, at:]], axis=1
+    )
     ylo, yhi = neighbours(y_first, y_last, "gy")
 
     at_x, at_y = lax.axis_index("gx"), lax.axis_index("gy")
@@ -374,24 +443,43 @@
     edges = jnp.stack(
         [at_x == 0, at_x == n_x - 1, at_y == 0, at_y == n_y - 1, core == 1]
     ).astype(jnp.int32)
-    lag = jnp.repeat(jnp.repeat(lag_index.astype(jnp.float32), PATCH, axis=1), PATCH, axis=2)
     own_patch = jnp.repeat(trainer_of[:, 0], BLOCK_ROWS)
-    own_row, own_col = own_patch[None, :], own_patch[:, None]
+    lag = lag_index.reshape(-1, lag_index.shape[2]).astype(jnp.float32)
 
     vmem = pl.BlockSpec(memory_space=pltpu.VMEM)
     smem = pl.BlockSpec(memory_space=pltpu.SMEM)
-    grant = pltpu.CompilerParams(vmem_limit_bytes=32 * 1024 * 1024)
+
+    def grant(mebibytes):
+        return pltpu.CompilerParams(vmem_limit_bytes=mebibytes * 1024 * 1024)
+
+    def shape(dims, kind):
+        return jax.ShapeDtypeStruct(dims, kind)
+
+    send_rows = 2 * devices * per
+    source_pick, target_pick, chosen = pl.pallas_call(
+        functools.partial(slots_kernel, slots),
+        out_shape=(
+            shape((send_rows, patches), jnp.bfloat16),
+            shape((send_rows, patches), jnp.bfloat16),
+            shape(((wide_x // PATCH) * wide_y, wide_z), jnp.float32),
+        ),
+        in_specs=[vmem] * 3,
+        out_specs=(vmem,) * 3,
+        compiler_params=grant(8),
+        name="slots",
+    )(own_patch[None, :], own_patch[:, None], lag)
+
     full = (FIELDS, wide_x + 2 * REACH, wide_y + 2 * LIFT, wide_z)
     new_fields, keep, give, send = pl.pallas_call(
-        functools.partial(window_kernel, (wide_x, wide_y, wide_z), 2 * devices * per, slots),
+        functools.partial(window_kernel, (wide_x, wide_y, wide_z), per),
         out_shape=(
-            jax.ShapeDtypeStruct(fields.shape, jnp.float32),
-            jax.ShapeDtypeStruct((features // 2, patches), jnp.bfloat16),
-            jax.ShapeDtypeStruct((features // 2, patches), jnp.bfloat16),
-            jax.ShapeDtypeStruct((2 * devices * per, EMBED), jnp.bfloat16),
+            shape(fields.shape, jnp.float32),
+            shape((features // 2, patches), jnp.bfloat16),
+            shape((features // 2, patches), jnp.bfloat16),
+            shape((send_rows, EMBED), jnp.bfloat16),
         ),
         in_specs=[smem] + [vmem] * 9,
-        out_specs=(vmem, vmem, vmem, vmem),
+        out_specs=(vmem,) * 4,
         scratch_shapes=[
             pltpu.VMEM(full, jnp.float32),
             pltpu.VMEM(full, jnp.float32),
@@ -399,9 +487,11 @@
             pltpu.VMEM((FIELDS * PATCH, PATCH * PATCH, patches), jnp.float32),
             pltpu.VMEM((features, 2 * patches), jnp.bfloat16),
         ],
-        compiler_params=pltpu.CompilerParams(vmem_limit_bytes=48 * 1024 * 1024),
+        compiler_params=grant(32),
         name="window",
-    )(edges, fields, xlo, xhi, ylo, yhi, lag, own_row, own_col, patch_weight)
+    )(
+        edges, fields, xlo, xhi, ylo, yhi, chosen, source_pick, target_pick, patch_weight
+    )
 
     pairs = [(i, i ^ 1) for i in range(n_x)]
     groups = [
@@ -410,31 +500,49 @@
     members = devices // 2
     got_picked = lax.ppermute(give, "gx", pairs)
     got = lax.all_to_all(send.reshape(devices, 2 * per, EMBED), axes, 0, 0, tiled=True)
-    source_grad, w_in_grad, b_in_grad, w_out_grad, b_out_grad = trainer_step(
-        got[:, :per].reshape(devices * per, EMBED),
-        got[:, per:].reshape(devices * per, EMBED),
-        w_in[0],
-        b_in[0],
-        w_out[0],
-        b_out[0],
-    )
-    back = lax.all_to_all(source_grad.reshape(devices, per, EMBED), axes, 0, 0, tiled=True)
+    rows = devices * per
+    hidden_size = w_in.shape[2]
+    width = EMBED // 2
+    source, hidden, error, pre_grad, b_in_grad, b_out_grad, back = pl.pallas_call(
+        functools.partial(trainer_kernel, per),
+        out_shape=(
+            shape((rows, EMBED), jnp.bfloat16),
+            shape((rows, hidden_size), jnp.bfloat16),
+            shape((rows, EMBED), jnp.bfloat16),
+            shape((rows, hidden_size), jnp.bfloat16),
+            shape((1, hidden_size), jnp.float32),
+            shape((1, EMBED), jnp.float32),
+            shape((2 * rows, width), jnp.bfloat16),
+        ),
+        in_specs=[vmem] * 5,
+        out_specs=(vmem,) * 7,
+        scratch_shapes=[
+            pltpu.VMEM((rows, EMBED), jnp.float32),
+            pltpu.VMEM((rows, hidden_size), jnp.float32),
+        ],
+        compiler_params=grant(32),
+        name="trainer",
+    )(got.reshape(send_rows, EMBED), w_in[0], b_in, w_out[0], b_out)
+    back = lax.all_to_all(back.reshape(devices, 2 * per, width), axes, 0, 0, tiled=True)
+    w_in_grad = contract_rows(source, pre_grad)
+    w_out_grad = contract_rows(hidden, error)
+    back, w_in_grad, w_out_grad = lax.optimization_barrier((back, w_in_grad, w_out_grad))
     own_grad = pl.pallas_call(
-        functools.partial(gather_kernel, devices * per, slots),
-        out_shape=jax.ShapeDtypeStruct((patches, EMBED), jnp.bfloat16),
+        gather_kernel,
+        out_shape=shape((patches, EMBED), jnp.bfloat16),
         in_specs=[vmem] * 3,
         out_specs=vmem,
+        compiler_params=grant(8),
         name="gather",
-    )(own_row, own_col, back.reshape(devices * per, EMBED))
+    )(source_pick, target_pick, back.reshape(send_rows, width))
     other_grad = lax.ppermute(own_grad, "gx", pairs)
-    width = EMBED // 2
     piece = features // members
     parts = pl.pallas_call(
         part_kernel,
         out_shape=jax.ShapeDtypeStruct((features, width), jnp.bfloat16),
         in_specs=[vmem] * 4,
         out_specs=vmem,
-        compiler_params=grant,
+        compiler_params=grant(16),
         name="part",
     )(keep, got_picked, own_grad, other_grad)
     parts = lax.all_to_all(
@@ -445,7 +553,7 @@
         out_shape=jax.ShapeDtypeStruct((members, piece, width), jnp.bfloat16),
         in_specs=[vmem],
         out_specs=vmem,
-        compiler_params=grant,
+        compiler_params=grant(16),
         name="total",
     )(parts)
     own_half = lax.all_to_all(copies, axes, 0, 0, axis_index_groups=groups, tiled=True)
@@ -456,16 +564,16 @@
         out_shape=jax.ShapeDtypeStruct((features, EMBED), jnp.float32),
         in_specs=[smem, vmem, vmem],
         out_specs=vmem,
-        compiler_params=grant,
+        compiler_params=grant(16),
         name="spread",
     )(edges[4:5], own_half, other_half)
     return (
         new_fields,
         patch_gradient,
         w_in_grad[None],
-        b_in_grad[None],
+        b_in_grad,
         w_out_grad[None],
-        b_out_grad[None],
+        b_out_grad,
     )
 
 

time: 197 us -> 174 us (0.88)
  blocking collectives: 81.8 us -> 47.8 us
  waiting for transfers between devices: 20.6 us -> 36.2 us
  starting transfers between devices: 22.5 us -> 37.4 us
  matrix products: 16.1 us -> 8.42 us
  local copies, waits for them, and re-layouts: 16.7 us -> 11.6 us
  other arithmetic: 5.25 us -> 1.53 us
  Pallas kernels: 32.2 us -> 29.8 us
    all_to_all x1 -> x0, blocking collectives: 33.6 us -> none  [per_device(): lax.all_to_all(send.reshape(devices, 2 * per, EMBED), axes, 0, 0, tiled=T...]
    all_to_all x1 -> x2, starting transfers between devices: 4.74 us -> 20 us  [the longest x1 15.3 us: per_device(): lax.all_to_all(send.reshape(devices, 2 * per, EMBED), axes, 0, 0, tiled=T...]
    all_to_all x1 -> x2, waiting for transfers between devices: 12.7 us -> 23.3 us  [the longest x1 17.8 us: per_device(): lax.all_to_all(send.reshape(devices, 2 * per, EMBED), axes, 0, 0, tiled=T...]
    dot_general x4 -> x0, matrix products: 9.37 us -> none  [the longest x2 4.36 us: contract_cols(): lax.dot_general(left, right, (((1,), (1,)), ((), ())), preferred_element_...]
    pallas_call x1, Pallas kernels: 25.6 us -> 17.3 us  [per_device(): pl.pallas_call(functools.partial(window_kernel, (wide_x, wide_y, wide_z),...]
    pallas_call x1 -> x3, Pallas kernels: 2.16 us -> 7.15 us  [the longest x1 6.44 us: per_device(): pl.pallas_call(functools.partial(trainer_kernel, per), out_shape=(shape((...]
    reshape x7 -> x0, local copies, waits for them, and re-layouts: 4.72 us -> none  [the longest x2 1.62 us: per_device(): jnp.repeat(jnp.repeat(lag_index.astype(jnp.float32), PATCH, axis=1), PATC...]
    convert_element_type x3 -> x1, other arithmetic: 3.76 us -> 0.01 us  [per_device(): lag = lag_index.reshape(-1, lag_index.shape[2]).astype(jnp.float32)]
  transfers between devices with their start and end apart: 8 -> 9, of which waited for: 5 -> 8; matrix products, arithmetic and copies ran while one was open for 6% -> 6% of each run, Pallas kernels for 1% -> 4%
where the time goes in v3:
time: 174 us
  blocking collectives  47.8 us (27%)
  starting transfers between devices  37.4 us (21%)
  waiting for transfers between devices  36.2 us (21%)
  Pallas kernels  29.8 us (17%)
  local copies, waits for them, and re-layouts  11.6 us (7%)
  matrix products  8.42 us (5%)
    all_to_all x1, blocking collectives, per_device(): lax.all_to_all(copies, axes, 0, 0, axis_index_groups=groups, tiled=True)  24.3 us
    all_to_all x1, blocking collectives, per_device(): lax.all_to_all(parts.reshape(members, piece, width), axes, 0, 0, axis_ind...  23.6 us
    all_to_all x1, waiting for transfers between devices, per_device(): lax.all_to_all(send.reshape(devices, 2 * per, EMBED), axes, 0, 0, tiled=T...  17.8 us
    pallas_call x1, Pallas kernels, per_device(): pl.pallas_call(functools.partial(window_kernel, (wide_x, wide_y, wide_z),...  17.3 us
    all_to_all x1, starting transfers between devices, per_device(): lax.all_to_all(send.reshape(devices, 2 * per, EMBED), axes, 0, 0, tiled=T...  15.3 us
    unnamed x38, local copies, waits for them, and re-layouts  10.4 us
    dot_general x2, matrix products, contract_rows(): lax.dot_general(left, right, (((0,), (0,)), ((), ())), preferred_element_...  8.42 us
    ppermute x2, starting transfers between devices, neighbours(): lax.ppermute(high_piece, axis, up)  6.74 us
  transfers between devices with their start and end apart: 9, of which 8 were waited for; matrix products, arithmetic and copies ran while one was open for 6% of the time, Pallas kernels for 4%

profile of v3, /device:TPU:1, one launch (start us, length us, event | category | flops | bytes accessed | tf_op | source)
XLA Modules:
  0.0 173.6 jit_solution(1713637232430768308)
XLA Ops:
  0.6 1.4 convert.6
  2.2 3.5 %collective-permute-start.1 = (bf16[5,6,32,128]{3,2,1,0:T(8,128)(2,1)S(1)}, bf16[5,6,32,128]{3,2,1,0:T(8,128)(2,1)S(1)}, u32[]{:S(2)}, u32[]{:S(2)}) collective-permute-start(bf16[5,6,32,128]{3,2,1,0:T(8,128)(2,1)S(1)} %get-tuple-element.42), channel_id=1, source_target_pairs={{8,0},{16,8},{24,16},{32,24},{40,32},{48,40},{56,48},{64,56},{72,6... | collective-permute-start | bytes 737288 | tf_op jit(solution)/shard_map/ppermute | solution.py:402
  5.6 3.5 %collective-permute-start = (bf16[5,6,32,128]{3,2,1,0:T(8,128)(2,1)S(1)}, bf16[5,6,32,128]{3,2,1,0:T(8,128)(2,1)S(1)}, u32[]{:S(2)}, u32[]{:S(2)}) collective-permute-start(bf16[5,6,32,128]{3,2,1,0:T(8,128)(2,1)S(1)} %get-tuple-element.43), channel_id=1, source_target_pairs={{0,8},{8,16},{16,24},{24,32},{32,40},{40,48},{48,56},{56,64},{64,7... | collective-permute-start | bytes 737288 | tf_op jit(solution)/shard_map/ppermute | solution.py:402
  9.2 1.9 %collective-permute-done.1.xhi_ref = bf16[5,6,32,128]{3,2,1,0:T(8,128)(2,1)S(1)} collective-permute-done((bf16[5,6,32,128]{3,2,1,0:T(8,128)(2,1)S(1)}, bf16[5,6,32,128]{3,2,1,0:T(8,128)(2,1)S(1)}, u32[]{:S(2)}, u32[]{:S(2)}) %collective-permute-start.1) | collective-permute-done | bytes 245792 | tf_op jit(solution)/shard_map/ppermute | solution.py:402
  11.1 2.8 %collective-permute-done.xlo_ref = bf16[5,6,32,128]{3,2,1,0:T(8,128)(2,1)S(1)} collective-permute-done((bf16[5,6,32,128]{3,2,1,0:T(8,128)(2,1)S(1)}, bf16[5,6,32,128]{3,2,1,0:T(8,128)(2,1)S(1)}, u32[]{:S(2)}, u32[]{:S(2)}) %collective-permute-start) | collective-permute-done | bytes 245792 | tf_op jit(solution)/shard_map/ppermute | solution.py:402
  14.0 3.2 %collective-permute-start.2 = (bf16[5,28,8,128]{3,2,1,0:T(8,128)(2,1)S(1)}, bf16[5,28,8,128]{3,2,1,0:T(8,128)(2,1)S(1)}, u32[]{:S(2)}, u32[]{:S(2)}) collective-permute-start(bf16[5,28,8,128]{3,2,1,0:T(8,128)(2,1)S(1)} %pad_maximum_fusion), channel_id=1, source_target_pairs={{0,1},{1,2},{2,3},{3,4},{4,5},{5,6},{6,7},{8,9},{9,10},{10,11},{11... | collective-permute-start | bytes 860168 | tf_op jit(solution)/shard_map/ppermute | solution.py:402
  17.2 1.3 collective-permute-start.3
  19.4 1.4 collective-permute-done.2.ylo_ref
  20.7 3.9 %collective-permute-done.3.yhi_ref = bf16[5,28,8,128]{3,2,1,0:T(8,128)(2,1)S(1)} collective-permute-done((bf16[5,28,8,128]{3,2,1,0:T(8,128)(2,1)S(1)}, bf16[5,28,8,128]{3,2,1,0:T(8,128)(2,1)S(1)}, u32[]{:S(2)}, u32[]{:S(2)}) %collective-permute-start.3) | collective-permute-done | bytes 286752 | tf_op jit(solution)/shard_map/ppermute | solution.py:402
  24.6 1.7 %copy-done.1 = bf16[2560,512]{1,0:T(8,128)(2,1)S(1)} copy-done((bf16[2560,512]{1,0:T(8,128)(2,1)S(1)}, bf16[2560,512]{1,0:T(8,128)(2,1)}, u32[]{:S(2)}) %copy-start.1) | copy-done | bytes 2621464
  26.4 17.3 %window.1 = (f32[5,16,32,128]{3,2,1,0:T(8,128)}, bf16[1280,128]{1,0:T(8,128)(2,1)S(1)}, bf16[1280,128]{1,0:T(8,128)(2,1)}, bf16[1024,512]{1,0:T(8,128)(2,1)}) custom-call(s32[5]{0:T(128)S(1)} %convert_element_type.12.edge_ref, f32[5,16,32,128]{3,2,1,0:T(8,128)S(1)} %copy-done, bf16[5,6,32,128]{3,2,1,0:T(8,128)(2,1)S(1)} %collective-permute-done.xlo_ref, ...), custom_call_target="tpu_custom_call" | custom-call | tf_op jit(solution)/shard_map/window/pallas_call | solution.py:473
  44.4 15.3 %all-to-all-start = ((bf16[128,8,512]{2,1,0:T(8,128)(2,1)}), bf16[128,8,512]{2,1,0:T(8,128)(2,1)S(1)}, u32[]{:S(2)}, u32[]{:S(2)}) async-start(bf16[128,8,512]{2,1,0:T(8,128)(2,1)} %bitcast.7), calls=%async_computation | async-start | bytes 2097152 | tf_op jit(solution)/shard_map/all_to_all | solution.py:502
  59.7 1.3 collective-permute-start.4
  61.0 17.8 %all-to-all-done = bf16[128,8,512]{2,1,0:T(8,128)(2,1)S(1)} async-done(((bf16[128,8,512]{2,1,0:T(8,128)(2,1)}), bf16[128,8,512]{2,1,0:T(8,128)(2,1)S(1)}, u32[]{:S(2)}, u32[]{:S(2)}) %all-to-all-start) | async-done | bytes 1048608 | tf_op jit(solution)/shard_map/all_to_all | solution.py:502
  78.8 1.6 copy-done.2
  80.4 1.6 copy-done.3
  82.0 6.4 %trainer.1 = (bf16[512,512]{1,0:T(8,128)(2,1)S(1)}, bf16[512,2048]{1,0:T(8,128)(2,1)S(1)}, bf16[512,512]{1,0:T(8,128)(2,1)S(1)}, bf16[512,2048]{1,0:T(8,128)(2,1...) custom-call(bf16[1024,512]{1,0:T(8,128)(2,1)S(1)} %bitcast.24, ...), custom_call_target="tpu_custom_call" | custom-call | tf_op jit(solution)/shard_map/trainer/pallas_call | solution.py:506
  88.5 1.3 copy-done.4
  90.6 0.8 copy-done.12
  92.2 4.7 %all-to-all-start.1 = ((bf16[128,8,256]{2,1,0:T(8,128)(2,1)}), bf16[128,8,256]{2,1,0:T(8,128)(2,1)S(1)}, u32[]{:S(2)}, u32[]{:S(2)}) async-start(bf16[128,8,256]{2,1,0:T(8,128)(2,1)} %bitcast.28), calls=%async_computation.1 | async-start | bytes 1048576 | tf_op jit(solution)/shard_map/all_to_all | solution.py:526
  96.9 5.1 %fusion.4 = f32[512,2048]{1,0:T(8,128)} fusion(bf16[512,512]{1,0:T(8,128)(2,1)} %copy-done.12, bf16[512,2048]{1,0:T(8,128)(2,1)} %copy-done.4), kind=kOutput, calls=%fused_computation.6 | convolution fusion | flops 1073741824 | bytes 6815744 | tf_op jit(solution)/shard_map/dot_general | solution.py:406
  102.0 3.3 %fusion.5 = f32[2048,512]{1,0:T(8,128)} fusion(bf16[512,2048]{1,0:T(8,128)(2,1)S(1)} %get-tuple-element.33, bf16[512,512]{1,0:T(8,128)(2,1)S(1)} %copy-done.10), kind=kOutput, calls=%fused_computation.7 | convolution fusion | flops 1073741824 | bytes 6815744 | tf_op jit(solution)/shard_map/dot_general | solution.py:406
  105.3 5.5 %all-to-all-done.1 = bf16[128,8,256]{2,1,0:T(8,128)(2,1)S(1)} async-done(((bf16[128,8,256]{2,1,0:T(8,128)(2,1)}), bf16[128,8,256]{2,1,0:T(8,128)(2,1)S(1)}, u32[]{:S(2)}, u32[]{:S(2)}) %all-to-all-start.1) | async-done | bytes 524320 | tf_op jit(solution)/shard_map/all_to_all | solution.py:526
  111.2 1.1 collective-permute-start.5
  112.3 1.0 collective-permute-done.5.other_grad_ref
  113.3 1.0 copy-done.14
  114.3 1.8 %part.1 = bf16[2560,256]{1,0:T(8,128)(2,1)S(1)} custom-call(bf16[1280,128]{1,0:T(8,128)(2,1)S(1)} %copy-done.14, bf16[1280,128]{1,0:T(8,128)(2,1)} %collective-permute-done.4.got_ref, bf16[128,512]{1,0:T(8,128)(2,1)S(1)} %gather.1.own_grad_ref, bf16[128,512]{1,0:T(8,128)(2,1)S(1)} %collective-permute-done.5.other_grad_ref), custom_call_target="tpu_custom_call" | custom-call | tf_op jit(solution)/shard_map/part/pallas_call | solution.py:540
  116.1 23.6 %all_to_all.20.parts_ref = bf16[64,40,256]{2,1,0:T(8,128)(2,1)S(1)} all-to-all(bf16[64,40,256]{2,1,0:T(8,128)(2,1)S(1)} %bitcast.21), channel_id=1, replica_groups={{0,1,2,3,4,5,6,7,16,17,18,19,20,21,22,23,32,33,34,35,36,37,38,39,48,49,..., dimensions={0} | all-to-all | bytes 2621440 | tf_op jit(solution)/shard_map/all_to_all | solution.py:548
  139.9 24.3 %all_to_all.21 = bf16[64,40,256]{2,1,0:T(8,128)(2,1)S(1)} all-to-all(bf16[64,40,256]{2,1,0:T(8,128)(2,1)S(1)} %total.1), channel_id=1, replica_groups={{0,1,2,3,4,5,6,7,16,17,18,19,20,21,22,23,32,33,34,35,36,37,38,39,48,49,..., dimensions={0} | all-to-all | bytes 2621440 | tf_op jit(solution)/shard_map/all_to_all | solution.py:559
  164.1 3.4 %collective-permute-start.6 = (bf16[2560,256]{1,0:T(8,128)(2,1)S(1)}, bf16[2560,256]{1,0:T(8,128)(2,1)S(1)}, u32[]{:S(2)}, u32[]{:S(2)}) collective-permute-start(bf16[2560,256]{1,0:T(8,128)(2,1)S(1)} %bitcast.22), channel_id=1, source_target_pairs={{0,8},{8,0},{16,24},{24,16},{32,40},{40,32},{48,56},{56,48},{64,72... | collective-permute-start | bytes 3932168 | tf_op jit(solution)/shard_map/ppermute | solution.py:561
  168.2 2.0 %collective-permute-done.6.other_ref = bf16[2560,256]{1,0:T(8,128)(2,1)S(1)} collective-permute-done((bf16[2560,256]{1,0:T(8,128)(2,1)S(1)}, bf16[2560,256]{1,0:T(8,128)(2,1)S(1)}, u32[]{:S(2)}, u32[]{:S(2)}) %collective-permute-start.6) | collective-permute-done | bytes 1310752 | tf_op jit(solution)/shard_map/ppermute | solution.py:561
  170.2 3.4 %spread.1 = f32[2560,512]{1,0:T(8,128)} custom-call(s32[1]{0:T(128)} %slice.39.core_ref, bf16[2560,256]{1,0:T(8,128)(2,1)S(1)} %bitcast.23, bf16[2560,256]{1,0:T(8,128)(2,1)S(1)} %collective-permute-done.6.other_ref), custom_call_target="tpu_custom_call" | custom-call | tf_op jit(solution)/shard_map/spread/pallas_call | solution.py:562
  (49 shorter events, 4.6 us)
Async XLA Ops:
  2.1 16.5 %copy-start.18 = (s32[64,1]{0,1:T(1,128)S(1)}, s32[64,1]{0,1:T(1,128)}, u32[]{:S(2)}) copy-start(s32[64,1]{0,1:T(1,128)} %param.10) | copy-start | bytes 772
  2.1 16.9 %copy-start.17 = (s32[2,4,16]{2,1,0:T(4,128)S(1)}, s32[2,4,16]{2,1,0:T(4,128)}, u32[]{:S(2)}) copy-start(s32[2,4,16]{2,1,0:T(4,128)} %param.11) | copy-start | bytes 1540
  2.1 22.5 %copy-start = (f32[5,16,32,128]{3,2,1,0:T(8,128)S(1)}, f32[5,16,32,128]{3,2,1,0:T(8,128)}, u32[]{:S(2)}) copy-start(f32[5,16,32,128]{3,2,1,0:T(8,128)} %f_ref.1) | copy-start | bytes 3932164
  2.2 8.9 %collective-permute-start.1 = (bf16[5,6,32,128]{3,2,1,0:T(8,128)(2,1)S(1)}, bf16[5,6,32,128]{3,2,1,0:T(8,128)(2,1)S(1)}, u32[]{:S(2)}, u32[]{:S(2)}) collective-permute-start(bf16[5,6,32,128]{3,2,1,0:T(8,128)(2,1)S(1)} %get-tuple-element.42), channel_id=1, source_target_pairs={{8,0},{16,8},{24,16},{32,24},{40,32},{48,40},{56,48},{64,56},{72,6... | collective-permute-start | bytes 737288 | tf_op jit(solution)/shard_map/ppermute | solution.py:402
  5.6 8.3 %collective-permute-start = (bf16[5,6,32,128]{3,2,1,0:T(8,128)(2,1)S(1)}, bf16[5,6,32,128]{3,2,1,0:T(8,128)(2,1)S(1)}, u32[]{:S(2)}, u32[]{:S(2)}) collective-permute-start(bf16[5,6,32,128]{3,2,1,0:T(8,128)(2,1)S(1)} %get-tuple-element.43), channel_id=1, source_target_pairs={{0,8},{8,16},{16,24},{24,32},{32,40},{40,48},{48,56},{56,64},{64,7... | collective-permute-start | bytes 737288 | tf_op jit(solution)/shard_map/ppermute | solution.py:402
  14.0 6.8 %collective-permute-start.2 = (bf16[5,28,8,128]{3,2,1,0:T(8,128)(2,1)S(1)}, bf16[5,28,8,128]{3,2,1,0:T(8,128)(2,1)S(1)}, u32[]{:S(2)}, u32[]{:S(2)}) collective-permute-start(bf16[5,28,8,128]{3,2,1,0:T(8,128)(2,1)S(1)} %pad_maximum_fusion), channel_id=1, source_target_pairs={{0,1},{1,2},{2,3},{3,4},{4,5},{5,6},{6,7},{8,9},{9,10},{10,11},{11... | collective-permute-start | bytes 860168 | tf_op jit(solution)/shard_map/ppermute | solution.py:402
  17.2 7.4 %collective-permute-start.3 = (bf16[5,28,8,128]{3,2,1,0:T(8,128)(2,1)S(1)}, bf16[5,28,8,128]{3,2,1,0:T(8,128)(2,1)S(1)}, u32[]{:S(2)}, u32[]{:S(2)}) collective-permute-start(bf16[5,28,8,128]{3,2,1,0:T(8,128)(2,1)S(1)} %pad_maximum_fusion.1), channel_id=1, source_target_pairs={{1,0},{2,1},{3,2},{4,3},{5,4},{6,5},{7,6},{9,8},{10,9},{11,10},{12... | collective-permute-start | bytes 860168 | tf_op jit(solution)/shard_map/ppermute | solution.py:402
  19.3 24.3 %copy-start.5 = (bf16[1024,128]{1,0:T(8,128)(2,1)}, bf16[1024,128]{1,0:T(8,128)(2,1)S(1)}, u32[]{:S(2)}) copy-start(bf16[1024,128]{1,0:T(8,128)(2,1)S(1)} %get-tuple-element.24.source_pick_ref) | copy-start | bytes 786436
  19.3 24.3 %copy-start.7 = (bf16[1024,128]{1,0:T(8,128)(2,1)}, bf16[1024,128]{1,0:T(8,128)(2,1)S(1)}, u32[]{:S(2)}) copy-start(bf16[1024,128]{1,0:T(8,128)(2,1)S(1)} %get-tuple-element.25.target_pick_ref) | copy-start | bytes 786436
  24.6 1.7 %copy-start.1 = (bf16[2560,512]{1,0:T(8,128)(2,1)S(1)}, bf16[2560,512]{1,0:T(8,128)(2,1)}, u32[]{:S(2)}) copy-start(bf16[2560,512]{1,0:T(8,128)(2,1)} %w_ref.1) | copy-start | bytes 7864324
  43.6 0.8 copy-start.13
  44.4 34.5 %copy-start.15 = (f32[1,2048]{1,0:T(1,128)S(1)}, f32[1,2048]{1,0:T(1,128)}, u32[]{:S(2)}) copy-start(f32[1,2048]{1,0:T(1,128)} %b_in_ref.1) | copy-start | bytes 24580
  44.4 34.5 %copy-start.16 = (f32[1,512]{1,0:T(1,128)S(1)}, f32[1,512]{1,0:T(1,128)}, u32[]{:S(2)}) copy-start(f32[1,512]{1,0:T(1,128)} %b_out_ref.1) | copy-start | bytes 6148
  44.4 34.4 %all-to-all-start = ((bf16[128,8,512]{2,1,0:T(8,128)(2,1)}), bf16[128,8,512]{2,1,0:T(8,128)(2,1)S(1)}, u32[]{:S(2)}, u32[]{:S(2)}) async-start(bf16[128,8,512]{2,1,0:T(8,128)(2,1)} %bitcast.7), calls=%async_computation | async-start | bytes 2097152 | tf_op jit(solution)/shard_map/all_to_all | solution.py:502
  59.7 52.6 %collective-permute-start.4 = (bf16[1280,128]{1,0:T(8,128)(2,1)}, bf16[1280,128]{1,0:T(8,128)(2,1)}, u32[]{:S(2)}, u32[]{:S(2)}) collective-permute-start(bf16[1280,128]{1,0:T(8,128)(2,1)} %get-tuple-element.28), channel_id=1, source_target_pairs={{0,8},{8,0},{16,24},{24,16},{32,40},{40,32},{48,56},{56,48},{64,72... | collective-permute-start | bytes 983048 | tf_op jit(solution)/shard_map/ppermute | solution.py:501
  78.8 1.6 copy-start.2
  80.4 1.6 copy-start.3
  88.5 1.3 copy-start.4
  89.8 0.8 copy-start.9
  90.6 0.8 copy-start.12
  91.4 0.8 copy-start.11
  92.2 18.7 %all-to-all-start.1 = ((bf16[128,8,256]{2,1,0:T(8,128)(2,1)}), bf16[128,8,256]{2,1,0:T(8,128)(2,1)S(1)}, u32[]{:S(2)}, u32[]{:S(2)}) async-start(bf16[128,8,256]{2,1,0:T(8,128)(2,1)} %bitcast.28), calls=%async_computation.1 | async-start | bytes 1048576 | tf_op jit(solution)/shard_map/all_to_all | solution.py:526
  96.9 5.1 %copy-start.10 = (bf16[512,512]{1,0:T(8,128)(2,1)S(1)}, bf16[512,512]{1,0:T(8,128)(2,1)}, u32[]{:S(2)}) copy-start(bf16[512,512]{1,0:T(8,128)(2,1)} %copy-done.9) | copy-start | bytes 1572868
  102.0 8.8 %copy-start.6 = (bf16[1024,128]{1,0:T(8,128)(2,1)S(1)}, bf16[1024,128]{1,0:T(8,128)(2,1)}, u32[]{:S(2)}) copy-start(bf16[1024,128]{1,0:T(8,128)(2,1)} %copy-done.5) | copy-start | bytes 786436
  102.0 8.8 %copy-start.8 = (bf16[1024,128]{1,0:T(8,128)(2,1)S(1)}, bf16[1024,128]{1,0:T(8,128)(2,1)}, u32[]{:S(2)}) copy-start(bf16[1024,128]{1,0:T(8,128)(2,1)} %copy-done.7) | copy-start | bytes 786436
  111.2 2.1 %collective-permute-start.5 = (bf16[128,512]{1,0:T(8,128)(2,1)S(1)}, bf16[128,512]{1,0:T(8,128)(2,1)S(1)}, u32[]{:S(2)}, u32[]{:S(2)}) collective-permute-start(bf16[128,512]{1,0:T(8,128)(2,1)S(1)} %gather.1.own_grad_ref), channel_id=1, source_target_pairs={{0,8},{8,0},{16,24},{24,16},{32,40},{40,32},{48,56},{56,48},{64,72... | collective-permute-start | bytes 393224 | tf_op jit(solution)/shard_map/ppermute | solution.py:538
  113.3 1.0 copy-start.14
  164.1 6.1 %collective-permute-start.6 = (bf16[2560,256]{1,0:T(8,128)(2,1)S(1)}, bf16[2560,256]{1,0:T(8,128)(2,1)S(1)}, u32[]{:S(2)}, u32[]{:S(2)}) collective-permute-start(bf16[2560,256]{1,0:T(8,128)(2,1)S(1)} %bitcast.22), channel_id=1, source_target_pairs={{0,8},{8,0},{16,24},{24,16},{32,40},{40,32},{48,56},{56,48},{64,72... | collective-permute-start | bytes 3932168 | tf_op jit(solution)/shard_map/ppermute | solution.py:561

commit v4 on v3

--- a/solution.py
+++ b/solution.py
@@ -115,6 +115,40 @@
     )
 
 
+def strip_layers(wide_x):
+    layers, place = [], 0
+    for layer in range(REACH):
+        beside = REACH - LIFT // 4 if layer < 4 else 0
+        rows = wide_x + 2 * beside
+        layers.append((layer, beside, rows, place))
+        place += rows
+    return layers, place
+
+
+def strips_kernel(f_ref, xlo_ref, xhi_ref, first_ref, last_ref, lines_ref):
+    wide_x, wide_y = f_ref.shape[1], f_ref.shape[2]
+    layers, _ = strip_layers(wide_x)
+    beside = layers[0][1]
+    for at, out_ref in ((0, first_ref), (wide_y - LIFT, last_ref)):
+        tile = slice(at, at + LIFT)
+        for row in range(wide_x + 2 * beside):
+            place = slice(row * LIFT, (row + 1) * LIFT)
+            if row < beside:
+                piece = xlo_ref[:, REACH - beside + row, tile].astype(jnp.float32)
+            elif row < beside + wide_x:
+                piece = f_ref[:, row - beside, tile]
+            else:
+                piece = xhi_ref[:, row - beside - wide_x, tile].astype(jnp.float32)
+            lines_ref[:, place] = piece
+        for field in range(FIELDS):
+            for layer, near, rows, place in layers:
+                line = layer if at == 0 else LIFT - 1 - layer
+                start = (beside - near) * LIFT + line
+                out_ref[field, place : place + rows] = lines_ref[
+                    field, pl.ds(start, rows, stride=LIFT), :
+                ].astype(jnp.bfloat16)
+
+
 def window_kernel(
     shape,
     per,
@@ -127,17 +161,23 @@
     chosen_ref,
     source_pick_ref,
     target_pick_ref,
-    w_ref,
-    new_ref,
-    keep_ref,
-    give_ref,
-    send_ref,
+    w_hbm,
+    new_hbm,
+    keep_hbm,
+    give_hbm,
+    send_hbm,
     first_ref,
     second_ref,
     shuffle_ref,
     natural_ref,
     both_ref,
+    w_ref,
+    new_ref,
+    send_ref,
+    done,
 ):
+    load_w = pltpu.make_async_copy(w_hbm, w_ref, done.at[0])
+    load_w.start()
     wide_x, wide_y, wide_z = shape
     patches = (wide_x // PATCH) * (wide_y // PATCH) * (wide_z // PATCH)
     top_x, top_y = REACH + wide_x, LIFT + wide_y
@@ -150,8 +190,16 @@
     first_ref[:, REACH:top_x, LIFT:top_y, :] = f_ref[...]
     first_ref[:, 0:REACH, LIFT:top_y, :] = xlo_ref[...].astype(jnp.float32)
     first_ref[:, top_x:full_x, LIFT:top_y, :] = xhi_ref[...].astype(jnp.float32)
-    first_ref[:, :, 0:LIFT, :] = ylo_ref[...].astype(jnp.float32)
-    first_ref[:, :, top_y:full_y, :] = yhi_ref[...].astype(jnp.float32)
+    for field in range(FIELDS):
+        for layer, beside, lines, place in strip_layers(wide_x)[0]:
+            rows = slice(REACH - beside, REACH - beside + lines)
+            packed = slice(place, place + lines)
+            first_ref[field, rows, LIFT - 1 - layer, :] = ylo_ref[field, packed].astype(
+                jnp.float32
+            )
+            first_ref[field, rows, top_y + layer, :] = yhi_ref[field, packed].astype(
+                jnp.float32
+            )
 
     def clear(ref, least):
         @pl.when(edge_ref[0] == 1)
@@ -253,50 +301,93 @@
     step(first_ref, second_ref, 2)
     step(second_ref, first_ref, 4)
     last_step(first_ref)
+    store_new = pltpu.make_async_copy(new_ref, new_hbm, done.at[1])
+    store_new.start()
     into_patches(chosen, keep_picked)
     into_patches(lambda field: new_ref[field], keep_target)
 
-    embedded = lax.dot_general(
-        both_ref[...], w_ref[...], (((0,), (0,)), ((), ())), preferred_element_type=jnp.float32
-    ).astype(jnp.bfloat16)
     half = both_ref.shape[0] // 2
     mine = pl.multiple_of(edge_ref[4] * half, half)
-    keep_ref[...] = both_ref[pl.ds(mine, half), 0:patches]
-    give_ref[...] = both_ref[pl.ds(half - mine, half), 0:patches]
+    lanes = slice(0, patches)
+    store_keep = pltpu.make_async_copy(both_ref.at[pl.ds(mine, half), lanes], keep_hbm, done.at[2])
+    store_give = pltpu.make_async_copy(
+        both_ref.at[pl.ds(half - mine, half), lanes], give_hbm, done.at[3]
+    )
+    store_give.start()
+    store_keep.start()
+    load_w.wait()
+    embedded = contract_rows(both_ref[...], w_ref[...]).astype(jnp.bfloat16)
     rows = send_ref.shape[0]
-    filled = jnp.sum(target_pick_ref[...].astype(jnp.float32), axis=1, keepdims=True)
-    target_half = (lax.broadcasted_iota(jnp.int32, (rows, 1), 0) // per) % 2 == 1
-    marker = jnp.where(target_half & (filled == 0.0), EMPTY, 0.0)
-    placed = jnp.dot(
-        source_pick_ref[...], embedded[0:patches], preferred_element_type=jnp.float32
-    )
-    placed = placed + jnp.dot(
-        target_pick_ref[...],
-        embedded[patches : 2 * patches],
-        preferred_element_type=jnp.float32,
-    )
-    send_ref[...] = (placed + marker).astype(jnp.bfloat16)
+    pieces = 4
+    stores = []
+    for piece in range(pieces):
+        lines = slice(piece * rows // pieces, (piece + 1) * rows // pieces)
+        wanted = target_pick_ref[lines]
+        filled = jnp.sum(wanted.astype(jnp.float32), axis=1, keepdims=True)
+        line = lax.broadcasted_iota(jnp.int32, (rows // pieces, 1), 0)
+        marker = jnp.where((line // per % 2 == 1) & (filled == 0.0), EMPTY, 0.0)
+        placed = jnp.dot(
+            source_pick_ref[lines], embedded[0:patches], preferred_element_type=jnp.float32
+        )
+        placed = placed + jnp.dot(
+            wanted, embedded[patches : 2 * patches], preferred_element_type=jnp.float32
+        )
+        send_ref[lines] = (placed + marker).astype(jnp.bfloat16)
+        store = pltpu.make_async_copy(send_ref.at[lines], send_hbm.at[lines], done.at[4 + piece])
+        store.start()
+        stores.append(store)
+    for store in [store_new, store_keep, store_give] + stores:
+        store.wait()
 
 
 def trainer_kernel(
     per,
     got_ref,
-    w_in_ref,
+    w_in_hbm,
     b_in_ref,
-    w_out_ref,
+    w_out_hbm,
     b_out_ref,
+    source_hbm,
+    hidden_hbm,
+    error_hbm,
+    pre_grad_hbm,
+    b_in_grad_ref,
+    b_out_grad_ref,
+    back_hbm,
+    target_ref,
+    slope_ref,
     source_ref,
     hidden_ref,
     error_ref,
     pre_grad_ref,
-    b_in_grad_ref,
-    b_out_grad_ref,
     back_ref,
-    target_ref,
-    slope_ref,
+    w_in_ref,
+    w_out_ref,
+    loaded,
+    stored,
 ):
+    chunk = 512
+    hidden_size = hidden_ref.shape[1]
+    starts = range(0, hidden_size, chunk)
+    loads = []
+    for at, start in enumerate(starts):
+        lanes = slice(start, start + chunk)
+        pair = (
+            pltpu.make_async_copy(w_in_hbm.at[:, lanes], w_in_ref.at[:, lanes], loaded.at[2 * at]),
+            pltpu.make_async_copy(w_out_hbm.at[lanes], w_out_ref.at[lanes], loaded.at[2 * at + 1]),
+        )
+        for load in pair:
+            load.start()
+        loads.append(pair)
+    stores = []
+
+    def store(src, dst):
+        copy = pltpu.make_async_copy(src, dst, stored.at[len(stores)])
+        copy.start()
+        stores.append(copy)
+
     rows = source_ref.shape[0]
-    width = back_ref.shape[1]
+    width = back_hbm.shape[1]
     small, large = 32 * per, 64 * per
     line = lax.broadcasted_iota(jnp.int32, (small, large), 0)
     taken = lax.broadcasted_iota(jnp.int32, (small, large), 1)
@@ -311,17 +402,19 @@
         ).astype(jnp.bfloat16)
         target_ref[lines] = jnp.dot(target_pick, block, preferred_element_type=jnp.float32)
 
-    chunk = 512
-    hidden_size = hidden_ref.shape[1]
+    store(source_ref, source_hbm)
     source = source_ref[...]
     predict = jnp.broadcast_to(b_out_ref[...], target_ref.shape)
-    for start in range(0, hidden_size, chunk):
+    for at, start in enumerate(starts):
         lanes = slice(start, start + chunk)
+        for load in loads[at]:
+            load.wait()
         pre = jnp.dot(source, w_in_ref[:, lanes], preferred_element_type=jnp.float32)
         pre = pre + b_in_ref[:, lanes]
         sigma = jax.nn.sigmoid(pre)
         hidden = (pre * sigma).astype(jnp.bfloat16)
         hidden_ref[:, lanes] = hidden
+        store(hidden_ref.at[:, lanes], hidden_hbm.at[:, lanes])
         slope_ref[:, lanes] = sigma * (1.0 + pre * (1.0 - sigma))
         predict = predict + jnp.dot(
             hidden, w_out_ref[lanes], preferred_element_type=jnp.float32
@@ -330,13 +423,15 @@
     error = jnp.where(wanted < FULL_BELOW, error_weight * (predict - wanted), 0.0)
     error = error.astype(jnp.bfloat16)
     error_ref[...] = error
+    store(error_ref, error_hbm)
     b_out_grad_ref[...] = jnp.sum(error.astype(jnp.float32), axis=0, keepdims=True)
     total = jnp.zeros(target_ref.shape, jnp.float32)
-    for start in range(0, hidden_size, chunk):
+    for start in starts:
         lanes = slice(start, start + chunk)
         upstream = contract_cols(error, w_out_ref[lanes])
         pre_grad = (upstream * slope_ref[:, lanes]).astype(jnp.bfloat16)
         pre_grad_ref[:, lanes] = pre_grad
+        store(pre_grad_ref.at[:, lanes], pre_grad_hbm.at[:, lanes])
         b_in_grad_ref[:, lanes] = jnp.sum(
             pre_grad.astype(jnp.float32), axis=0, keepdims=True
         )
@@ -356,7 +451,11 @@
                 gradient[lines, half * width : (half + 1) * width],
                 preferred_element_type=jnp.float32,
             )
-        back_ref[at * large : (at + 1) * large] = block.astype(jnp.bfloat16)
+        lines = slice(at * large, (at + 1) * large)
+        back_ref[lines] = block.astype(jnp.bfloat16)
+        store(back_ref.at[lines], back_hbm.at[lines])
+    for copy in stores:
+        copy.wait()
 
 
 def gather_kernel(source_pick_ref, target_pick_ref, back_ref, out_ref):
@@ -367,10 +466,20 @@
         ).astype(jnp.bfloat16)
 
 
-def part_kernel(keep_ref, got_ref, own_grad_ref, other_grad_ref, part_ref):
+def part_kernel(
+    keep_hbm, got_hbm, own_grad_ref, other_grad_ref, part_ref, keep_ref, got_ref, loaded
+):
+    loads = (
+        pltpu.make_async_copy(keep_hbm, keep_ref, loaded.at[0]),
+        pltpu.make_async_copy(got_hbm, got_ref, loaded.at[1]),
+    )
+    for load in loads:
+        load.start()
     half = keep_ref.shape[0]
     width = part_ref.shape[1]
+    loads[0].wait()
     total = jnp.dot(keep_ref[...], own_grad_ref[...], preferred_element_type=jnp.float32)
+    loads[1].wait()
     total = total + jnp.dot(
         got_ref[...], other_grad_ref[...], preferred_element_type=jnp.float32
     )
@@ -385,14 +494,27 @@
     copies_ref[...] = jnp.broadcast_to(total[None], copies_ref.shape)
 
 
-def spread_kernel(core_ref, own_ref, other_ref, out_ref):
-    half, width = out_ref.shape[0] // 2, own_ref.shape[1]
-    mine = pl.multiple_of(core_ref[0] * half, half)
-    for side in range(EMBED // width):
-        lanes = slice(side * width, (side + 1) * width)
-        rows = slice(side * half, (side + 1) * half)
-        out_ref[pl.ds(mine, half), lanes] = own_ref[rows].astype(jnp.float32)
-        out_ref[pl.ds(half - mine, half), lanes] = other_ref[rows].astype(jnp.float32)
+def spread_kernel(other, edge_ref, half_ref, *rest):
+    out_hbm, wide_ref, done = rest[-3:]
+    half, width = wide_ref.shape[0], half_ref.shape[1]
+    core = 1 - edge_ref[4] if other else edge_ref[4]
+    begin = core * half
+    pieces = 4
+    stores = []
+    for piece in range(pieces):
+        lines = slice(piece * half // pieces, (piece + 1) * half // pieces)
+        for side in range(EMBED // width):
+            lanes = slice(side * width, (side + 1) * width)
+            rows = slice(side * half + lines.start, side * half + lines.stop)
+            wide_ref[lines, lanes] = half_ref[rows].astype(jnp.float32)
+        at = pl.multiple_of(begin + lines.start, half // pieces)
+        store = pltpu.make_async_copy(
+            wide_ref.at[lines], out_hbm.at[pl.ds(at, half // pieces)], done.at[piece]
+        )
+        store.start()
+        stores.append(store)
+    for store in stores:
+        store.wait()
 
 
 def neighbours(low_piece, high_piece, axis):
@@ -429,15 +551,6 @@
         return piece.astype(jnp.bfloat16)
 
     xlo, xhi = neighbours(narrow(fields[:, :REACH]), narrow(fields[:, wide_x - REACH :]), "gx")
-    y_first = jnp.concatenate(
-        [xlo[:, :, :LIFT], narrow(fields[:, :, :LIFT]), xhi[:, :, :LIFT]], axis=1
-    )
-    at = wide_y - LIFT
-    y_last = jnp.concatenate(
-        [xlo[:, :, at:], narrow(fields[:, :, at:]), xhi[:, :, at:]], axis=1
-    )
-    ylo, yhi = neighbours(y_first, y_last, "gy")
-
     at_x, at_y = lax.axis_index("gx"), lax.axis_index("gy")
     core = at_x % 2
     edges = jnp.stack(
@@ -448,12 +561,25 @@
 
     vmem = pl.BlockSpec(memory_space=pltpu.VMEM)
     smem = pl.BlockSpec(memory_space=pltpu.SMEM)
+    hbm = pl.BlockSpec(memory_space=pltpu.HBM)
 
     def grant(mebibytes):
         return pltpu.CompilerParams(vmem_limit_bytes=mebibytes * 1024 * 1024)
 
     def shape(dims, kind):
         return jax.ShapeDtypeStruct(dims, kind)
+
+    layers, strip = strip_layers(wide_x)
+    y_first, y_last = pl.pallas_call(
+        strips_kernel,
+        out_shape=(shape((FIELDS, strip, wide_z), jnp.bfloat16),) * 2,
+        in_specs=[vmem] * 3,
+        out_specs=(vmem,) * 2,
+        scratch_shapes=[pltpu.VMEM((FIELDS, layers[0][2] * LIFT, wide_z), jnp.float32)],
+        compiler_params=grant(8),
+        name="strips",
+    )(fields, xlo, xhi)
+    ylo, yhi = neighbours(y_first, y_last, "gy")
 
     send_rows = 2 * devices * per
     source_pick, target_pick, chosen = pl.pallas_call(
@@ -478,14 +604,18 @@
             shape((features // 2, patches), jnp.bfloat16),
             shape((send_rows, EMBED), jnp.bfloat16),
         ),
-        in_specs=[smem] + [vmem] * 9,
-        out_specs=(vmem,) * 4,
+        in_specs=[smem] + [vmem] * 8 + [hbm],
+        out_specs=(hbm,) * 4,
         scratch_shapes=[
             pltpu.VMEM(full, jnp.float32),
             pltpu.VMEM(full, jnp.float32),
             pltpu.VMEM((FIELDS, wide_x, wide_y, wide_z), jnp.float32),
             pltpu.VMEM((FIELDS * PATCH, PATCH * PATCH, patches), jnp.float32),
             pltpu.VMEM((features, 2 * patches), jnp.bfloat16),
+            pltpu.VMEM((features, EMBED), jnp.bfloat16),
+            pltpu.VMEM((FIELDS, wide_x, wide_y, wide_z), jnp.float32),
+            pltpu.VMEM((send_rows, EMBED), jnp.bfloat16),
+            pltpu.SemaphoreType.DMA((8,)),
         ],
         compiler_params=grant(32),
         name="window",
@@ -514,11 +644,20 @@
             shape((1, EMBED), jnp.float32),
             shape((2 * rows, width), jnp.bfloat16),
         ),
-        in_specs=[vmem] * 5,
-        out_specs=(vmem,) * 7,
+        in_specs=[vmem, hbm, vmem, hbm, vmem],
+        out_specs=(hbm, hbm, hbm, hbm, vmem, vmem, hbm),
         scratch_shapes=[
             pltpu.VMEM((rows, EMBED), jnp.float32),
             pltpu.VMEM((rows, hidden_size), jnp.float32),
+            pltpu.VMEM((rows, EMBED), jnp.bfloat16),
+            pltpu.VMEM((rows, hidden_size), jnp.bfloat16),
+            pltpu.VMEM((rows, EMBED), jnp.bfloat16),
+            pltpu.VMEM((rows, hidden_size), jnp.bfloat16),
+            pltpu.VMEM((2 * rows, width), jnp.bfloat16),
+            pltpu.VMEM((EMBED, hidden_size), jnp.bfloat16),
+            pltpu.VMEM((hidden_size, EMBED), jnp.bfloat16),
+            pltpu.SemaphoreType.DMA((8,)),
+            pltpu.SemaphoreType.DMA((16,)),
         ],
         compiler_params=grant(32),
         name="trainer",
@@ -539,9 +678,14 @@
     piece = features // members
     parts = pl.pallas_call(
         part_kernel,
-        out_shape=jax.ShapeDtypeStruct((features, width), jnp.bfloat16),
-        in_specs=[vmem] * 4,
+        out_shape=shape((features, width), jnp.bfloat16),
+        in_specs=[hbm, hbm, vmem, vmem],
         out_specs=vmem,
+        scratch_shapes=[
+            pltpu.VMEM((features // 2, patches), jnp.bfloat16),
+            pltpu.VMEM((features // 2, patches), jnp.bfloat16),
+            pltpu.SemaphoreType.DMA((2,)),
+        ],
         compiler_params=grant(16),
         name="part",
     )(keep, got_picked, own_grad, other_grad)
@@ -559,14 +703,24 @@
     own_half = lax.all_to_all(copies, axes, 0, 0, axis_index_groups=groups, tiled=True)
     own_half = own_half.reshape(features, width)
     other_half = lax.ppermute(own_half, "gx", pairs)
-    patch_gradient = pl.pallas_call(
-        spread_kernel,
-        out_shape=jax.ShapeDtypeStruct((features, EMBED), jnp.float32),
-        in_specs=[smem, vmem, vmem],
-        out_specs=vmem,
-        compiler_params=grant(16),
-        name="spread",
-    )(edges[4:5], own_half, other_half)
+
+    def spread(other, *operands):
+        return pl.pallas_call(
+            functools.partial(spread_kernel, other),
+            out_shape=shape((features, EMBED), jnp.float32),
+            in_specs=[smem, vmem] + [hbm] * (len(operands) - 2),
+            out_specs=hbm,
+            scratch_shapes=[
+                pltpu.VMEM((features // 2, EMBED), jnp.float32),
+                pltpu.SemaphoreType.DMA((4,)),
+            ],
+            input_output_aliases={2: 0} if other else {},
+            compiler_params=grant(8),
+            name="spread_other" if other else "spread_own",
+        )(*operands)
+
+    patch_gradient = spread(False, edges, own_half)
+    patch_gradient = spread(True, edges, other_half, patch_gradient)
     return (
         new_fields,
         patch_gradient,

time: 174 us -> 177 us (1.017)
  Pallas kernels: 29.8 us -> 36 us
  waiting for transfers between devices: 36.2 us -> 33.5 us
    pallas_call x1, Pallas kernels: 6.44 us -> 12.2 us  [per_device(): pl.pallas_call(functools.partial(trainer_kernel, per), out_shape=(shape((...]
    pallas_call x2 -> x4, Pallas kernels: 5.2 us -> 6.32 us  [the longest x2 4.2 us: spread(): pl.pallas_call(functools.partial(spread_kernel, other), out_shape=shape((...]
    unnamed x38 -> x36, local copies, waits for them, and re-layouts: 10.4 us -> 11.3 us
  transfers between devices with their start and end apart: 9 -> 9, of which waited for: 8 -> 8; matrix products, arithmetic and copies ran while one was open for 6% -> 5% of each run, Pallas kernels for 4% -> 8%
where the time goes in v4:
time: 177 us
  blocking collectives  47.8 us (27%)
  starting transfers between devices  36.6 us (21%)
  Pallas kernels  36 us (20%)
  waiting for transfers between devices  33.5 us (19%)
  local copies, waits for them, and re-layouts  11.7 us (7%)
  matrix products  8.42 us (5%)
    all_to_all x1, blocking collectives, per_device(): lax.all_to_all(copies, axes, 0, 0, axis_index_groups=groups, tiled=True)  24.3 us
    all_to_all x1, blocking collectives, per_device(): lax.all_to_all(parts.reshape(members, piece, width), axes, 0, 0, axis_ind...  23.6 us
    all_to_all x1, waiting for transfers between devices, per_device(): lax.all_to_all(send.reshape(devices, 2 * per, EMBED), axes, 0, 0, tiled=T...  17.8 us
    pallas_call x1, Pallas kernels, per_device(): pl.pallas_call(functools.partial(window_kernel, (wide_x, wide_y, wide_z),...  16.5 us
    all_to_all x1, starting transfers between devices, per_device(): lax.all_to_all(send.reshape(devices, 2 * per, EMBED), axes, 0, 0, tiled=T...  14.7 us
    pallas_call x1, Pallas kernels, per_device(): pl.pallas_call(functools.partial(trainer_kernel, per), out_shape=(shape((...  12.2 us
    unnamed x36, local copies, waits for them, and re-layouts  11.3 us
    dot_general x2, matrix products, contract_rows(): lax.dot_general(left, right, (((0,), (0,)), ((), ())), preferred_element_...  8.42 us
  transfers between devices with their start and end apart: 9, of which 8 were waited for; matrix products, arithmetic and copies ran while one was open for 5% of the time, Pallas kernels for 8%

profile of v4, /device:TPU:1, one launch (start us, length us, event | category | flops | bytes accessed | tf_op | source)
XLA Modules:
  0.0 176.7 jit_solution(15800762342988583621)
XLA Ops:
  0.7 1.5 convert.4
  2.2 3.3 %collective-permute-start.1 = (bf16[5,6,32,128]{3,2,1,0:T(8,128)(2,1)S(1)}, bf16[5,6,32,128]{3,2,1,0:T(8,128)(2,1)S(1)}, u32[]{:S(2)}, u32[]{:S(2)}) collective-permute-start(bf16[5,6,32,128]{3,2,1,0:T(8,128)(2,1)S(1)} %get-tuple-element.44), channel_id=1, source_target_pairs={{8,0},{16,8},{24,16},{32,24},{40,32},{48,40},{56,48},{64,56},{72,6... | collective-permute-start | bytes 737288 | tf_op jit(solution)/shard_map/ppermute | solution.py:524
  5.6 3.5 %collective-permute-start = (bf16[5,6,32,128]{3,2,1,0:T(8,128)(2,1)S(1)}, bf16[5,6,32,128]{3,2,1,0:T(8,128)(2,1)S(1)}, u32[]{:S(2)}, u32[]{:S(2)}) collective-permute-start(bf16[5,6,32,128]{3,2,1,0:T(8,128)(2,1)S(1)} %get-tuple-element.45), channel_id=1, source_target_pairs={{0,8},{8,16},{16,24},{24,32},{32,40},{40,48},{48,56},{56,64},{64,7... | collective-permute-start | bytes 737288 | tf_op jit(solution)/shard_map/ppermute | solution.py:524
  9.1 1.9 %collective-permute-done.1.xhi_ref = bf16[5,6,32,128]{3,2,1,0:T(8,128)(2,1)S(1)} collective-permute-done((bf16[5,6,32,128]{3,2,1,0:T(8,128)(2,1)S(1)}, bf16[5,6,32,128]{3,2,1,0:T(8,128)(2,1)S(1)}, u32[]{:S(2)}, u32[]{:S(2)}) %collective-permute-start.1) | collective-permute-done | bytes 245792 | tf_op jit(solution)/shard_map/ppermute | solution.py:524
  11.1 2.8 %collective-permute-done.xlo_ref = bf16[5,6,32,128]{3,2,1,0:T(8,128)(2,1)S(1)} collective-permute-done((bf16[5,6,32,128]{3,2,1,0:T(8,128)(2,1)S(1)}, bf16[5,6,32,128]{3,2,1,0:T(8,128)(2,1)S(1)}, u32[]{:S(2)}, u32[]{:S(2)}) %collective-permute-start) | collective-permute-done | bytes 245792 | tf_op jit(solution)/shard_map/ppermute | solution.py:524
  14.1 3.2 %collective-permute-start.2 = (bf16[5,128,128]{2,1,0:T(8,128)(2,1)S(1)}, bf16[5,128,128]{2,1,0:T(8,128)(2,1)S(1)}, u32[]{:S(2)}, u32[]{:S(2)}) collective-permute-start(bf16[5,128,128]{2,1,0:T(8,128)(2,1)S(1)} %get-tuple-element.25), channel_id=1, source_target_pairs={{0,1},{1,2},{2,3},{3,4},{4,5},{5,6},{6,7},{8,9},{9,10},{10,11},{11... | collective-permute-start | bytes 491528 | tf_op jit(solution)/shard_map/ppermute | solution.py:524
  17.3 1.3 collective-permute-start.3
  19.5 3.8 %collective-permute-done.3.yhi_ref = bf16[5,128,128]{2,1,0:T(8,128)(2,1)S(1)} collective-permute-done((bf16[5,128,128]{2,1,0:T(8,128)(2,1)S(1)}, bf16[5,128,128]{2,1,0:T(8,128)(2,1)S(1)}, u32[]{:S(2)}, u32[]{:S(2)}) %collective-permute-start.3) | collective-permute-done | bytes 163872 | tf_op jit(solution)/shard_map/ppermute | solution.py:524
  23.4 1.7 copy-done.1
  25.1 16.5 %window.1 = (f32[5,16,32,128]{3,2,1,0:T(8,128)}, bf16[1280,128]{1,0:T(8,128)(2,1)S(1)}, bf16[1280,128]{1,0:T(8,128)(2,1)}, bf16[1024,512]{1,0:T(8,128)(2,1)S(1)}) custom-call(s32[5]{0:T(128)S(1)} %convert_element_type.10.edge_ref, f32[5,16,32,128]{3,2,1,0:T(8,128)S(1)} %copy-done, bf16[5,6,32,128]{3,2,1,0:T(8,128)(2,1)S(1)} %collective-permute-done.xlo_ref, ...), custom_call_target="tpu_custom_call" | custom-call | tf_op jit(solution)/shard_map/window/pallas_call | solution.py:599
  41.6 1.0 copy-done.5
  43.3 14.7 %all-to-all-start = ((bf16[128,8,512]{2,1,0:T(8,128)(2,1)}), bf16[128,8,512]{2,1,0:T(8,128)(2,1)S(1)}, u32[]{:S(2)}, u32[]{:S(2)}) async-start(bf16[128,8,512]{2,1,0:T(8,128)(2,1)} %bitcast.28), calls=%async_computation | async-start | bytes 2097152 | tf_op jit(solution)/shard_map/all_to_all | solution.py:632
  58.0 1.3 collective-permute-start.4
  59.3 17.8 %all-to-all-done = bf16[128,8,512]{2,1,0:T(8,128)(2,1)S(1)} async-done(((bf16[128,8,512]{2,1,0:T(8,128)(2,1)}), bf16[128,8,512]{2,1,0:T(8,128)(2,1)S(1)}, u32[]{:S(2)}, u32[]{:S(2)}) %all-to-all-start) | async-done | bytes 1048608 | tf_op jit(solution)/shard_map/all_to_all | solution.py:632
  77.2 1.6 copy-done.2
  78.8 1.6 copy-done.3
  80.3 12.2 %trainer.1 = (bf16[512,512]{1,0:T(8,128)(2,1)S(1)}, bf16[512,2048]{1,0:T(8,128)(2,1)S(1)}, bf16[512,512]{1,0:T(8,128)(2,1)S(1)}, bf16[512,2048]{1,0:T(8,128)(2,1...) custom-call(bf16[1024,512]{1,0:T(8,128)(2,1)S(1)} %bitcast.24, ...), custom_call_target="tpu_custom_call" | custom-call | tf_op jit(solution)/shard_map/trainer/pallas_call | solution.py:636
  92.6 1.3 copy-done.4
  94.7 0.8 copy-done.11
  96.3 4.7 %all-to-all-start.1 = ((bf16[128,8,256]{2,1,0:T(8,128)(2,1)}), bf16[128,8,256]{2,1,0:T(8,128)(2,1)S(1)}, u32[]{:S(2)}, u32[]{:S(2)}) async-start(bf16[128,8,256]{2,1,0:T(8,128)(2,1)} %bitcast.29), calls=%async_computation.1 | async-start | bytes 1048576 | tf_op jit(solution)/shard_map/all_to_all | solution.py:665
  101.0 5.1 %fusion.1 = f32[512,2048]{1,0:T(8,128)} fusion(bf16[512,512]{1,0:T(8,128)(2,1)} %copy-done.11, bf16[512,2048]{1,0:T(8,128)(2,1)} %copy-done.4), kind=kOutput, calls=%fused_computation.1 | convolution fusion | flops 1073741824 | bytes 6815744 | tf_op jit(solution)/shard_map/dot_general | solution.py:528
  106.1 3.3 %fusion.2 = f32[2048,512]{1,0:T(8,128)} fusion(bf16[512,2048]{1,0:T(8,128)(2,1)S(1)} %get-tuple-element.37, bf16[512,512]{1,0:T(8,128)(2,1)S(1)} %copy-done.9), kind=kOutput, calls=%fused_computation.2 | convolution fusion | flops 1073741824 | bytes 6815744 | tf_op jit(solution)/shard_map/dot_general | solution.py:528
  109.4 5.5 %all-to-all-done.1 = bf16[128,8,256]{2,1,0:T(8,128)(2,1)S(1)} async-done(((bf16[128,8,256]{2,1,0:T(8,128)(2,1)}), bf16[128,8,256]{2,1,0:T(8,128)(2,1)S(1)}, u32[]{:S(2)}, u32[]{:S(2)}) %all-to-all-start.1) | async-done | bytes 524320 | tf_op jit(solution)/shard_map/all_to_all | solution.py:665
  115.3 1.1 collective-permute-start.5
  116.4 1.0 collective-permute-done.5.other_grad_ref
  117.4 1.0 copy-done.13
  118.3 1.9 %part.1 = bf16[2560,256]{1,0:T(8,128)(2,1)S(1)} custom-call(bf16[1280,128]{1,0:T(8,128)(2,1)S(1)} %copy-done.13, bf16[1280,128]{1,0:T(8,128)(2,1)} %collective-permute-done.4.got_hbm, bf16[128,512]{1,0:T(8,128)(2,1)S(1)} %gather.1.own_grad_ref, bf16[128,512]{1,0:T(8,128)(2,1)S(1)} %collective-permute-done.5.other_grad_ref), custom_call_target="tpu_custom_call" | custom-call | tf_op jit(solution)/shard_map/part/pallas_call | solution.py:679
  120.3 23.6 %all_to_all.20.parts_ref = bf16[64,40,256]{2,1,0:T(8,128)(2,1)S(1)} all-to-all(bf16[64,40,256]{2,1,0:T(8,128)(2,1)S(1)} %bitcast.21), channel_id=1, replica_groups={{0,1,2,3,4,5,6,7,16,17,18,19,20,21,22,23,32,33,34,35,36,37,38,39,48,49,..., dimensions={0} | all-to-all | bytes 2621440 | tf_op jit(solution)/shard_map/all_to_all | solution.py:692
  144.1 24.3 %all_to_all.21 = bf16[64,40,256]{2,1,0:T(8,128)(2,1)S(1)} all-to-all(bf16[64,40,256]{2,1,0:T(8,128)(2,1)S(1)} %total.1), channel_id=1, replica_groups={{0,1,2,3,4,5,6,7,16,17,18,19,20,21,22,23,32,33,34,35,36,37,38,39,48,49,..., dimensions={0} | all-to-all | bytes 2621440 | tf_op jit(solution)/shard_map/all_to_all | solution.py:703
  168.3 3.4 %collective-permute-start.6 = (bf16[2560,256]{1,0:T(8,128)(2,1)S(1)}, bf16[2560,256]{1,0:T(8,128)(2,1)S(1)}, u32[]{:S(2)}, u32[]{:S(2)}) collective-permute-start(bf16[2560,256]{1,0:T(8,128)(2,1)S(1)} %bitcast.22), channel_id=1, source_target_pairs={{0,8},{8,0},{16,24},{24,16},{32,40},{40,32},{48,56},{56,48},{64,72... | collective-permute-start | bytes 3932168 | tf_op jit(solution)/shard_map/ppermute | solution.py:705
  171.8 2.1 %spread_own.1.rest_0_ = f32[2560,512]{1,0:T(8,128)} custom-call(s32[5]{0:T(128)S(1)} %convert_element_type.10.edge_ref, bf16[2560,256]{1,0:T(8,128)(2,1)S(1)} %bitcast.23), custom_call_target="tpu_custom_call" | custom-call | tf_op jit(solution)/shard_map/spread_own/pallas_call | solution.py:708
  174.4 2.1 %spread_other.1 = f32[2560,512]{1,0:T(8,128)} custom-call(s32[5]{0:T(128)S(1)} %convert_element_type.10.edge_ref, bf16[2560,256]{1,0:T(8,128)(2,1)S(1)} %collective-permute-done.6.half_ref, f32[2560,512]{1,0:T(8,128)} %spread_own.1.rest_0_), custom_call_target="tpu_custom_call", output_to_operand_aliasing={{}: (2, {})} | custom-call | tf_op jit(solution)/shard_map/spread_other/pallas_call | solution.py:708
  (43 shorter events, 4.6 us)
Async XLA Ops:
  0.6 13.2 %copy-start = (f32[5,16,32,128]{3,2,1,0:T(8,128)S(1)}, f32[5,16,32,128]{3,2,1,0:T(8,128)}, u32[]{:S(2)}) copy-start(f32[5,16,32,128]{3,2,1,0:T(8,128)} %f_ref.3) | copy-start | bytes 3932164
  0.6 18.0 %copy-start.17 = (s32[64,1]{0,1:T(1,128)S(1)}, s32[64,1]{0,1:T(1,128)}, u32[]{:S(2)}) copy-start(s32[64,1]{0,1:T(1,128)} %param.10) | copy-start | bytes 772
  0.7 18.4 %copy-start.16 = (s32[2,4,16]{2,1,0:T(4,128)S(1)}, s32[2,4,16]{2,1,0:T(4,128)}, u32[]{:S(2)}) copy-start(s32[2,4,16]{2,1,0:T(4,128)} %param.11) | copy-start | bytes 1540
  2.2 8.8 %collective-permute-start.1 = (bf16[5,6,32,128]{3,2,1,0:T(8,128)(2,1)S(1)}, bf16[5,6,32,128]{3,2,1,0:T(8,128)(2,1)S(1)}, u32[]{:S(2)}, u32[]{:S(2)}) collective-permute-start(bf16[5,6,32,128]{3,2,1,0:T(8,128)(2,1)S(1)} %get-tuple-element.44), channel_id=1, source_target_pairs={{8,0},{16,8},{24,16},{32,24},{40,32},{48,40},{56,48},{64,56},{72,6... | collective-permute-start | bytes 737288 | tf_op jit(solution)/shard_map/ppermute | solution.py:524
  5.6 8.3 %collective-permute-start = (bf16[5,6,32,128]{3,2,1,0:T(8,128)(2,1)S(1)}, bf16[5,6,32,128]{3,2,1,0:T(8,128)(2,1)S(1)}, u32[]{:S(2)}, u32[]{:S(2)}) collective-permute-start(bf16[5,6,32,128]{3,2,1,0:T(8,128)(2,1)S(1)} %get-tuple-element.45), channel_id=1, source_target_pairs={{0,8},{8,16},{16,24},{24,32},{32,40},{40,48},{48,56},{56,64},{64,7... | collective-permute-start | bytes 737288 | tf_op jit(solution)/shard_map/ppermute | solution.py:524
  14.1 5.5 %collective-permute-start.2 = (bf16[5,128,128]{2,1,0:T(8,128)(2,1)S(1)}, bf16[5,128,128]{2,1,0:T(8,128)(2,1)S(1)}, u32[]{:S(2)}, u32[]{:S(2)}) collective-permute-start(bf16[5,128,128]{2,1,0:T(8,128)(2,1)S(1)} %get-tuple-element.25), channel_id=1, source_target_pairs={{0,1},{1,2},{2,3},{3,4},{4,5},{5,6},{6,7},{8,9},{9,10},{10,11},{11... | collective-permute-start | bytes 491528 | tf_op jit(solution)/shard_map/ppermute | solution.py:524
  17.3 6.1 %collective-permute-start.3 = (bf16[5,128,128]{2,1,0:T(8,128)(2,1)S(1)}, bf16[5,128,128]{2,1,0:T(8,128)(2,1)S(1)}, u32[]{:S(2)}, u32[]{:S(2)}) collective-permute-start(bf16[5,128,128]{2,1,0:T(8,128)(2,1)S(1)} %get-tuple-element.26), channel_id=1, source_target_pairs={{1,0},{2,1},{3,2},{4,3},{5,4},{6,5},{7,6},{9,8},{10,9},{11,10},{12... | collective-permute-start | bytes 491528 | tf_op jit(solution)/shard_map/ppermute | solution.py:524
  19.4 22.2 %copy-start.6 = (bf16[1024,128]{1,0:T(8,128)(2,1)}, bf16[1024,128]{1,0:T(8,128)(2,1)S(1)}, u32[]{:S(2)}) copy-start(bf16[1024,128]{1,0:T(8,128)(2,1)S(1)} %get-tuple-element.29.target_pick_ref) | copy-start | bytes 786436
  23.4 1.7 copy-start.1
  41.6 1.0 copy-start.5
  42.6 0.7 copy-start.12
  43.3 33.8 %copy-start.14 = (f32[1,2048]{1,0:T(1,128)S(1)}, f32[1,2048]{1,0:T(1,128)}, u32[]{:S(2)}) copy-start(f32[1,2048]{1,0:T(1,128)} %b_in_ref.1) | copy-start | bytes 24580
  43.3 33.8 %copy-start.15 = (f32[1,512]{1,0:T(1,128)S(1)}, f32[1,512]{1,0:T(1,128)}, u32[]{:S(2)}) copy-start(f32[1,512]{1,0:T(1,128)} %b_out_ref.1) | copy-start | bytes 6148
  43.3 33.8 %all-to-all-start = ((bf16[128,8,512]{2,1,0:T(8,128)(2,1)}), bf16[128,8,512]{2,1,0:T(8,128)(2,1)S(1)}, u32[]{:S(2)}, u32[]{:S(2)}) async-start(bf16[128,8,512]{2,1,0:T(8,128)(2,1)} %bitcast.28), calls=%async_computation | async-start | bytes 2097152 | tf_op jit(solution)/shard_map/all_to_all | solution.py:632
  58.0 58.4 %collective-permute-start.4 = (bf16[1280,128]{1,0:T(8,128)(2,1)}, bf16[1280,128]{1,0:T(8,128)(2,1)}, u32[]{:S(2)}, u32[]{:S(2)}) collective-permute-start(bf16[1280,128]{1,0:T(8,128)(2,1)} %get-tuple-element.32), channel_id=1, source_target_pairs={{0,8},{8,0},{16,24},{24,16},{32,40},{40,32},{48,56},{56,48},{64,72... | collective-permute-start | bytes 983048 | tf_op jit(solution)/shard_map/ppermute | solution.py:631
  77.2 1.6 copy-start.2
  78.8 1.6 copy-start.3
  92.6 1.3 copy-start.4
  93.9 0.8 copy-start.8
  94.7 0.8 copy-start.11
  95.5 0.8 copy-start.10
  96.3 18.7 %all-to-all-start.1 = ((bf16[128,8,256]{2,1,0:T(8,128)(2,1)}), bf16[128,8,256]{2,1,0:T(8,128)(2,1)S(1)}, u32[]{:S(2)}, u32[]{:S(2)}) async-start(bf16[128,8,256]{2,1,0:T(8,128)(2,1)} %bitcast.29), calls=%async_computation.1 | async-start | bytes 1048576 | tf_op jit(solution)/shard_map/all_to_all | solution.py:665
  101.0 5.1 %copy-start.9 = (bf16[512,512]{1,0:T(8,128)(2,1)S(1)}, bf16[512,512]{1,0:T(8,128)(2,1)}, u32[]{:S(2)}) copy-start(bf16[512,512]{1,0:T(8,128)(2,1)} %copy-done.8) | copy-start | bytes 1572868
  106.1 8.8 %copy-start.7 = (bf16[1024,128]{1,0:T(8,128)(2,1)S(1)}, bf16[1024,128]{1,0:T(8,128)(2,1)}, u32[]{:S(2)}) copy-start(bf16[1024,128]{1,0:T(8,128)(2,1)} %copy-done.6) | copy-start | bytes 786436
  115.3 2.1 %collective-permute-start.5 = (bf16[128,512]{1,0:T(8,128)(2,1)S(1)}, bf16[128,512]{1,0:T(8,128)(2,1)S(1)}, u32[]{:S(2)}, u32[]{:S(2)}) collective-permute-start(bf16[128,512]{1,0:T(8,128)(2,1)S(1)} %gather.1.own_grad_ref), channel_id=1, source_target_pairs={{0,8},{8,0},{16,24},{24,16},{32,40},{40,32},{48,56},{56,48},{64,72... | collective-permute-start | bytes 393224 | tf_op jit(solution)/shard_map/ppermute | solution.py:677
  117.4 1.0 copy-start.13
  168.3 6.1 %collective-permute-start.6 = (bf16[2560,256]{1,0:T(8,128)(2,1)S(1)}, bf16[2560,256]{1,0:T(8,128)(2,1)S(1)}, u32[]{:S(2)}, u32[]{:S(2)}) collective-permute-start(bf16[2560,256]{1,0:T(8,128)(2,1)S(1)} %bitcast.22), channel_id=1, source_target_pairs={{0,8},{8,0},{16,24},{24,16},{32,40},{40,32},{48,56},{56,48},{64,72... | collective-permute-start | bytes 3932168 | tf_op jit(solution)/shard_map/ppermute | solution.py:705

commit v5 on v4

--- a/solution.py
+++ b/solution.py
@@ -343,51 +343,22 @@
 def trainer_kernel(
     per,
     got_ref,
-    w_in_hbm,
+    w_in_ref,
     b_in_ref,
-    w_out_hbm,
+    w_out_ref,
     b_out_ref,
-    source_hbm,
-    hidden_hbm,
-    error_hbm,
-    pre_grad_hbm,
-    b_in_grad_ref,
-    b_out_grad_ref,
-    back_hbm,
-    target_ref,
-    slope_ref,
     source_ref,
     hidden_ref,
     error_ref,
     pre_grad_ref,
+    b_in_grad_ref,
+    b_out_grad_ref,
     back_ref,
-    w_in_ref,
-    w_out_ref,
-    loaded,
-    stored,
+    target_ref,
+    slope_ref,
 ):
-    chunk = 512
-    hidden_size = hidden_ref.shape[1]
-    starts = range(0, hidden_size, chunk)
-    loads = []
-    for at, start in enumerate(starts):
-        lanes = slice(start, start + chunk)
-        pair = (
-            pltpu.make_async_copy(w_in_hbm.at[:, lanes], w_in_ref.at[:, lanes], loaded.at[2 * at]),
-            pltpu.make_async_copy(w_out_hbm.at[lanes], w_out_ref.at[lanes], loaded.at[2 * at + 1]),
-        )
-        for load in pair:
-            load.start()
-        loads.append(pair)
-    stores = []
-
-    def store(src, dst):
-        copy = pltpu.make_async_copy(src, dst, stored.at[len(stores)])
-        copy.start()
-        stores.append(copy)
-
     rows = source_ref.shape[0]
-    width = back_hbm.shape[1]
+    width = back_ref.shape[1]
     small, large = 32 * per, 64 * per
     line = lax.broadcasted_iota(jnp.int32, (small, large), 0)
     taken = lax.broadcasted_iota(jnp.int32, (small, large), 1)
@@ -402,19 +373,17 @@
         ).astype(jnp.bfloat16)
         target_ref[lines] = jnp.dot(target_pick, block, preferred_element_type=jnp.float32)
 
-    store(source_ref, source_hbm)
+    chunk = 512
+    hidden_size = hidden_ref.shape[1]
     source = source_ref[...]
     predict = jnp.broadcast_to(b_out_ref[...], target_ref.shape)
-    for at, start in enumerate(starts):
+    for start in range(0, hidden_size, chunk):
         lanes = slice(start, start + chunk)
-        for load in loads[at]:
-            load.wait()
         pre = jnp.dot(source, w_in_ref[:, lanes], preferred_element_type=jnp.float32)
         pre = pre + b_in_ref[:, lanes]
         sigma = jax.nn.sigmoid(pre)
         hidden = (pre * sigma).astype(jnp.bfloat16)
         hidden_ref[:, lanes] = hidden
-        store(hidden_ref.at[:, lanes], hidden_hbm.at[:, lanes])
         slope_ref[:, lanes] = sigma * (1.0 + pre * (1.0 - sigma))
         predict = predict + jnp.dot(
             hidden, w_out_ref[lanes], preferred_element_type=jnp.float32
@@ -423,15 +392,13 @@
     error = jnp.where(wanted < FULL_BELOW, error_weight * (predict - wanted), 0.0)
     error = error.astype(jnp.bfloat16)
     error_ref[...] = error
-    store(error_ref, error_hbm)
     b_out_grad_ref[...] = jnp.sum(error.astype(jnp.float32), axis=0, keepdims=True)
     total = jnp.zeros(target_ref.shape, jnp.float32)
-    for start in starts:
+    for start in range(0, hidden_size, chunk):
         lanes = slice(start, start + chunk)
         upstream = contract_cols(error, w_out_ref[lanes])
         pre_grad = (upstream * slope_ref[:, lanes]).astype(jnp.bfloat16)
         pre_grad_ref[:, lanes] = pre_grad
-        store(pre_grad_ref.at[:, lanes], pre_grad_hbm.at[:, lanes])
         b_in_grad_ref[:, lanes] = jnp.sum(
             pre_grad.astype(jnp.float32), axis=0, keepdims=True
         )
@@ -451,11 +418,7 @@
                 gradient[lines, half * width : (half + 1) * width],
                 preferred_element_type=jnp.float32,
             )
-        lines = slice(at * large, (at + 1) * large)
-        back_ref[lines] = block.astype(jnp.bfloat16)
-        store(back_ref.at[lines], back_hbm.at[lines])
-    for copy in stores:
-        copy.wait()
+        back_ref[at * large : (at + 1) * large] = block.astype(jnp.bfloat16)
 
 
 def gather_kernel(source_pick_ref, target_pick_ref, back_ref, out_ref):
@@ -617,7 +580,7 @@
             pltpu.VMEM((send_rows, EMBED), jnp.bfloat16),
             pltpu.SemaphoreType.DMA((8,)),
         ],
-        compiler_params=grant(32),
+        compiler_params=grant(50),
         name="window",
     )(
         edges, fields, xlo, xhi, ylo, yhi, chosen, source_pick, target_pick, patch_weight
@@ -644,22 +607,13 @@
             shape((1, EMBED), jnp.float32),
             shape((2 * rows, width), jnp.bfloat16),
         ),
-        in_specs=[vmem, hbm, vmem, hbm, vmem],
-        out_specs=(hbm, hbm, hbm, hbm, vmem, vmem, hbm),
+        in_specs=[vmem] * 5,
+        out_specs=(vmem,) * 7,
         scratch_shapes=[
             pltpu.VMEM((rows, EMBED), jnp.float32),
             pltpu.VMEM((rows, hidden_size), jnp.float32),
-            pltpu.VMEM((rows, EMBED), jnp.bfloat16),
-            pltpu.VMEM((rows, hidden_size), jnp.bfloat16),
-            pltpu.VMEM((rows, EMBED), jnp.bfloat16),
-            pltpu.VMEM((rows, hidden_size), jnp.bfloat16),
-            pltpu.VMEM((2 * rows, width), jnp.bfloat16),
-            pltpu.VMEM((EMBED, hidden_size), jnp.bfloat16),
-            pltpu.VMEM((hidden_size, EMBED), jnp.bfloat16),
-            pltpu.SemaphoreType.DMA((8,)),
-            pltpu.SemaphoreType.DMA((16,)),
         ],
-        compiler_params=grant(32),
+        compiler_params=grant(50),
         name="trainer",
     )(got.reshape(send_rows, EMBED), w_in[0], b_in, w_out[0], b_out)
     back = lax.all_to_all(back.reshape(devices, 2 * per, width), axes, 0, 0, tiled=True)
@@ -686,7 +640,7 @@
             pltpu.VMEM((features // 2, patches), jnp.bfloat16),
             pltpu.SemaphoreType.DMA((2,)),
         ],
-        compiler_params=grant(16),
+        compiler_params=grant(24),
         name="part",
     )(keep, got_picked, own_grad, other_grad)
     parts = lax.all_to_all(

time: 177 us -> 163 us (0.921)
  local copies, waits for them, and re-layouts: 11.7 us -> 0.46 us
  Pallas kernels: 36 us -> 32.9 us
    unnamed x36 -> x14, local copies, waits for them, and re-layouts: 11.3 us -> 0.04 us
    pallas_call x1, Pallas kernels: 12.2 us -> 9.09 us  [per_device(): pl.pallas_call(functools.partial(trainer_kernel, per), out_shape=(shape((...]
  transfers between devices with their start and end apart: 9 -> 9, of which waited for: 8 -> 8; matrix products, arithmetic and copies ran while one was open for 5% -> 5% of each run, Pallas kernels for 8% -> 7%
where the time goes in v5:
time: 163 us; the launch traced here: 162 us
  blocking collectives  47.8 us (29%)
  starting transfers between devices  36.6 us (22%)
  waiting for transfers between devices  33.6 us (21%)
  Pallas kernels  32.9 us (20%)
  matrix products  8.36 us (5%)
    all_to_all x1, blocking collectives, per_device(): lax.all_to_all(copies, axes, 0, 0, axis_index_groups=groups, tiled=True)  24.3 us
    all_to_all x1, blocking collectives, per_device(): lax.all_to_all(parts.reshape(members, piece, width), axes, 0, 0, axis_ind...  23.5 us
    all_to_all x1, waiting for transfers between devices, per_device(): lax.all_to_all(send.reshape(devices, 2 * per, EMBED), axes, 0, 0, tiled=T...  17.8 us
    pallas_call x1, Pallas kernels, per_device(): pl.pallas_call(functools.partial(window_kernel, (wide_x, wide_y, wide_z),...  17.3 us
    all_to_all x1, starting transfers between devices, per_device(): lax.all_to_all(send.reshape(devices, 2 * per, EMBED), axes, 0, 0, tiled=T...  14.7 us
    pallas_call x1, Pallas kernels, per_device(): pl.pallas_call(functools.partial(trainer_kernel, per), out_shape=(shape((...  9.09 us
    dot_general x2, matrix products, contract_rows(): lax.dot_general(left, right, (((0,), (0,)), ((), ())), preferred_element_...  8.36 us
    ppermute x2, starting transfers between devices, neighbours(): lax.ppermute(high_piece, axis, up)  6.74 us
  transfers between devices with their start and end apart: 9, of which 8 were waited for; matrix products, arithmetic and copies ran while one was open for 5% of the time, Pallas kernels for 7%

profile of v5, /device:TPU:1, one launch (start us, length us, event | category | flops | bytes accessed | tf_op | source)
XLA Modules:
  0.0 162.3 jit_solution(8223029534749751268)
XLA Ops:
  0.7 1.5 convert.4
  2.2 3.3 %collective-permute-start.1 = (bf16[5,6,32,128]{3,2,1,0:T(8,128)(2,1)S(1)}, bf16[5,6,32,128]{3,2,1,0:T(8,128)(2,1)S(1)}, u32[]{:S(2)}, u32[]{:S(2)}) collective-permute-start(bf16[5,6,32,128]{3,2,1,0:T(8,128)(2,1)S(1)} %get-tuple-element.44), channel_id=1, source_target_pairs={{8,0},{16,8},{24,16},{32,24},{40,32},{48,40},{56,48},{64,56},{72,6... | collective-permute-start | bytes 737288 | tf_op jit(solution)/shard_map/ppermute | solution.py:487
  5.6 3.5 %collective-permute-start = (bf16[5,6,32,128]{3,2,1,0:T(8,128)(2,1)S(1)}, bf16[5,6,32,128]{3,2,1,0:T(8,128)(2,1)S(1)}, u32[]{:S(2)}, u32[]{:S(2)}) collective-permute-start(bf16[5,6,32,128]{3,2,1,0:T(8,128)(2,1)S(1)} %get-tuple-element.45), channel_id=1, source_target_pairs={{0,8},{8,16},{16,24},{24,32},{32,40},{40,48},{48,56},{56,64},{64,7... | collective-permute-start | bytes 737288 | tf_op jit(solution)/shard_map/ppermute | solution.py:487
  9.1 1.9 %collective-permute-done.1.xhi_ref = bf16[5,6,32,128]{3,2,1,0:T(8,128)(2,1)S(1)} collective-permute-done((bf16[5,6,32,128]{3,2,1,0:T(8,128)(2,1)S(1)}, bf16[5,6,32,128]{3,2,1,0:T(8,128)(2,1)S(1)}, u32[]{:S(2)}, u32[]{:S(2)}) %collective-permute-start.1) | collective-permute-done | bytes 245792 | tf_op jit(solution)/shard_map/ppermute | solution.py:487
  11.1 2.8 %collective-permute-done.xlo_ref = bf16[5,6,32,128]{3,2,1,0:T(8,128)(2,1)S(1)} collective-permute-done((bf16[5,6,32,128]{3,2,1,0:T(8,128)(2,1)S(1)}, bf16[5,6,32,128]{3,2,1,0:T(8,128)(2,1)S(1)}, u32[]{:S(2)}, u32[]{:S(2)}) %collective-permute-start) | collective-permute-done | bytes 245792 | tf_op jit(solution)/shard_map/ppermute | solution.py:487
  13.9 0.2 strips.1
  14.1 3.2 %collective-permute-start.2 = (bf16[5,128,128]{2,1,0:T(8,128)(2,1)S(1)}, bf16[5,128,128]{2,1,0:T(8,128)(2,1)S(1)}, u32[]{:S(2)}, u32[]{:S(2)}) collective-permute-start(bf16[5,128,128]{2,1,0:T(8,128)(2,1)S(1)} %get-tuple-element.25), channel_id=1, source_target_pairs={{0,1},{1,2},{2,3},{3,4},{4,5},{5,6},{6,7},{8,9},{9,10},{10,11},{11... | collective-permute-start | bytes 491528 | tf_op jit(solution)/shard_map/ppermute | solution.py:487
  17.3 1.3 collective-permute-start.3
  18.7 0.1 broadcast_in_dim_reshape.6.own_row_ref
  19.0 0.4 slots.1
  19.4 0.1 collective-permute-done.2.ylo_ref
  19.5 3.8 %collective-permute-done.3.yhi_ref = bf16[5,128,128]{2,1,0:T(8,128)(2,1)S(1)} collective-permute-done((bf16[5,128,128]{2,1,0:T(8,128)(2,1)S(1)}, bf16[5,128,128]{2,1,0:T(8,128)(2,1)S(1)}, u32[]{:S(2)}, u32[]{:S(2)}) %collective-permute-start.3) | collective-permute-done | bytes 163872 | tf_op jit(solution)/shard_map/ppermute | solution.py:487
  23.4 17.3 %window.1 = (f32[5,16,32,128]{3,2,1,0:T(8,128)}, bf16[1280,128]{1,0:T(8,128)(2,1)S(1)}, bf16[1280,128]{1,0:T(8,128)(2,1)S(1)}, bf16[1024,512]{1,0:T(8,128)(2,1)}) custom-call(s32[5]{0:T(128)S(1)} %convert_element_type.10.edge_ref, f32[5,16,32,128]{3,2,1,0:T(8,128)} %f_ref.3, bf16[5,6,32,128]{3,2,1,0:T(8,128)(2,1)S(1)} %collective-permute-done.xlo_ref, ...), custom_call_target="tpu_custom_call" | custom-call | tf_op jit(solution)/shard_map/window/pallas_call | solution.py:562
  40.7 14.7 %all-to-all-start = ((bf16[128,8,512]{2,1,0:T(8,128)(2,1)}), bf16[128,8,512]{2,1,0:T(8,128)(2,1)S(1)}, u32[]{:S(2)}, u32[]{:S(2)}) async-start(bf16[128,8,512]{2,1,0:T(8,128)(2,1)} %bitcast.7), calls=%async_computation | async-start | bytes 2097152 | tf_op jit(solution)/shard_map/all_to_all | solution.py:595
  55.5 1.3 collective-permute-start.4
  56.8 17.8 %all-to-all-done = bf16[128,8,512]{2,1,0:T(8,128)(2,1)S(1)} async-done(((bf16[128,8,512]{2,1,0:T(8,128)(2,1)}), bf16[128,8,512]{2,1,0:T(8,128)(2,1)S(1)}, u32[]{:S(2)}, u32[]{:S(2)}) %all-to-all-start) | async-done | bytes 1048608 | tf_op jit(solution)/shard_map/all_to_all | solution.py:595
  74.6 9.1 %trainer.1 = (bf16[512,512]{1,0:T(8,128)(2,1)S(1)}, bf16[512,2048]{1,0:T(8,128)(2,1)}, bf16[512,512]{1,0:T(8,128)(2,1)S(1)}, bf16[512,2048]{1,0:T(8,128)(2,1)}, ...) custom-call(bf16[1024,512]{1,0:T(8,128)(2,1)S(1)} %bitcast.24, bf16[512,2048]{1,0:T(8,128)(2,1)} %bitcast.29, ...), custom_call_target="tpu_custom_call" | custom-call | tf_op jit(solution)/shard_map/trainer/pallas_call | solution.py:599
  83.7 4.7 %all-to-all-start.1 = ((bf16[128,8,256]{2,1,0:T(8,128)(2,1)}), bf16[128,8,256]{2,1,0:T(8,128)(2,1)S(1)}, u32[]{:S(2)}, u32[]{:S(2)}) async-start(bf16[128,8,256]{2,1,0:T(8,128)(2,1)} %bitcast.11), calls=%async_computation.1 | async-start | bytes 1048576 | tf_op jit(solution)/shard_map/all_to_all | solution.py:619
  88.4 5.0 %fusion.1 = f32[512,2048]{1,0:T(8,128)} fusion(bf16[512,512]{1,0:T(8,128)(2,1)S(1)} %get-tuple-element.35, bf16[512,2048]{1,0:T(8,128)(2,1)} %get-tuple-element.36), kind=kOutput, calls=%fused_computation.1 | convolution fusion | flops 1073741824 | bytes 6815744 | tf_op jit(solution)/shard_map/dot_general | solution.py:491
  93.4 3.3 %fusion.2 = f32[2048,512]{1,0:T(8,128)} fusion(bf16[512,2048]{1,0:T(8,128)(2,1)S(1)} %copy-done.4, bf16[512,512]{1,0:T(8,128)(2,1)S(1)} %get-tuple-element.38), kind=kOutput, calls=%fused_computation.2 | convolution fusion | flops 1073741824 | bytes 6815744 | tf_op jit(solution)/shard_map/dot_general | solution.py:491
  96.8 5.6 %all-to-all-done.1 = bf16[128,8,256]{2,1,0:T(8,128)(2,1)S(1)} async-done(((bf16[128,8,256]{2,1,0:T(8,128)(2,1)}), bf16[128,8,256]{2,1,0:T(8,128)(2,1)S(1)}, u32[]{:S(2)}, u32[]{:S(2)}) %all-to-all-start.1) | async-done | bytes 524320 | tf_op jit(solution)/shard_map/all_to_all | solution.py:619
  102.3 0.3 gather.1.own_grad_ref
  102.7 1.1 collective-permute-start.5
  103.8 1.0 collective-permute-done.5.other_grad_ref
  104.8 1.1 part.1
  105.9 23.5 %all_to_all.20.parts_ref = bf16[64,40,256]{2,1,0:T(8,128)(2,1)S(1)} all-to-all(bf16[64,40,256]{2,1,0:T(8,128)(2,1)S(1)} %bitcast.21), channel_id=1, replica_groups={{0,1,2,3,4,5,6,7,16,17,18,19,20,21,22,23,32,33,34,35,36,37,38,39,48,49,..., dimensions={0} | all-to-all | bytes 2621440 | tf_op jit(solution)/shard_map/all_to_all | solution.py:646
  129.4 0.2 total.1
  129.7 24.3 %all_to_all.21 = bf16[64,40,256]{2,1,0:T(8,128)(2,1)S(1)} all-to-all(bf16[64,40,256]{2,1,0:T(8,128)(2,1)S(1)} %total.1), channel_id=1, replica_groups={{0,1,2,3,4,5,6,7,16,17,18,19,20,21,22,23,32,33,34,35,36,37,38,39,48,49,..., dimensions={0} | all-to-all | bytes 2621440 | tf_op jit(solution)/shard_map/all_to_all | solution.py:657
  153.9 3.4 %collective-permute-start.6 = (bf16[2560,256]{1,0:T(8,128)(2,1)S(1)}, bf16[2560,256]{1,0:T(8,128)(2,1)S(1)}, u32[]{:S(2)}, u32[]{:S(2)}) collective-permute-start(bf16[2560,256]{1,0:T(8,128)(2,1)S(1)} %bitcast.22), channel_id=1, source_target_pairs={{0,8},{8,0},{16,24},{24,16},{32,40},{40,32},{48,56},{56,48},{64,72... | collective-permute-start | bytes 3932168 | tf_op jit(solution)/shard_map/ppermute | solution.py:659
  157.4 2.1 %spread_own.1.rest_0_ = f32[2560,512]{1,0:T(8,128)} custom-call(s32[5]{0:T(128)S(1)} %convert_element_type.10.edge_ref, bf16[2560,256]{1,0:T(8,128)(2,1)S(1)} %bitcast.23), custom_call_target="tpu_custom_call" | custom-call | tf_op jit(solution)/shard_map/spread_own/pallas_call | solution.py:662
  159.5 0.6 collective-permute-done.6.half_ref
  160.0 2.1 %spread_other.1 = f32[2560,512]{1,0:T(8,128)} custom-call(s32[5]{0:T(128)S(1)} %convert_element_type.10.edge_ref, bf16[2560,256]{1,0:T(8,128)(2,1)S(1)} %collective-permute-done.6.half_ref, f32[2560,512]{1,0:T(8,128)} %spread_own.1.rest_0_), custom_call_target="tpu_custom_call", output_to_operand_aliasing={{}: (2, {})} | custom-call | tf_op jit(solution)/shard_map/spread_other/pallas_call | solution.py:662
  (21 shorter events, 0.3 us)
Async XLA Ops:
  0.6 13.2 %copy-start = (f32[5,16,32,128]{3,2,1,0:T(8,128)S(1)}, f32[5,16,32,128]{3,2,1,0:T(8,128)}, u32[]{:S(2)}) copy-start(f32[5,16,32,128]{3,2,1,0:T(8,128)} %f_ref.3) | copy-start | bytes 3932164
  0.6 18.0 %copy-start.6 = (s32[64,1]{0,1:T(1,128)S(1)}, s32[64,1]{0,1:T(1,128)}, u32[]{:S(2)}) copy-start(s32[64,1]{0,1:T(1,128)} %param.10) | copy-start | bytes 772
  0.7 18.4 %copy-start.5 = (s32[2,4,16]{2,1,0:T(4,128)S(1)}, s32[2,4,16]{2,1,0:T(4,128)}, u32[]{:S(2)}) copy-start(s32[2,4,16]{2,1,0:T(4,128)} %param.11) | copy-start | bytes 1540
  2.2 8.8 %collective-permute-start.1 = (bf16[5,6,32,128]{3,2,1,0:T(8,128)(2,1)S(1)}, bf16[5,6,32,128]{3,2,1,0:T(8,128)(2,1)S(1)}, u32[]{:S(2)}, u32[]{:S(2)}) collective-permute-start(bf16[5,6,32,128]{3,2,1,0:T(8,128)(2,1)S(1)} %get-tuple-element.44), channel_id=1, source_target_pairs={{8,0},{16,8},{24,16},{32,24},{40,32},{48,40},{56,48},{64,56},{72,6... | collective-permute-start | bytes 737288 | tf_op jit(solution)/shard_map/ppermute | solution.py:487
  5.6 8.3 %collective-permute-start = (bf16[5,6,32,128]{3,2,1,0:T(8,128)(2,1)S(1)}, bf16[5,6,32,128]{3,2,1,0:T(8,128)(2,1)S(1)}, u32[]{:S(2)}, u32[]{:S(2)}) collective-permute-start(bf16[5,6,32,128]{3,2,1,0:T(8,128)(2,1)S(1)} %get-tuple-element.45), channel_id=1, source_target_pairs={{0,8},{8,16},{16,24},{24,32},{32,40},{40,48},{48,56},{56,64},{64,7... | collective-permute-start | bytes 737288 | tf_op jit(solution)/shard_map/ppermute | solution.py:487
  14.1 5.5 %collective-permute-start.2 = (bf16[5,128,128]{2,1,0:T(8,128)(2,1)S(1)}, bf16[5,128,128]{2,1,0:T(8,128)(2,1)S(1)}, u32[]{:S(2)}, u32[]{:S(2)}) collective-permute-start(bf16[5,128,128]{2,1,0:T(8,128)(2,1)S(1)} %get-tuple-element.25), channel_id=1, source_target_pairs={{0,1},{1,2},{2,3},{3,4},{4,5},{5,6},{6,7},{8,9},{9,10},{10,11},{11... | collective-permute-start | bytes 491528 | tf_op jit(solution)/shard_map/ppermute | solution.py:487
  17.3 6.1 %collective-permute-start.3 = (bf16[5,128,128]{2,1,0:T(8,128)(2,1)S(1)}, bf16[5,128,128]{2,1,0:T(8,128)(2,1)S(1)}, u32[]{:S(2)}, u32[]{:S(2)}) collective-permute-start(bf16[5,128,128]{2,1,0:T(8,128)(2,1)S(1)} %get-tuple-element.26), channel_id=1, source_target_pairs={{1,0},{2,1},{3,2},{4,3},{5,4},{6,5},{7,6},{9,8},{10,9},{11,10},{12... | collective-permute-start | bytes 491528 | tf_op jit(solution)/shard_map/ppermute | solution.py:487
  40.7 14.7 %copy-start.3 = (bf16[1280,128]{1,0:T(8,128)(2,1)}, bf16[1280,128]{1,0:T(8,128)(2,1)S(1)}, u32[]{:S(2)}) copy-start(bf16[1280,128]{1,0:T(8,128)(2,1)S(1)} %get-tuple-element.32) | copy-start | bytes 983044
  40.7 33.9 %copy-start.1 = (f32[1,2048]{1,0:T(1,128)S(1)}, f32[1,2048]{1,0:T(1,128)}, u32[]{:S(2)}) copy-start(f32[1,2048]{1,0:T(1,128)} %b_in_ref.1) | copy-start | bytes 24580
  40.7 33.9 %copy-start.2 = (f32[1,512]{1,0:T(1,128)S(1)}, f32[1,512]{1,0:T(1,128)}, u32[]{:S(2)}) copy-start(f32[1,512]{1,0:T(1,128)} %b_out_ref.1) | copy-start | bytes 6148
  40.7 33.8 %all-to-all-start = ((bf16[128,8,512]{2,1,0:T(8,128)(2,1)}), bf16[128,8,512]{2,1,0:T(8,128)(2,1)S(1)}, u32[]{:S(2)}, u32[]{:S(2)}) async-start(bf16[128,8,512]{2,1,0:T(8,128)(2,1)} %bitcast.7), calls=%async_computation | async-start | bytes 2097152 | tf_op jit(solution)/shard_map/all_to_all | solution.py:595
  55.5 48.3 %collective-permute-start.4 = (bf16[1280,128]{1,0:T(8,128)(2,1)}, bf16[1280,128]{1,0:T(8,128)(2,1)S(1)}, u32[]{:S(2)}, u32[]{:S(2)}) collective-permute-start(bf16[1280,128]{1,0:T(8,128)(2,1)} %copy-done.3), channel_id=1, source_target_pairs={{0,8},{8,0},{16,24},{24,16},{32,40},{40,32},{48,56},{56,48},{64,72... | collective-permute-start | bytes 983048 | tf_op jit(solution)/shard_map/ppermute | solution.py:594
  83.7 18.7 %all-to-all-start.1 = ((bf16[128,8,256]{2,1,0:T(8,128)(2,1)}), bf16[128,8,256]{2,1,0:T(8,128)(2,1)S(1)}, u32[]{:S(2)}, u32[]{:S(2)}) async-start(bf16[128,8,256]{2,1,0:T(8,128)(2,1)} %bitcast.11), calls=%async_computation.1 | async-start | bytes 1048576 | tf_op jit(solution)/shard_map/all_to_all | solution.py:619
  88.4 5.0 %copy-start.4 = (bf16[512,2048]{1,0:T(8,128)(2,1)S(1)}, bf16[512,2048]{1,0:T(8,128)(2,1)}, u32[]{:S(2)}) copy-start(bf16[512,2048]{1,0:T(8,128)(2,1)} %get-tuple-element.37) | copy-start | bytes 6291460
  102.7 2.1 %collective-permute-start.5 = (bf16[128,512]{1,0:T(8,128)(2,1)S(1)}, bf16[128,512]{1,0:T(8,128)(2,1)S(1)}, u32[]{:S(2)}, u32[]{:S(2)}) collective-permute-start(bf16[128,512]{1,0:T(8,128)(2,1)S(1)} %gather.1.own_grad_ref), channel_id=1, source_target_pairs={{0,8},{8,0},{16,24},{24,16},{32,40},{40,32},{48,56},{56,48},{64,72... | collective-permute-start | bytes 393224 | tf_op jit(solution)/shard_map/ppermute | solution.py:631
  153.9 6.1 %collective-permute-start.6 = (bf16[2560,256]{1,0:T(8,128)(2,1)S(1)}, bf16[2560,256]{1,0:T(8,128)(2,1)S(1)}, u32[]{:S(2)}, u32[]{:S(2)}) collective-permute-start(bf16[2560,256]{1,0:T(8,128)(2,1)S(1)} %bitcast.22), channel_id=1, source_target_pairs={{0,8},{8,0},{16,24},{24,16},{32,40},{40,32},{48,56},{56,48},{64,72... | collective-permute-start | bytes 3932168 | tf_op jit(solution)/shard_map/ppermute | solution.py:659

commit v6 on v5

--- a/solution.py
+++ b/solution.py
@@ -115,38 +115,39 @@
     )
 
 
-def strip_layers(wide_x):
-    layers, place = [], 0
-    for layer in range(REACH):
-        beside = REACH - LIFT // 4 if layer < 4 else 0
-        rows = wide_x + 2 * beside
-        layers.append((layer, beside, rows, place))
-        place += rows
-    return layers, place
-
-
-def strips_kernel(f_ref, xlo_ref, xhi_ref, first_ref, last_ref, lines_ref):
+CORNER = 4
+
+
+def faces_kernel(f_ref, x_first_ref, x_last_ref, y_first_ref, y_last_ref, lines_ref):
     wide_x, wide_y = f_ref.shape[1], f_ref.shape[2]
-    layers, _ = strip_layers(wide_x)
-    beside = layers[0][1]
+    x_first_ref[...] = f_ref[:, :REACH].astype(jnp.bfloat16)
+    x_last_ref[...] = f_ref[:, wide_x - REACH :].astype(jnp.bfloat16)
+    for at, out_ref in ((0, y_first_ref), (wide_y - LIFT, y_last_ref)):
+        for field in range(FIELDS):
+            for row in range(wide_x):
+                lines_ref[row * LIFT : (row + 1) * LIFT] = f_ref[field, row, at : at + LIFT]
+            for layer in range(REACH):
+                line = layer if at == 0 else LIFT - 1 - layer
+                out_ref[field, layer * wide_x : (layer + 1) * wide_x] = lines_ref[
+                    pl.ds(line, wide_x, stride=LIFT), :
+                ].astype(jnp.bfloat16)
+
+
+def corners_kernel(xlo_ref, xhi_ref, first_ref, last_ref, lines_ref):
+    wide_y = xlo_ref.shape[2]
     for at, out_ref in ((0, first_ref), (wide_y - LIFT, last_ref)):
-        tile = slice(at, at + LIFT)
-        for row in range(wide_x + 2 * beside):
-            place = slice(row * LIFT, (row + 1) * LIFT)
-            if row < beside:
-                piece = xlo_ref[:, REACH - beside + row, tile].astype(jnp.float32)
-            elif row < beside + wide_x:
-                piece = f_ref[:, row - beside, tile]
-            else:
-                piece = xhi_ref[:, row - beside - wide_x, tile].astype(jnp.float32)
-            lines_ref[:, place] = piece
         for field in range(FIELDS):
-            for layer, near, rows, place in layers:
+            for row in range(CORNER):
+                for begin, ref, base in ((0, xlo_ref, REACH - CORNER), (CORNER, xhi_ref, 0)):
+                    place = (begin + row) * LIFT
+                    lines_ref[place : place + LIFT] = ref[
+                        field, base + row, at : at + LIFT
+                    ].astype(jnp.float32)
+            picked = []
+            for layer in range(CORNER):
                 line = layer if at == 0 else LIFT - 1 - layer
-                start = (beside - near) * LIFT + line
-                out_ref[field, place : place + rows] = lines_ref[
-                    field, pl.ds(start, rows, stride=LIFT), :
-                ].astype(jnp.bfloat16)
+                picked.append(lines_ref[pl.ds(line, 2 * CORNER, stride=LIFT), :])
+            out_ref[field] = jnp.concatenate(picked, axis=0).astype(jnp.bfloat16)
 
 
 def window_kernel(
@@ -158,6 +159,8 @@
     xhi_ref,
     ylo_ref,
     yhi_ref,
+    corner_lo_ref,
+    corner_hi_ref,
     chosen_ref,
     source_pick_ref,
     target_pick_ref,
@@ -191,15 +194,24 @@
     first_ref[:, 0:REACH, LIFT:top_y, :] = xlo_ref[...].astype(jnp.float32)
     first_ref[:, top_x:full_x, LIFT:top_y, :] = xhi_ref[...].astype(jnp.float32)
     for field in range(FIELDS):
-        for layer, beside, lines, place in strip_layers(wide_x)[0]:
-            rows = slice(REACH - beside, REACH - beside + lines)
-            packed = slice(place, place + lines)
-            first_ref[field, rows, LIFT - 1 - layer, :] = ylo_ref[field, packed].astype(
-                jnp.float32
-            )
-            first_ref[field, rows, top_y + layer, :] = yhi_ref[field, packed].astype(
-                jnp.float32
-            )
+        for low, face_ref, corner_ref in (
+            (True, ylo_ref, corner_lo_ref),
+            (False, yhi_ref, corner_hi_ref),
+        ):
+            face = face_ref[field].astype(jnp.float32)
+            corner = corner_ref[field].astype(jnp.float32)
+            for layer in range(REACH):
+                line = LIFT - 1 - layer if low else top_y + layer
+                first_ref[field, REACH:top_x, line, :] = face[
+                    layer * wide_x : (layer + 1) * wide_x
+                ]
+                if layer >= CORNER:
+                    continue
+                at = layer * 2 * CORNER
+                first_ref[field, REACH - CORNER : REACH, line, :] = corner[at : at + CORNER]
+                first_ref[field, top_x : top_x + CORNER, line, :] = corner[
+                    at + CORNER : at + 2 * CORNER
+                ]
 
     def clear(ref, least):
         @pl.when(edge_ref[0] == 1)
@@ -510,10 +522,6 @@
     per = slots * BLOCK_ROWS
     features = FIELDS * PATCH**3
 
-    def narrow(piece):
-        return piece.astype(jnp.bfloat16)
-
-    xlo, xhi = neighbours(narrow(fields[:, :REACH]), narrow(fields[:, wide_x - REACH :]), "gx")
     at_x, at_y = lax.axis_index("gx"), lax.axis_index("gy")
     core = at_x % 2
     edges = jnp.stack(
@@ -532,17 +540,29 @@
     def shape(dims, kind):
         return jax.ShapeDtypeStruct(dims, kind)
 
-    layers, strip = strip_layers(wide_x)
-    y_first, y_last = pl.pallas_call(
-        strips_kernel,
-        out_shape=(shape((FIELDS, strip, wide_z), jnp.bfloat16),) * 2,
-        in_specs=[vmem] * 3,
+    face = shape((FIELDS, REACH, wide_y, wide_z), jnp.bfloat16)
+    side = shape((FIELDS, REACH * wide_x, wide_z), jnp.bfloat16)
+    x_first, x_last, y_first, y_last = pl.pallas_call(
+        faces_kernel,
+        out_shape=(face, face, side, side),
+        in_specs=[vmem],
+        out_specs=(vmem,) * 4,
+        scratch_shapes=[pltpu.VMEM((wide_x * LIFT, wide_z), jnp.float32)],
+        compiler_params=grant(8),
+        name="faces",
+    )(fields)
+    xlo, xhi = neighbours(x_first, x_last, "gx")
+    ylo, yhi = neighbours(y_first, y_last, "gy")
+    corner_first, corner_last = pl.pallas_call(
+        corners_kernel,
+        out_shape=(shape((FIELDS, 2 * CORNER * CORNER, wide_z), jnp.bfloat16),) * 2,
+        in_specs=[vmem] * 2,
         out_specs=(vmem,) * 2,
-        scratch_shapes=[pltpu.VMEM((FIELDS, layers[0][2] * LIFT, wide_z), jnp.float32)],
+        scratch_shapes=[pltpu.VMEM((2 * CORNER * LIFT, wide_z), jnp.float32)],
         compiler_params=grant(8),
-        name="strips",
-    )(fields, xlo, xhi)
-    ylo, yhi = neighbours(y_first, y_last, "gy")
+        name="corners",
+    )(xlo, xhi)
+    corner_lo, corner_hi = neighbours(corner_first, corner_last, "gy")
 
     send_rows = 2 * devices * per
     source_pick, target_pick, chosen = pl.pallas_call(
@@ -567,7 +587,7 @@
             shape((features // 2, patches), jnp.bfloat16),
             shape((send_rows, EMBED), jnp.bfloat16),
         ),
-        in_specs=[smem] + [vmem] * 8 + [hbm],
+        in_specs=[smem] + [vmem] * 10 + [hbm],
         out_specs=(hbm,) * 4,
         scratch_shapes=[
             pltpu.VMEM(full, jnp.float32),
@@ -583,7 +603,18 @@
         compiler_params=grant(50),
         name="window",
     )(
-        edges, fields, xlo, xhi, ylo, yhi, chosen, source_pick, target_pick, patch_weight
+        edges,
+        fields,
+        xlo,
+        xhi,
+        ylo,
+        yhi,
+        corner_lo,
+        corner_hi,
+        chosen,
+        source_pick,
+        target_pick,
+        patch_weight,
     )
 
     pairs = [(i, i ^ 1) for i in range(n_x)]

time: 163 us -> 166 us (1.018)
  starting transfers between devices: 36.6 us -> 44.7 us
  waiting for transfers between devices: 33.6 us -> 27.3 us
  local copies, waits for them, and re-layouts: 0.46 us -> 2.38 us
    ppermute x2 -> x3, starting transfers between devices: 6.74 us -> 11.3 us  [neighbours(): lax.ppermute(high_piece, axis, up)]
    all_to_all x1, starting transfers between devices: 14.7 us -> 18.3 us  [per_device(): lax.all_to_all(send.reshape(devices, 2 * per, EMBED), axes, 0, 0, tiled=T...]
    ppermute x2 -> x3, waiting for transfers between devices: 5.76 us -> 2.35 us  [neighbours(): lax.ppermute(low_piece, axis, down)]
    ppermute x2 -> x3, waiting for transfers between devices: 2.93 us -> 0.01 us  [neighbours(): lax.ppermute(high_piece, axis, up)]
    ppermute x2 -> x3, starting transfers between devices: 4.62 us -> 4.5 us  [neighbours(): lax.ppermute(low_piece, axis, down)]
  transfers between devices with their start and end apart: 9 -> 11, of which waited for: 8 -> 6; matrix products, arithmetic and copies ran while one was open for 5% -> 6% of each run, Pallas kernels for 7% -> 7%
where the time goes in v6:
time: 166 us; the launch traced here: 165 us
  blocking collectives  47.8 us (29%)
  starting transfers between devices  44.7 us (27%)
  Pallas kernels  32.9 us (20%)
  waiting for transfers between devices  27.3 us (16%)
  matrix products  8.36 us (5%)
  local copies, waits for them, and re-layouts  2.38 us (1%)
    all_to_all x1, blocking collectives, per_device(): lax.all_to_all(copies, axes, 0, 0, axis_index_groups=groups, tiled=True)  24.3 us
    all_to_all x1, blocking collectives, per_device(): lax.all_to_all(parts.reshape(members, piece, width), axes, 0, 0, axis_ind...  23.6 us
    all_to_all x1, starting transfers between devices, per_device(): lax.all_to_all(send.reshape(devices, 2 * per, EMBED), axes, 0, 0, tiled=T...  18.3 us
    all_to_all x1, waiting for transfers between devices, per_device(): lax.all_to_all(send.reshape(devices, 2 * per, EMBED), axes, 0, 0, tiled=T...  17.8 us
    pallas_call x1, Pallas kernels, per_device(): pl.pallas_call(functools.partial(window_kernel, (wide_x, wide_y, wide_z),...  17.3 us
    ppermute x3, starting transfers between devices, neighbours(): lax.ppermute(high_piece, axis, up)  11.3 us
    pallas_call x1, Pallas kernels, per_device(): pl.pallas_call(functools.partial(trainer_kernel, per), out_shape=(shape((...  9.08 us
    dot_general x2, matrix products, contract_rows(): lax.dot_general(left, right, (((0,), (0,)), ((), ())), preferred_element_...  8.36 us
  transfers between devices with their start and end apart: 11, of which 6 were waited for; matrix products, arithmetic and copies ran while one was open for 6% of the time, Pallas kernels for 7%

profile of v6, /device:TPU:1, one launch (start us, length us, event | category | flops | bytes accessed | tf_op | source)
XLA Modules:
  0.0 165.1 jit_solution(11195911535533222471)
XLA Ops:
  0.6 1.3 copy-done
  2.2 4.9 %collective-permute-start = (bf16[5,6,32,128]{3,2,1,0:T(8,128)(2,1)S(1)}, bf16[5,6,32,128]{3,2,1,0:T(8,128)(2,1)S(1)}, u32[]{:S(2)}, u32[]{:S(2)}) collective-permute-start(bf16[5,6,32,128]{3,2,1,0:T(8,128)(2,1)S(1)} %get-tuple-element.29), channel_id=1, source_target_pairs={{0,8},{8,16},{16,24},{24,32},{32,40},{40,48},{48,56},{56,64},{64,7... | collective-permute-start | bytes 737288 | tf_op jit(solution)/shard_map/ppermute | solution.py:499
  7.1 1.9 %collective-permute-start.1 = (bf16[5,6,32,128]{3,2,1,0:T(8,128)(2,1)S(1)}, bf16[5,6,32,128]{3,2,1,0:T(8,128)(2,1)S(1)}, u32[]{:S(2)}, u32[]{:S(2)}) collective-permute-start(bf16[5,6,32,128]{3,2,1,0:T(8,128)(2,1)S(1)} %get-tuple-element.30), channel_id=1, source_target_pairs={{8,0},{16,8},{24,16},{32,24},{40,32},{48,40},{56,48},{64,56},{72,6... | collective-permute-start | bytes 737288 | tf_op jit(solution)/shard_map/ppermute | solution.py:499
  9.0 3.2 %collective-permute-start.2 = (bf16[5,96,128]{2,1,0:T(8,128)(2,1)S(1)}, bf16[5,96,128]{2,1,0:T(8,128)(2,1)S(1)}, u32[]{:S(2)}, u32[]{:S(2)}) collective-permute-start(bf16[5,96,128]{2,1,0:T(8,128)(2,1)S(1)} %get-tuple-element.31), channel_id=1, source_target_pairs={{0,1},{1,2},{2,3},{3,4},{4,5},{5,6},{6,7},{8,9},{9,10},{10,11},{11... | collective-permute-start | bytes 368648 | tf_op jit(solution)/shard_map/ppermute | solution.py:499
  12.2 1.3 collective-permute-start.3
  13.6 1.1 collective-permute-done.1.xhi_ref
  14.7 3.2 %collective-permute-start.4 = (bf16[5,32,128]{2,1,0:T(8,128)(2,1)S(1)}, bf16[5,32,128]{2,1,0:T(8,128)(2,1)S(1)}, u32[]{:S(2)}, u32[]{:S(2)}) collective-permute-start(bf16[5,32,128]{2,1,0:T(8,128)(2,1)S(1)} %get-tuple-element.33), channel_id=1, source_target_pairs={{0,1},{1,2},{2,3},{3,4},{4,5},{5,6},{6,7},{8,9},{9,10},{10,11},{11... | collective-permute-start | bytes 122888 | tf_op jit(solution)/shard_map/ppermute | solution.py:499
  17.9 1.3 collective-permute-start.5
  19.2 0.7 broadcast_in_dim.9
  20.3 0.7 convert_element_type.9
  21.0 0.4 slots.1
  21.4 1.3 collective-permute-done.5.corner_hi_ref
  22.7 17.3 %window.1 = (f32[5,16,32,128]{3,2,1,0:T(8,128)}, bf16[1280,128]{1,0:T(8,128)(2,1)S(1)}, bf16[1280,128]{1,0:T(8,128)(2,1)}, bf16[1024,512]{1,0:T(8,128)(2,1)}) custom-call(s32[5]{0:T(128)S(1)} %convert_element_type.8.edge_ref, f32[5,16,32,128]{3,2,1,0:T(8,128)} %f_ref.3, bf16[5,6,32,128]{3,2,1,0:T(8,128)(2,1)S(1)} %collective-permute-done.xlo_ref, ...), custom_call_target="tpu_custom_call" | custom-call | tf_op jit(solution)/shard_map/window/pallas_call | solution.py:582
  40.0 18.3 %all-to-all-start = ((bf16[128,8,512]{2,1,0:T(8,128)(2,1)}), bf16[128,8,512]{2,1,0:T(8,128)(2,1)S(1)}, u32[]{:S(2)}, u32[]{:S(2)}) async-start(bf16[128,8,512]{2,1,0:T(8,128)(2,1)} %bitcast.7), calls=%async_computation | async-start | bytes 2097152 | tf_op jit(solution)/shard_map/all_to_all | solution.py:626
  58.3 1.3 collective-permute-start.6
  59.6 17.8 %all-to-all-done = bf16[128,8,512]{2,1,0:T(8,128)(2,1)S(1)} async-done(((bf16[128,8,512]{2,1,0:T(8,128)(2,1)}), bf16[128,8,512]{2,1,0:T(8,128)(2,1)S(1)}, u32[]{:S(2)}, u32[]{:S(2)}) %all-to-all-start) | async-done | bytes 1048608 | tf_op jit(solution)/shard_map/all_to_all | solution.py:626
  77.4 9.1 %trainer.1 = (bf16[512,512]{1,0:T(8,128)(2,1)S(1)}, bf16[512,2048]{1,0:T(8,128)(2,1)}, bf16[512,512]{1,0:T(8,128)(2,1)S(1)}, bf16[512,2048]{1,0:T(8,128)(2,1)}, ...) custom-call(bf16[1024,512]{1,0:T(8,128)(2,1)S(1)} %bitcast.24, bf16[512,2048]{1,0:T(8,128)(2,1)} %bitcast.29, ...), custom_call_target="tpu_custom_call" | custom-call | tf_op jit(solution)/shard_map/trainer/pallas_call | solution.py:630
  86.5 4.7 %all-to-all-start.1 = ((bf16[128,8,256]{2,1,0:T(8,128)(2,1)}), bf16[128,8,256]{2,1,0:T(8,128)(2,1)S(1)}, u32[]{:S(2)}, u32[]{:S(2)}) async-start(bf16[128,8,256]{2,1,0:T(8,128)(2,1)} %bitcast.11), calls=%async_computation.1 | async-start | bytes 1048576 | tf_op jit(solution)/shard_map/all_to_all | solution.py:650
  91.2 5.0 %fusion = f32[512,2048]{1,0:T(8,128)} fusion(bf16[512,512]{1,0:T(8,128)(2,1)S(1)} %get-tuple-element.43, bf16[512,2048]{1,0:T(8,128)(2,1)} %get-tuple-element.44), kind=kOutput, calls=%fused_computation | convolution fusion | flops 1073741824 | bytes 6815744 | tf_op jit(solution)/shard_map/dot_general | solution.py:503
  96.3 3.3 %fusion.1 = f32[2048,512]{1,0:T(8,128)} fusion(bf16[512,2048]{1,0:T(8,128)(2,1)S(1)} %copy-done.3, bf16[512,512]{1,0:T(8,128)(2,1)S(1)} %get-tuple-element.46), kind=kOutput, calls=%fused_computation.1 | convolution fusion | flops 1073741824 | bytes 6815744 | tf_op jit(solution)/shard_map/dot_general | solution.py:503
  99.6 5.6 %all-to-all-done.1 = bf16[128,8,256]{2,1,0:T(8,128)(2,1)S(1)} async-done(((bf16[128,8,256]{2,1,0:T(8,128)(2,1)}), bf16[128,8,256]{2,1,0:T(8,128)(2,1)S(1)}, u32[]{:S(2)}, u32[]{:S(2)}) %all-to-all-start.1) | async-done | bytes 524320 | tf_op jit(solution)/shard_map/all_to_all | solution.py:650
  105.2 0.3 gather.1.own_grad_ref
  105.5 1.1 collective-permute-start.7
  106.6 1.0 collective-permute-done.7.other_grad_ref
  107.6 1.1 part.1
  108.7 23.6 %all_to_all.20.parts_ref = bf16[64,40,256]{2,1,0:T(8,128)(2,1)S(1)} all-to-all(bf16[64,40,256]{2,1,0:T(8,128)(2,1)S(1)} %bitcast.21), channel_id=1, replica_groups={{0,1,2,3,4,5,6,7,16,17,18,19,20,21,22,23,32,33,34,35,36,37,38,39,48,49,..., dimensions={0} | all-to-all | bytes 2621440 | tf_op jit(solution)/shard_map/all_to_all | solution.py:677
  132.3 0.2 total.1
  132.5 24.3 %all_to_all.21 = bf16[64,40,256]{2,1,0:T(8,128)(2,1)S(1)} all-to-all(bf16[64,40,256]{2,1,0:T(8,128)(2,1)S(1)} %total.1), channel_id=1, replica_groups={{0,1,2,3,4,5,6,7,16,17,18,19,20,21,22,23,32,33,34,35,36,37,38,39,48,49,..., dimensions={0} | all-to-all | bytes 2621440 | tf_op jit(solution)/shard_map/all_to_all | solution.py:688
  156.8 3.4 %collective-permute-start.8 = (bf16[2560,256]{1,0:T(8,128)(2,1)S(1)}, bf16[2560,256]{1,0:T(8,128)(2,1)S(1)}, u32[]{:S(2)}, u32[]{:S(2)}) collective-permute-start(bf16[2560,256]{1,0:T(8,128)(2,1)S(1)} %bitcast.22), channel_id=1, source_target_pairs={{0,8},{8,0},{16,24},{24,16},{32,40},{40,32},{48,56},{56,48},{64,72... | collective-permute-start | bytes 3932168 | tf_op jit(solution)/shard_map/ppermute | solution.py:690
  160.2 2.1 %spread_own.1.rest_0_ = f32[2560,512]{1,0:T(8,128)} custom-call(s32[5]{0:T(128)S(1)} %convert_element_type.8.edge_ref, bf16[2560,256]{1,0:T(8,128)(2,1)S(1)} %bitcast.23), custom_call_target="tpu_custom_call" | custom-call | tf_op jit(solution)/shard_map/spread_own/pallas_call | solution.py:693
  162.3 0.6 collective-permute-done.8.half_ref
  162.9 2.1 %spread_other.1 = f32[2560,512]{1,0:T(8,128)} custom-call(s32[5]{0:T(128)S(1)} %convert_element_type.8.edge_ref, bf16[2560,256]{1,0:T(8,128)(2,1)S(1)} %collective-permute-done.8.half_ref, f32[2560,512]{1,0:T(8,128)} %spread_own.1.rest_0_), custom_call_target="tpu_custom_call", output_to_operand_aliasing={{}: (2, {})} | custom-call | tf_op jit(solution)/shard_map/spread_other/pallas_call | solution.py:693
  (18 shorter events, 0.7 us)
Async XLA Ops:
  0.6 1.3 copy-start
  2.2 11.4 %collective-permute-start = (bf16[5,6,32,128]{3,2,1,0:T(8,128)(2,1)S(1)}, bf16[5,6,32,128]{3,2,1,0:T(8,128)(2,1)S(1)}, u32[]{:S(2)}, u32[]{:S(2)}) collective-permute-start(bf16[5,6,32,128]{3,2,1,0:T(8,128)(2,1)S(1)} %get-tuple-element.29), channel_id=1, source_target_pairs={{0,8},{8,16},{16,24},{24,32},{32,40},{40,48},{48,56},{56,64},{64,7... | collective-permute-start | bytes 737288 | tf_op jit(solution)/shard_map/ppermute | solution.py:499
  7.1 7.5 %collective-permute-start.1 = (bf16[5,6,32,128]{3,2,1,0:T(8,128)(2,1)S(1)}, bf16[5,6,32,128]{3,2,1,0:T(8,128)(2,1)S(1)}, u32[]{:S(2)}, u32[]{:S(2)}) collective-permute-start(bf16[5,6,32,128]{3,2,1,0:T(8,128)(2,1)S(1)} %get-tuple-element.30), channel_id=1, source_target_pairs={{8,0},{16,8},{24,16},{32,24},{40,32},{48,40},{56,48},{64,56},{72,6... | collective-permute-start | bytes 737288 | tf_op jit(solution)/shard_map/ppermute | solution.py:499
  9.0 12.3 %collective-permute-start.2 = (bf16[5,96,128]{2,1,0:T(8,128)(2,1)S(1)}, bf16[5,96,128]{2,1,0:T(8,128)(2,1)S(1)}, u32[]{:S(2)}, u32[]{:S(2)}) collective-permute-start(bf16[5,96,128]{2,1,0:T(8,128)(2,1)S(1)} %get-tuple-element.31), channel_id=1, source_target_pairs={{0,1},{1,2},{2,3},{3,4},{4,5},{5,6},{6,7},{8,9},{9,10},{10,11},{11... | collective-permute-start | bytes 368648 | tf_op jit(solution)/shard_map/ppermute | solution.py:499
  12.2 9.1 %collective-permute-start.3 = (bf16[5,96,128]{2,1,0:T(8,128)(2,1)S(1)}, bf16[5,96,128]{2,1,0:T(8,128)(2,1)S(1)}, u32[]{:S(2)}, u32[]{:S(2)}) collective-permute-start(bf16[5,96,128]{2,1,0:T(8,128)(2,1)S(1)} %get-tuple-element.32), channel_id=1, source_target_pairs={{1,0},{2,1},{3,2},{4,3},{5,4},{6,5},{7,6},{9,8},{10,9},{11,10},{12... | collective-permute-start | bytes 368648 | tf_op jit(solution)/shard_map/ppermute | solution.py:499
  14.7 6.7 %collective-permute-start.4 = (bf16[5,32,128]{2,1,0:T(8,128)(2,1)S(1)}, bf16[5,32,128]{2,1,0:T(8,128)(2,1)S(1)}, u32[]{:S(2)}, u32[]{:S(2)}) collective-permute-start(bf16[5,32,128]{2,1,0:T(8,128)(2,1)S(1)} %get-tuple-element.33), channel_id=1, source_target_pairs={{0,1},{1,2},{2,3},{3,4},{4,5},{5,6},{6,7},{8,9},{9,10},{10,11},{11... | collective-permute-start | bytes 122888 | tf_op jit(solution)/shard_map/ppermute | solution.py:499
  17.9 4.7 %collective-permute-start.5 = (bf16[5,32,128]{2,1,0:T(8,128)(2,1)S(1)}, bf16[5,32,128]{2,1,0:T(8,128)(2,1)S(1)}, u32[]{:S(2)}, u32[]{:S(2)}) collective-permute-start(bf16[5,32,128]{2,1,0:T(8,128)(2,1)S(1)} %get-tuple-element.34), channel_id=1, source_target_pairs={{1,0},{2,1},{3,2},{4,3},{5,4},{6,5},{7,6},{9,8},{10,9},{11,10},{12... | collective-permute-start | bytes 122888 | tf_op jit(solution)/shard_map/ppermute | solution.py:499
  40.0 37.5 %copy-start.1 = (f32[1,2048]{1,0:T(1,128)S(1)}, f32[1,2048]{1,0:T(1,128)}, u32[]{:S(2)}) copy-start(f32[1,2048]{1,0:T(1,128)} %b_in_ref.1) | copy-start | bytes 24580
  40.0 37.5 %copy-start.2 = (f32[1,512]{1,0:T(1,128)S(1)}, f32[1,512]{1,0:T(1,128)}, u32[]{:S(2)}) copy-start(f32[1,512]{1,0:T(1,128)} %b_out_ref.1) | copy-start | bytes 6148
  40.0 37.5 %all-to-all-start = ((bf16[128,8,512]{2,1,0:T(8,128)(2,1)}), bf16[128,8,512]{2,1,0:T(8,128)(2,1)S(1)}, u32[]{:S(2)}, u32[]{:S(2)}) async-start(bf16[128,8,512]{2,1,0:T(8,128)(2,1)} %bitcast.7), calls=%async_computation | async-start | bytes 2097152 | tf_op jit(solution)/shard_map/all_to_all | solution.py:626
  58.3 48.3 %collective-permute-start.6 = (bf16[1280,128]{1,0:T(8,128)(2,1)}, bf16[1280,128]{1,0:T(8,128)(2,1)S(1)}, u32[]{:S(2)}, u32[]{:S(2)}) collective-permute-start(bf16[1280,128]{1,0:T(8,128)(2,1)} %get-tuple-element.40), channel_id=1, source_target_pairs={{0,8},{8,0},{16,24},{24,16},{32,40},{40,32},{48,56},{56,48},{64,72... | collective-permute-start | bytes 983048 | tf_op jit(solution)/shard_map/ppermute | solution.py:625
  86.5 18.7 %all-to-all-start.1 = ((bf16[128,8,256]{2,1,0:T(8,128)(2,1)}), bf16[128,8,256]{2,1,0:T(8,128)(2,1)S(1)}, u32[]{:S(2)}, u32[]{:S(2)}) async-start(bf16[128,8,256]{2,1,0:T(8,128)(2,1)} %bitcast.11), calls=%async_computation.1 | async-start | bytes 1048576 | tf_op jit(solution)/shard_map/all_to_all | solution.py:650
  91.2 5.0 %copy-start.3 = (bf16[512,2048]{1,0:T(8,128)(2,1)S(1)}, bf16[512,2048]{1,0:T(8,128)(2,1)}, u32[]{:S(2)}) copy-start(bf16[512,2048]{1,0:T(8,128)(2,1)} %get-tuple-element.45) | copy-start | bytes 6291460
  105.5 2.1 %collective-permute-start.7 = (bf16[128,512]{1,0:T(8,128)(2,1)S(1)}, bf16[128,512]{1,0:T(8,128)(2,1)S(1)}, u32[]{:S(2)}, u32[]{:S(2)}) collective-permute-start(bf16[128,512]{1,0:T(8,128)(2,1)S(1)} %gather.1.own_grad_ref), channel_id=1, source_target_pairs={{0,8},{8,0},{16,24},{24,16},{32,40},{40,32},{48,56},{56,48},{64,72... | collective-permute-start | bytes 393224 | tf_op jit(solution)/shard_map/ppermute | solution.py:662
  156.8 6.1 %collective-permute-start.8 = (bf16[2560,256]{1,0:T(8,128)(2,1)S(1)}, bf16[2560,256]{1,0:T(8,128)(2,1)S(1)}, u32[]{:S(2)}, u32[]{:S(2)}) collective-permute-start(bf16[2560,256]{1,0:T(8,128)(2,1)S(1)} %bitcast.22), channel_id=1, source_target_pairs={{0,8},{8,0},{16,24},{24,16},{32,40},{40,32},{48,56},{56,48},{64,72... | collective-permute-start | bytes 3932168 | tf_op jit(solution)/shard_map/ppermute | solution.py:690

commit v7 on v5

--- a/solution.py
+++ b/solution.py
@@ -55,34 +55,27 @@
     return (pieces[-1] - pieces[1]) * PUSH[-1] + (pieces[2] - pieces[-2]) * PUSH[2]
 
 
-def one_row(src, row, own_z, push_z, window):
+def one_row(src, row, own_z, push_z, begin, end):
     def along(field):
-        middle = src[field, row]
-        xs = {k: src[field, row + k] for k in OFFSETS}
-        ys = {k: rolled(middle, k, 0) for k in OFFSETS}
+        middle = src[field, row, begin:end]
+        xs = {k: src[field, row + k, begin:end] for k in OFFSETS}
+        ys = {k: src[field, row, begin + k : end + k] for k in OFFSETS}
         zs = {k: rolled(middle, k, 1) for k in OFFSETS}
-        return middle, xs, ys, zs
-
-    def own(middle, xs, ys, zs):
-        return (
-            middle * MIDDLE + weighted(xs, OWN_X) + weighted(ys, OWN_Y) + weighted(zs, own_z)
-        )
-
-    cut = (lambda v: v) if window is None else (lambda v: v[window[0] : window[1]])
-    parts = along(4)
-    pressure = cut(own(*parts))
-    px, py, pz = cut(slope_of(parts[1])), cut(slope_of(parts[2])), cut(weighted(parts[3], push_z))
-    parts = along(1)
-    first = cut(own(*parts)) + px
-    spread = cut(slope_of(parts[1]))
-    parts = along(2)
-    second = cut(own(*parts)) + py
-    spread = spread + cut(slope_of(parts[2]))
-    parts = along(3)
-    third = cut(own(*parts)) + pz
-    spread = spread + cut(weighted(parts[3], push_z))
-    parts = along(0)
-    density = cut(own(*parts)) + spread
+        total = middle * MIDDLE + weighted(xs, OWN_X) + weighted(ys, OWN_Y)
+        return total + weighted(zs, own_z), xs, ys, zs
+
+    pressure, xs, ys, zs = along(4)
+    px, py, pz = slope_of(xs), slope_of(ys), weighted(zs, push_z)
+    first, xs, _, _ = along(1)
+    first = first + px
+    spread = slope_of(xs)
+    second, _, ys, _ = along(2)
+    second = second + py
+    spread = spread + slope_of(ys)
+    third, _, _, zs = along(3)
+    third = third + pz
+    spread = spread + weighted(zs, push_z)
+    density = along(0)[0] + spread
     return density, first, second, third, pressure + spread
 
 
@@ -115,38 +108,41 @@
     )
 
 
-def strip_layers(wide_x):
-    layers, place = [], 0
-    for layer in range(REACH):
-        beside = REACH - LIFT // 4 if layer < 4 else 0
-        rows = wide_x + 2 * beside
-        layers.append((layer, beside, rows, place))
-        place += rows
-    return layers, place
-
-
-def strips_kernel(f_ref, xlo_ref, xhi_ref, first_ref, last_ref, lines_ref):
+CORNER = 4
+
+
+def y_faces_kernel(f_ref, first_ref, last_ref, lines_ref):
     wide_x, wide_y = f_ref.shape[1], f_ref.shape[2]
-    layers, _ = strip_layers(wide_x)
-    beside = layers[0][1]
     for at, out_ref in ((0, first_ref), (wide_y - LIFT, last_ref)):
-        tile = slice(at, at + LIFT)
-        for row in range(wide_x + 2 * beside):
-            place = slice(row * LIFT, (row + 1) * LIFT)
-            if row < beside:
-                piece = xlo_ref[:, REACH - beside + row, tile].astype(jnp.float32)
-            elif row < beside + wide_x:
-                piece = f_ref[:, row - beside, tile]
-            else:
-                piece = xhi_ref[:, row - beside - wide_x, tile].astype(jnp.float32)
-            lines_ref[:, place] = piece
         for field in range(FIELDS):
-            for layer, near, rows, place in layers:
+            for row in range(wide_x):
+                lines_ref[row * LIFT : (row + 1) * LIFT] = f_ref[field, row, at : at + LIFT]
+            for layer in range(REACH):
                 line = layer if at == 0 else LIFT - 1 - layer
-                start = (beside - near) * LIFT + line
-                out_ref[field, place : place + rows] = lines_ref[
-                    field, pl.ds(start, rows, stride=LIFT), :
+                out_ref[field, layer * wide_x : (layer + 1) * wide_x] = lines_ref[
+                    pl.ds(line, wide_x, stride=LIFT), :
                 ].astype(jnp.bfloat16)
+
+
+def x_faces_kernel(f_ref, ylo_ref, yhi_ref, first_ref, last_ref, lines_ref):
+    wide_x, wide_y = f_ref.shape[1], f_ref.shape[2]
+    tall = wide_y + 2 * CORNER
+    for at, out_ref in ((0, first_ref), (wide_x - REACH, last_ref)):
+        for field in range(FIELDS):
+            low = ylo_ref[field].astype(jnp.float32)
+            high = yhi_ref[field].astype(jnp.float32)
+            for row in range(REACH):
+                begin = row * tall + CORNER
+                lines_ref[begin : begin + wide_y] = f_ref[field, at + row]
+            for layer in range(CORNER):
+                rows = slice(layer * wide_x + at, layer * wide_x + at + REACH)
+                below, above = CORNER - 1 - layer, CORNER + wide_y + layer
+                lines_ref[pl.ds(below, REACH, stride=tall), :] = low[rows]
+                lines_ref[pl.ds(above, REACH, stride=tall), :] = high[rows]
+            for row in range(REACH):
+                out_ref[field, row] = lines_ref[row * tall : (row + 1) * tall].astype(
+                    jnp.bfloat16
+                )
 
 
 def window_kernel(
@@ -188,18 +184,17 @@
     push_z = {k: jnp.where(inside[k], PUSH[k], 0.0) for k in OFFSETS}
 
     first_ref[:, REACH:top_x, LIFT:top_y, :] = f_ref[...]
-    first_ref[:, 0:REACH, LIFT:top_y, :] = xlo_ref[...].astype(jnp.float32)
-    first_ref[:, top_x:full_x, LIFT:top_y, :] = xhi_ref[...].astype(jnp.float32)
+    reached = slice(LIFT - CORNER, top_y + CORNER)
+    first_ref[:, 0:REACH, reached, :] = xlo_ref[...].astype(jnp.float32)
+    first_ref[:, top_x:full_x, reached, :] = xhi_ref[...].astype(jnp.float32)
     for field in range(FIELDS):
-        for layer, beside, lines, place in strip_layers(wide_x)[0]:
-            rows = slice(REACH - beside, REACH - beside + lines)
-            packed = slice(place, place + lines)
-            first_ref[field, rows, LIFT - 1 - layer, :] = ylo_ref[field, packed].astype(
-                jnp.float32
-            )
-            first_ref[field, rows, top_y + layer, :] = yhi_ref[field, packed].astype(
-                jnp.float32
-            )
+        for low, face_ref in ((True, ylo_ref), (False, yhi_ref)):
+            face = face_ref[field].astype(jnp.float32)
+            for layer in range(REACH):
+                line = LIFT - 1 - layer if low else top_y + layer
+                first_ref[field, REACH:top_x, line, :] = face[
+                    layer * wide_x : (layer + 1) * wide_x
+                ]
 
     def clear(ref, least):
         @pl.when(edge_ref[0] == 1)
@@ -221,23 +216,26 @@
             ref[:, :, top_y:full_y] = jnp.zeros((FIELDS, full_x, LIFT, wide_z), jnp.float32)
 
     def step(src, dst, least):
+        begin = LIFT - REACH + least
+        end = begin + wide_y + LIFT
+
         def body(row, carry):
-            done = one_row(src, row, own_z, push_z, None)
+            done = one_row(src, row, own_z, push_z, begin, end)
             for field in range(FIELDS):
-                dst[field, row] = done[field]
+                dst[field, row, begin:end] = done[field]
             return carry
 
-        lax.fori_loop(least, full_x - least, body, 0, unroll=2)
+        lax.fori_loop(least, full_x - least, body, 0, unroll=4)
         clear(dst, least)
 
     def last_step(src):
         def body(row, carry):
-            done = one_row(src, row, own_z, push_z, (LIFT, top_y))
+            done = one_row(src, row, own_z, push_z, LIFT, top_y)
             for field in range(FIELDS):
                 new_ref[field, row - REACH] = done[field]
             return carry
 
-        lax.fori_loop(REACH, top_x, body, 0, unroll=2)
+        lax.fori_loop(REACH, top_x, body, 0, unroll=4)
 
     z_count = wide_z // PATCH
     lane_r = lax.broadcasted_iota(jnp.int32, (wide_z, wide_z), 0)
@@ -510,10 +508,6 @@
     per = slots * BLOCK_ROWS
     features = FIELDS * PATCH**3
 
-    def narrow(piece):
-        return piece.astype(jnp.bfloat16)
-
-    xlo, xhi = neighbours(narrow(fields[:, :REACH]), narrow(fields[:, wide_x - REACH :]), "gx")
     at_x, at_y = lax.axis_index("gx"), lax.axis_index("gy")
     core = at_x % 2
     edges = jnp.stack(
@@ -532,17 +526,27 @@
     def shape(dims, kind):
         return jax.ShapeDtypeStruct(dims, kind)
 
-    layers, strip = strip_layers(wide_x)
+    tall = wide_y + 2 * CORNER
     y_first, y_last = pl.pallas_call(
-        strips_kernel,
-        out_shape=(shape((FIELDS, strip, wide_z), jnp.bfloat16),) * 2,
+        y_faces_kernel,
+        out_shape=(shape((FIELDS, REACH * wide_x, wide_z), jnp.bfloat16),) * 2,
+        in_specs=[vmem],
+        out_specs=(vmem,) * 2,
+        scratch_shapes=[pltpu.VMEM((wide_x * LIFT, wide_z), jnp.float32)],
+        compiler_params=grant(8),
+        name="y_faces",
+    )(fields)
+    ylo, yhi = neighbours(y_first, y_last, "gy")
+    x_first, x_last = pl.pallas_call(
+        x_faces_kernel,
+        out_shape=(shape((FIELDS, REACH, tall, wide_z), jnp.bfloat16),) * 2,
         in_specs=[vmem] * 3,
         out_specs=(vmem,) * 2,
-        scratch_shapes=[pltpu.VMEM((FIELDS, layers[0][2] * LIFT, wide_z), jnp.float32)],
+        scratch_shapes=[pltpu.VMEM((REACH * tall, wide_z), jnp.float32)],
         compiler_params=grant(8),
-        name="strips",
-    )(fields, xlo, xhi)
-    ylo, yhi = neighbours(y_first, y_last, "gy")
+        name="x_faces",
+    )(fields, ylo, yhi)
+    xlo, xhi = neighbours(x_first, x_last, "gx")
 
     send_rows = 2 * devices * per
     source_pick, target_pick, chosen = pl.pallas_call(

time: 163 us -> 161 us (0.988)
  Pallas kernels: 32.9 us -> 30.1 us
    pallas_call x1, Pallas kernels: 17.3 us -> 14.4 us  [per_device(): pl.pallas_call(functools.partial(window_kernel, (wide_x, wide_y, wide_z),...]
    ppermute x2, starting transfers between devices: 6.74 us -> 9.57 us  [neighbours(): lax.ppermute(high_piece, axis, up)]
    ppermute x2, waiting for transfers between devices: 5.76 us -> 8.17 us  [neighbours(): lax.ppermute(low_piece, axis, down)]
    all_to_all x1, starting transfers between devices: 14.7 us -> 13 us  [per_device(): lax.all_to_all(send.reshape(devices, 2 * per, EMBED), axes, 0, 0, tiled=T...]
where the time goes in v7:
time: 161 us; the launch traced here: 160 us
  blocking collectives  47.8 us (30%)
  starting transfers between devices  36.4 us (23%)
  waiting for transfers between devices  34.7 us (22%)
  Pallas kernels  30.1 us (19%)
  matrix products  8.36 us (5%)
  local copies, waits for them, and re-layouts  1.73 us (1%)
    all_to_all x1, blocking collectives, per_device(): lax.all_to_all(copies, axes, 0, 0, axis_index_groups=groups, tiled=True)  24.3 us
    all_to_all x1, blocking collectives, per_device(): lax.all_to_all(parts.reshape(members, piece, width), axes, 0, 0, axis_ind...  23.6 us
    all_to_all x1, waiting for transfers between devices, per_device(): lax.all_to_all(send.reshape(devices, 2 * per, EMBED), axes, 0, 0, tiled=T...  17.8 us
    pallas_call x1, Pallas kernels, per_device(): pl.pallas_call(functools.partial(window_kernel, (wide_x, wide_y, wide_z),...  14.4 us
    all_to_all x1, starting transfers between devices, per_device(): lax.all_to_all(send.reshape(devices, 2 * per, EMBED), axes, 0, 0, tiled=T...  13 us
    ppermute x2, starting transfers between devices, neighbours(): lax.ppermute(high_piece, axis, up)  9.57 us
    pallas_call x1, Pallas kernels, per_device(): pl.pallas_call(functools.partial(trainer_kernel, per), out_shape=(shape((...  9.08 us
    dot_general x2, matrix products, contract_rows(): lax.dot_general(left, right, (((0,), (0,)), ((), ())), preferred_element_...  8.36 us
  transfers between devices with their start and end apart: 9, of which 8 were waited for; matrix products, arithmetic and copies ran while one was open for 5% of the time, Pallas kernels for 7%

profile of v7, /device:TPU:1, one launch (start us, length us, event | category | flops | bytes accessed | tf_op | source)
XLA Modules:
  0.0 160.0 jit_solution(8249849104570894812)
XLA Ops:
  0.6 1.3 copy-done
  2.0 0.2 y_faces.1
  2.1 4.0 %collective-permute-start = (bf16[5,96,128]{2,1,0:T(8,128)(2,1)S(1)}, bf16[5,96,128]{2,1,0:T(8,128)(2,1)S(1)}, u32[]{:S(2)}, u32[]{:S(2)}) collective-permute-start(bf16[5,96,128]{2,1,0:T(8,128)(2,1)S(1)} %get-tuple-element.27), channel_id=1, source_target_pairs={{0,1},{1,2},{2,3},{3,4},{4,5},{5,6},{6,7},{8,9},{9,10},{10,11},{11... | collective-permute-start | bytes 368648 | tf_op jit(solution)/shard_map/ppermute | solution.py:485
  6.2 1.3 collective-permute-start.1
  7.5 0.5 collective-permute-done.ylo_ref
  8.0 3.8 %collective-permute-done.1.yhi_ref = bf16[5,96,128]{2,1,0:T(8,128)(2,1)S(1)} collective-permute-done((bf16[5,96,128]{2,1,0:T(8,128)(2,1)S(1)}, bf16[5,96,128]{2,1,0:T(8,128)(2,1)S(1)}, u32[]{:S(2)}, u32[]{:S(2)}) %collective-permute-start.1) | collective-permute-done | bytes 122912 | tf_op jit(solution)/shard_map/ppermute | solution.py:485
  11.8 0.2 x_faces.1
  12.0 5.5 %collective-permute-start.2 = (bf16[5,6,40,128]{3,2,1,0:T(8,128)(2,1)S(1)}, bf16[5,6,40,128]{3,2,1,0:T(8,128)(2,1)S(1)}, u32[]{:S(2)}, u32[]{:S(2)}) collective-permute-start(bf16[5,6,40,128]{3,2,1,0:T(8,128)(2,1)S(1)} %get-tuple-element.29), channel_id=1, source_target_pairs={{0,8},{8,16},{16,24},{24,32},{32,40},{40,48},{48,56},{56,64},{64,7... | collective-permute-start | bytes 921608 | tf_op jit(solution)/shard_map/ppermute | solution.py:485
  17.5 1.9 %collective-permute-start.3 = (bf16[5,6,40,128]{3,2,1,0:T(8,128)(2,1)S(1)}, bf16[5,6,40,128]{3,2,1,0:T(8,128)(2,1)S(1)}, u32[]{:S(2)}, u32[]{:S(2)}) collective-permute-start(bf16[5,6,40,128]{3,2,1,0:T(8,128)(2,1)S(1)} %get-tuple-element.30), channel_id=1, source_target_pairs={{8,0},{16,8},{24,16},{32,24},{40,32},{48,40},{56,48},{64,56},{72,6... | collective-permute-start | bytes 921608 | tf_op jit(solution)/shard_map/ppermute | solution.py:485
  19.9 0.4 slots.1
  20.3 1.0 collective-permute-done.2.xlo_ref
  21.3 4.4 %collective-permute-done.3.xhi_ref = bf16[5,6,40,128]{3,2,1,0:T(8,128)(2,1)S(1)} collective-permute-done((bf16[5,6,40,128]{3,2,1,0:T(8,128)(2,1)S(1)}, bf16[5,6,40,128]{3,2,1,0:T(8,128)(2,1)S(1)}, u32[]{:S(2)}, u32[]{:S(2)}) %collective-permute-start.3) | collective-permute-done | bytes 307232 | tf_op jit(solution)/shard_map/ppermute | solution.py:485
  25.7 14.4 %window.1 = (f32[5,16,32,128]{3,2,1,0:T(8,128)}, bf16[1280,128]{1,0:T(8,128)(2,1)S(1)}, bf16[1280,128]{1,0:T(8,128)(2,1)}, bf16[1024,512]{1,0:T(8,128)(2,1)}) custom-call(s32[5]{0:T(128)S(1)} %convert_element_type.8.edge_ref, f32[5,16,32,128]{3,2,1,0:T(8,128)} %f_ref.5, bf16[5,6,40,128]{3,2,1,0:T(8,128)(2,1)S(1)} %collective-permute-done.2.xlo_ref, ...), custom_call_target="tpu_custom_call" | custom-call | tf_op jit(solution)/shard_map/window/pallas_call | solution.py:566
  40.2 13.0 %all-to-all-start = ((bf16[128,8,512]{2,1,0:T(8,128)(2,1)}), bf16[128,8,512]{2,1,0:T(8,128)(2,1)S(1)}, u32[]{:S(2)}, u32[]{:S(2)}) async-start(bf16[128,8,512]{2,1,0:T(8,128)(2,1)} %bitcast.7), calls=%async_computation | async-start | bytes 2097152 | tf_op jit(solution)/shard_map/all_to_all | solution.py:599
  53.2 1.3 collective-permute-start.4
  54.5 17.8 %all-to-all-done = bf16[128,8,512]{2,1,0:T(8,128)(2,1)S(1)} async-done(((bf16[128,8,512]{2,1,0:T(8,128)(2,1)}), bf16[128,8,512]{2,1,0:T(8,128)(2,1)S(1)}, u32[]{:S(2)}, u32[]{:S(2)}) %all-to-all-start) | async-done | bytes 1048608 | tf_op jit(solution)/shard_map/all_to_all | solution.py:599
  72.4 9.1 %trainer.1 = (bf16[512,512]{1,0:T(8,128)(2,1)S(1)}, bf16[512,2048]{1,0:T(8,128)(2,1)}, bf16[512,512]{1,0:T(8,128)(2,1)S(1)}, bf16[512,2048]{1,0:T(8,128)(2,1)}, ...) custom-call(bf16[1024,512]{1,0:T(8,128)(2,1)S(1)} %bitcast.24, bf16[512,2048]{1,0:T(8,128)(2,1)} %bitcast.29, ...), custom_call_target="tpu_custom_call" | custom-call | tf_op jit(solution)/shard_map/trainer/pallas_call | solution.py:603
  81.4 4.7 %all-to-all-start.1 = ((bf16[128,8,256]{2,1,0:T(8,128)(2,1)}), bf16[128,8,256]{2,1,0:T(8,128)(2,1)S(1)}, u32[]{:S(2)}, u32[]{:S(2)}) async-start(bf16[128,8,256]{2,1,0:T(8,128)(2,1)} %bitcast.11), calls=%async_computation.1 | async-start | bytes 1048576 | tf_op jit(solution)/shard_map/all_to_all | solution.py:623
  86.2 5.0 %fusion = f32[512,2048]{1,0:T(8,128)} fusion(bf16[512,512]{1,0:T(8,128)(2,1)S(1)} %get-tuple-element.39, bf16[512,2048]{1,0:T(8,128)(2,1)} %get-tuple-element.40), kind=kOutput, calls=%fused_computation | convolution fusion | flops 1073741824 | bytes 6815744 | tf_op jit(solution)/shard_map/dot_general | solution.py:489
  91.2 3.3 %fusion.1 = f32[2048,512]{1,0:T(8,128)} fusion(bf16[512,2048]{1,0:T(8,128)(2,1)S(1)} %copy-done.3, bf16[512,512]{1,0:T(8,128)(2,1)S(1)} %get-tuple-element.42), kind=kOutput, calls=%fused_computation.1 | convolution fusion | flops 1073741824 | bytes 6815744 | tf_op jit(solution)/shard_map/dot_general | solution.py:489
  94.5 5.6 %all-to-all-done.1 = bf16[128,8,256]{2,1,0:T(8,128)(2,1)S(1)} async-done(((bf16[128,8,256]{2,1,0:T(8,128)(2,1)}), bf16[128,8,256]{2,1,0:T(8,128)(2,1)S(1)}, u32[]{:S(2)}, u32[]{:S(2)}) %all-to-all-start.1) | async-done | bytes 524320 | tf_op jit(solution)/shard_map/all_to_all | solution.py:623
  100.1 0.3 gather.1.own_grad_ref
  100.4 1.1 collective-permute-start.5
  101.5 1.0 collective-permute-done.5.other_grad_ref
  102.5 1.1 part.1
  103.6 23.6 %all_to_all.20.parts_ref = bf16[64,40,256]{2,1,0:T(8,128)(2,1)S(1)} all-to-all(bf16[64,40,256]{2,1,0:T(8,128)(2,1)S(1)} %bitcast.21), channel_id=1, replica_groups={{0,1,2,3,4,5,6,7,16,17,18,19,20,21,22,23,32,33,34,35,36,37,38,39,48,49,..., dimensions={0} | all-to-all | bytes 2621440 | tf_op jit(solution)/shard_map/all_to_all | solution.py:650
  127.2 0.2 total.1
  127.4 24.3 %all_to_all.21 = bf16[64,40,256]{2,1,0:T(8,128)(2,1)S(1)} all-to-all(bf16[64,40,256]{2,1,0:T(8,128)(2,1)S(1)} %total.1), channel_id=1, replica_groups={{0,1,2,3,4,5,6,7,16,17,18,19,20,21,22,23,32,33,34,35,36,37,38,39,48,49,..., dimensions={0} | all-to-all | bytes 2621440 | tf_op jit(solution)/shard_map/all_to_all | solution.py:661
  151.7 3.4 %collective-permute-start.6 = (bf16[2560,256]{1,0:T(8,128)(2,1)S(1)}, bf16[2560,256]{1,0:T(8,128)(2,1)S(1)}, u32[]{:S(2)}, u32[]{:S(2)}) collective-permute-start(bf16[2560,256]{1,0:T(8,128)(2,1)S(1)} %bitcast.22), channel_id=1, source_target_pairs={{0,8},{8,0},{16,24},{24,16},{32,40},{40,32},{48,56},{56,48},{64,72... | collective-permute-start | bytes 3932168 | tf_op jit(solution)/shard_map/ppermute | solution.py:663
  155.1 2.1 %spread_own.1.rest_0_ = f32[2560,512]{1,0:T(8,128)} custom-call(s32[5]{0:T(128)S(1)} %convert_element_type.8.edge_ref, bf16[2560,256]{1,0:T(8,128)(2,1)S(1)} %bitcast.23), custom_call_target="tpu_custom_call" | custom-call | tf_op jit(solution)/shard_map/spread_own/pallas_call | solution.py:666
  157.2 0.6 collective-permute-done.6.half_ref
  157.8 2.1 %spread_other.1 = f32[2560,512]{1,0:T(8,128)} custom-call(s32[5]{0:T(128)S(1)} %convert_element_type.8.edge_ref, bf16[2560,256]{1,0:T(8,128)(2,1)S(1)} %collective-permute-done.6.half_ref, f32[2560,512]{1,0:T(8,128)} %spread_own.1.rest_0_), custom_call_target="tpu_custom_call", output_to_operand_aliasing={{}: (2, {})} | custom-call | tf_op jit(solution)/shard_map/spread_other/pallas_call | solution.py:666
  (18 shorter events, 0.4 us)
Async XLA Ops:
  0.6 1.3 copy-start
  2.0 17.5 %copy-start.5 = (s32[64,1]{0,1:T(1,128)S(1)}, s32[64,1]{0,1:T(1,128)}, u32[]{:S(2)}) copy-start(s32[64,1]{0,1:T(1,128)} %param.10) | copy-start | bytes 772
  2.0 17.9 %copy-start.4 = (s32[2,4,16]{2,1,0:T(4,128)S(1)}, s32[2,4,16]{2,1,0:T(4,128)}, u32[]{:S(2)}) copy-start(s32[2,4,16]{2,1,0:T(4,128)} %param.11) | copy-start | bytes 1540
  2.1 5.9 %collective-permute-start = (bf16[5,96,128]{2,1,0:T(8,128)(2,1)S(1)}, bf16[5,96,128]{2,1,0:T(8,128)(2,1)S(1)}, u32[]{:S(2)}, u32[]{:S(2)}) collective-permute-start(bf16[5,96,128]{2,1,0:T(8,128)(2,1)S(1)} %get-tuple-element.27), channel_id=1, source_target_pairs={{0,1},{1,2},{2,3},{3,4},{4,5},{5,6},{6,7},{8,9},{9,10},{10,11},{11... | collective-permute-start | bytes 368648 | tf_op jit(solution)/shard_map/ppermute | solution.py:485
  6.2 5.6 %collective-permute-start.1 = (bf16[5,96,128]{2,1,0:T(8,128)(2,1)S(1)}, bf16[5,96,128]{2,1,0:T(8,128)(2,1)S(1)}, u32[]{:S(2)}, u32[]{:S(2)}) collective-permute-start(bf16[5,96,128]{2,1,0:T(8,128)(2,1)S(1)} %get-tuple-element.28), channel_id=1, source_target_pairs={{1,0},{2,1},{3,2},{4,3},{5,4},{6,5},{7,6},{9,8},{10,9},{11,10},{12... | collective-permute-start | bytes 368648 | tf_op jit(solution)/shard_map/ppermute | solution.py:485
  12.0 9.3 %collective-permute-start.2 = (bf16[5,6,40,128]{3,2,1,0:T(8,128)(2,1)S(1)}, bf16[5,6,40,128]{3,2,1,0:T(8,128)(2,1)S(1)}, u32[]{:S(2)}, u32[]{:S(2)}) collective-permute-start(bf16[5,6,40,128]{3,2,1,0:T(8,128)(2,1)S(1)} %get-tuple-element.29), channel_id=1, source_target_pairs={{0,8},{8,16},{16,24},{24,32},{32,40},{40,48},{48,56},{56,64},{64,7... | collective-permute-start | bytes 921608 | tf_op jit(solution)/shard_map/ppermute | solution.py:485
  17.5 8.2 %collective-permute-start.3 = (bf16[5,6,40,128]{3,2,1,0:T(8,128)(2,1)S(1)}, bf16[5,6,40,128]{3,2,1,0:T(8,128)(2,1)S(1)}, u32[]{:S(2)}, u32[]{:S(2)}) collective-permute-start(bf16[5,6,40,128]{3,2,1,0:T(8,128)(2,1)S(1)} %get-tuple-element.30), channel_id=1, source_target_pairs={{8,0},{16,8},{24,16},{32,24},{40,32},{48,40},{56,48},{64,56},{72,6... | collective-permute-start | bytes 921608 | tf_op jit(solution)/shard_map/ppermute | solution.py:485
  40.1 32.2 %copy-start.1 = (f32[1,2048]{1,0:T(1,128)S(1)}, f32[1,2048]{1,0:T(1,128)}, u32[]{:S(2)}) copy-start(f32[1,2048]{1,0:T(1,128)} %b_in_ref.1) | copy-start | bytes 24580
  40.2 32.2 %copy-start.2 = (f32[1,512]{1,0:T(1,128)S(1)}, f32[1,512]{1,0:T(1,128)}, u32[]{:S(2)}) copy-start(f32[1,512]{1,0:T(1,128)} %b_out_ref.1) | copy-start | bytes 6148
  40.2 32.2 %all-to-all-start = ((bf16[128,8,512]{2,1,0:T(8,128)(2,1)}), bf16[128,8,512]{2,1,0:T(8,128)(2,1)S(1)}, u32[]{:S(2)}, u32[]{:S(2)}) async-start(bf16[128,8,512]{2,1,0:T(8,128)(2,1)} %bitcast.7), calls=%async_computation | async-start | bytes 2097152 | tf_op jit(solution)/shard_map/all_to_all | solution.py:599
  53.2 48.3 %collective-permute-start.4 = (bf16[1280,128]{1,0:T(8,128)(2,1)}, bf16[1280,128]{1,0:T(8,128)(2,1)S(1)}, u32[]{:S(2)}, u32[]{:S(2)}) collective-permute-start(bf16[1280,128]{1,0:T(8,128)(2,1)} %get-tuple-element.36), channel_id=1, source_target_pairs={{0,8},{8,0},{16,24},{24,16},{32,40},{40,32},{48,56},{56,48},{64,72... | collective-permute-start | bytes 983048 | tf_op jit(solution)/shard_map/ppermute | solution.py:598
  81.4 18.7 %all-to-all-start.1 = ((bf16[128,8,256]{2,1,0:T(8,128)(2,1)}), bf16[128,8,256]{2,1,0:T(8,128)(2,1)S(1)}, u32[]{:S(2)}, u32[]{:S(2)}) async-start(bf16[128,8,256]{2,1,0:T(8,128)(2,1)} %bitcast.11), calls=%async_computation.1 | async-start | bytes 1048576 | tf_op jit(solution)/shard_map/all_to_all | solution.py:623
  86.1 5.0 %copy-start.3 = (bf16[512,2048]{1,0:T(8,128)(2,1)S(1)}, bf16[512,2048]{1,0:T(8,128)(2,1)}, u32[]{:S(2)}) copy-start(bf16[512,2048]{1,0:T(8,128)(2,1)} %get-tuple-element.41) | copy-start | bytes 6291460
  100.4 2.1 %collective-permute-start.5 = (bf16[128,512]{1,0:T(8,128)(2,1)S(1)}, bf16[128,512]{1,0:T(8,128)(2,1)S(1)}, u32[]{:S(2)}, u32[]{:S(2)}) collective-permute-start(bf16[128,512]{1,0:T(8,128)(2,1)S(1)} %gather.1.own_grad_ref), channel_id=1, source_target_pairs={{0,8},{8,0},{16,24},{24,16},{32,40},{40,32},{48,56},{56,48},{64,72... | collective-permute-start | bytes 393224 | tf_op jit(solution)/shard_map/ppermute | solution.py:635
  151.7 6.1 %collective-permute-start.6 = (bf16[2560,256]{1,0:T(8,128)(2,1)S(1)}, bf16[2560,256]{1,0:T(8,128)(2,1)S(1)}, u32[]{:S(2)}, u32[]{:S(2)}) collective-permute-start(bf16[2560,256]{1,0:T(8,128)(2,1)S(1)} %bitcast.22), channel_id=1, source_target_pairs={{0,8},{8,0},{16,24},{24,16},{32,40},{40,32},{48,56},{56,48},{64,72... | collective-permute-start | bytes 3932168 | tf_op jit(solution)/shard_map/ppermute | solution.py:663

commit v8 on v7

--- a/solution.py
+++ b/solution.py
@@ -111,38 +111,65 @@
 CORNER = 4
 
 
-def y_faces_kernel(f_ref, first_ref, last_ref, lines_ref):
+def by_parity(parity, act, near_ref, far_ref):
+    @pl.when(parity == 0)
+    def _():
+        act(far_ref, near_ref)
+
+    @pl.when(parity == 1)
+    def _():
+        act(near_ref, far_ref)
+
+
+def y_faces_kernel(edge_ref, f_ref, near_ref, far_ref, lines_ref):
     wide_x, wide_y = f_ref.shape[1], f_ref.shape[2]
-    for at, out_ref in ((0, first_ref), (wide_y - LIFT, last_ref)):
-        for field in range(FIELDS):
-            for row in range(wide_x):
-                lines_ref[row * LIFT : (row + 1) * LIFT] = f_ref[field, row, at : at + LIFT]
-            for layer in range(REACH):
-                line = layer if at == 0 else LIFT - 1 - layer
-                out_ref[field, layer * wide_x : (layer + 1) * wide_x] = lines_ref[
-                    pl.ds(line, wide_x, stride=LIFT), :
-                ].astype(jnp.bfloat16)
-
-
-def x_faces_kernel(f_ref, ylo_ref, yhi_ref, first_ref, last_ref, lines_ref):
+
+    def write(first_ref, last_ref):
+        for at, out_ref in ((0, first_ref), (wide_y - LIFT, last_ref)):
+            for field in range(FIELDS):
+                for row in range(wide_x):
+                    lines_ref[row * LIFT : (row + 1) * LIFT] = f_ref[field, row, at : at + LIFT]
+                for layer in range(REACH):
+                    line = layer if at == 0 else LIFT - 1 - layer
+                    out_ref[field, layer * wide_x : (layer + 1) * wide_x] = lines_ref[
+                        pl.ds(line, wide_x, stride=LIFT), :
+                    ].astype(jnp.bfloat16)
+
+    by_parity(edge_ref[5], write, near_ref, far_ref)
+
+
+def x_faces_kernel(edge_ref, f_ref, y_near_ref, y_far_ref, near_ref, far_ref, lines_ref):
     wide_x, wide_y = f_ref.shape[1], f_ref.shape[2]
     tall = wide_y + 2 * CORNER
-    for at, out_ref in ((0, first_ref), (wide_x - REACH, last_ref)):
+    ends = (0, wide_x - REACH)
+
+    def corners(ylo_ref, yhi_ref):
         for field in range(FIELDS):
             low = ylo_ref[field].astype(jnp.float32)
             high = yhi_ref[field].astype(jnp.float32)
+            for end, at in enumerate(ends):
+                for layer in range(CORNER):
+                    rows = slice(layer * wide_x + at, layer * wide_x + at + REACH)
+                    below, above = CORNER - 1 - layer, CORNER + wide_y + layer
+                    lines_ref[field, end, pl.ds(below, REACH, stride=tall), :] = low[rows]
+                    lines_ref[field, end, pl.ds(above, REACH, stride=tall), :] = high[rows]
+
+    by_parity(edge_ref[5], corners, y_near_ref, y_far_ref)
+    for field in range(FIELDS):
+        for end, at in enumerate(ends):
             for row in range(REACH):
                 begin = row * tall + CORNER
-                lines_ref[begin : begin + wide_y] = f_ref[field, at + row]
-            for layer in range(CORNER):
-                rows = slice(layer * wide_x + at, layer * wide_x + at + REACH)
-                below, above = CORNER - 1 - layer, CORNER + wide_y + layer
-                lines_ref[pl.ds(below, REACH, stride=tall), :] = low[rows]
-                lines_ref[pl.ds(above, REACH, stride=tall), :] = high[rows]
-            for row in range(REACH):
-                out_ref[field, row] = lines_ref[row * tall : (row + 1) * tall].astype(
-                    jnp.bfloat16
-                )
+                lines_ref[field, end, begin : begin + wide_y] = f_ref[field, at + row]
+
+    def write(first_ref, last_ref):
+        for field in range(FIELDS):
+            for end, out_ref in enumerate((first_ref, last_ref)):
+                for row in range(REACH):
+                    out_ref[field, row] = lines_ref[
+                        field, end, row * tall : (row + 1) * tall
+                    ].astype(jnp.bfloat16)
+
+    by_parity(edge_ref[4], write, near_ref, far_ref)
 
 
 def window_kernel(
@@ -150,10 +177,10 @@
     per,
     edge_ref,
     f_ref,
-    xlo_ref,
-    xhi_ref,
-    ylo_ref,
-    yhi_ref,
+    x_near_ref,
+    x_far_ref,
+    y_near_ref,
+    y_far_ref,
     chosen_ref,
     source_pick_ref,
     target_pick_ref,
@@ -185,16 +212,23 @@
 
     first_ref[:, REACH:top_x, LIFT:top_y, :] = f_ref[...]
     reached = slice(LIFT - CORNER, top_y + CORNER)
-    first_ref[:, 0:REACH, reached, :] = xlo_ref[...].astype(jnp.float32)
-    first_ref[:, top_x:full_x, reached, :] = xhi_ref[...].astype(jnp.float32)
-    for field in range(FIELDS):
-        for low, face_ref in ((True, ylo_ref), (False, yhi_ref)):
-            face = face_ref[field].astype(jnp.float32)
-            for layer in range(REACH):
-                line = LIFT - 1 - layer if low else top_y + layer
-                first_ref[field, REACH:top_x, line, :] = face[
-                    layer * wide_x : (layer + 1) * wide_x
-                ]
+
+    def beside_x(xlo_ref, xhi_ref):
+        first_ref[:, 0:REACH, reached, :] = xlo_ref[...].astype(jnp.float32)
+        first_ref[:, top_x:full_x, reached, :] = xhi_ref[...].astype(jnp.float32)
+
+    def beside_y(ylo_ref, yhi_ref):
+        for field in range(FIELDS):
+            for low, face_ref in ((True, ylo_ref), (False, yhi_ref)):
+                face = face_ref[field].astype(jnp.float32)
+                for layer in range(REACH):
+                    line = LIFT - 1 - layer if low else top_y + layer
+                    first_ref[field, REACH:top_x, line, :] = face[
+                        layer * wide_x : (layer + 1) * wide_x
+                    ]
+
+    by_parity(edge_ref[4], beside_x, x_near_ref, x_far_ref)
+    by_parity(edge_ref[5], beside_y, y_near_ref, y_far_ref)
 
     def clear(ref, least):
         @pl.when(edge_ref[0] == 1)
@@ -478,11 +512,11 @@
         store.wait()
 
 
-def neighbours(low_piece, high_piece, axis):
+def swapped(near_piece, far_piece, axis):
     count = lax.axis_size(axis)
-    up = [(i, i + 1) for i in range(count - 1)]
-    down = [(b, a) for a, b in up]
-    return lax.ppermute(high_piece, axis, up), lax.ppermute(low_piece, axis, down)
+    near = [(i, i ^ 1) for i in range(count)]
+    far = [pair for i in range(1, count - 1, 2) for pair in ((i, i + 1), (i + 1, i))]
+    return lax.ppermute(near_piece, axis, near), lax.ppermute(far_piece, axis, far)
 
 
 def contract_rows(left, right):
@@ -509,9 +543,15 @@
     features = FIELDS * PATCH**3
 
     at_x, at_y = lax.axis_index("gx"), lax.axis_index("gy")
-    core = at_x % 2
     edges = jnp.stack(
-        [at_x == 0, at_x == n_x - 1, at_y == 0, at_y == n_y - 1, core == 1]
+        [
+            at_x == 0,
+            at_x == n_x - 1,
+            at_y == 0,
+            at_y == n_y - 1,
+            at_x % 2 == 1,
+            at_y % 2 == 1,
+        ]
     ).astype(jnp.int32)
     own_patch = jnp.repeat(trainer_of[:, 0], BLOCK_ROWS)
     lag = lag_index.reshape(-1, lag_index.shape[2]).astype(jnp.float32)
@@ -527,26 +567,26 @@
         return jax.ShapeDtypeStruct(dims, kind)
 
     tall = wide_y + 2 * CORNER
-    y_first, y_last = pl.pallas_call(
+    y_near, y_far = pl.pallas_call(
         y_faces_kernel,
         out_shape=(shape((FIELDS, REACH * wide_x, wide_z), jnp.bfloat16),) * 2,
-        in_specs=[vmem],
+        in_specs=[smem, vmem],
         out_specs=(vmem,) * 2,
         scratch_shapes=[pltpu.VMEM((wide_x * LIFT, wide_z), jnp.float32)],
         compiler_params=grant(8),
         name="y_faces",
-    )(fields)
-    ylo, yhi = neighbours(y_first, y_last, "gy")
-    x_first, x_last = pl.pallas_call(
+    )(edges, fields)
+    y_near, y_far = swapped(y_near, y_far, "gy")
+    x_near, x_far = pl.pallas_call(
         x_faces_kernel,
         out_shape=(shape((FIELDS, REACH, tall, wide_z), jnp.bfloat16),) * 2,
-        in_specs=[vmem] * 3,
+        in_specs=[smem] + [vmem] * 3,
         out_specs=(vmem,) * 2,
-        scratch_shapes=[pltpu.VMEM((REACH * tall, wide_z), jnp.float32)],
+        scratch_shapes=[pltpu.VMEM((FIELDS, 2, REACH * tall, wide_z), jnp.float32)],
         compiler_params=grant(8),
         name="x_faces",
-    )(fields, ylo, yhi)
-    xlo, xhi = neighbours(x_first, x_last, "gx")
+    )(edges, fields, y_near, y_far)
+    x_near, x_far = swapped(x_near, x_far, "gx")
 
     send_rows = 2 * devices * per
     source_pick, target_pick, chosen = pl.pallas_call(
@@ -587,7 +627,16 @@
         compiler_params=grant(50),
         name="window",
     )(
-        edges, fields, xlo, xhi, ylo, yhi, chosen, source_pick, target_pick, patch_weight
+        edges,
+        fields,
+        x_near,
+        x_far,
+        y_near,
+        y_far,
+        chosen,
+        source_pick,
+        target_pick,
+        patch_weight,
     )
 
     pairs = [(i, i ^ 1) for i in range(n_x)]

time: 161 us -> 159 us (0.988)
  starting transfers between devices: 36.4 us -> 33.7 us
    ppermute x4, starting transfers between devices: 12.8 us -> 8.19 us  [the longest x2 4.26 us: swapped(): lax.ppermute(far_piece, axis, far)]
    all_to_all x1, starting transfers between devices: 13 us -> 14.9 us  [per_device(): lax.all_to_all(send.reshape(devices, 2 * per, EMBED), axes, 0, 0, tiled=T...]
  transfers between devices with their start and end apart: 9 -> 9, of which waited for: 8 -> 6; matrix products, arithmetic and copies ran while one was open for 5% -> 5% of each run, Pallas kernels for 7% -> 8%
where the time goes in v8:
time: 159 us
  blocking collectives  47.8 us (30%)
  waiting for transfers between devices  34.8 us (22%)
  starting transfers between devices  33.7 us (21%)
  Pallas kernels  31.2 us (20%)
  matrix products  8.36 us (5%)
  local copies, waits for them, and re-layouts  1.74 us (1%)
    all_to_all x1, blocking collectives, per_device(): lax.all_to_all(copies, axes, 0, 0, axis_index_groups=groups, tiled=True)  24.3 us
    all_to_all x1, blocking collectives, per_device(): lax.all_to_all(parts.reshape(members, piece, width), axes, 0, 0, axis_ind...  23.5 us
    all_to_all x1, waiting for transfers between devices, per_device(): lax.all_to_all(send.reshape(devices, 2 * per, EMBED), axes, 0, 0, tiled=T...  17.8 us
    all_to_all x1, starting transfers between devices, per_device(): lax.all_to_all(send.reshape(devices, 2 * per, EMBED), axes, 0, 0, tiled=T...  14.9 us
    pallas_call x1, Pallas kernels, per_device(): pl.pallas_call(functools.partial(window_kernel, (wide_x, wide_y, wide_z),...  14.4 us
    pallas_call x1, Pallas kernels, per_device(): pl.pallas_call(functools.partial(trainer_kernel, per), out_shape=(shape((...  9.09 us
    dot_general x2, matrix products, contract_rows(): lax.dot_general(left, right, (((0,), (0,)), ((), ())), preferred_element_...  8.36 us
    ppermute x2, waiting for transfers between devices, swapped(): lax.ppermute(far_piece, axis, far)  7.91 us
  transfers between devices with their start and end apart: 9, of which 6 were waited for; matrix products, arithmetic and copies ran while one was open for 5% of the time, Pallas kernels for 8%

profile of v8, /device:TPU:1, one launch (start us, length us, event | category | flops | bytes accessed | tf_op | source)
XLA Modules:
  0.0 158.6 jit_solution(4096314675932379709)
XLA Ops:
  0.7 0.1 stack.27
  0.8 1.3 copy-done
  2.1 0.7 y_faces.1
  2.8 2.2 %collective-permute-start = (bf16[5,96,128]{2,1,0:T(8,128)(2,1)S(1)}, bf16[5,96,128]{2,1,0:T(8,128)(2,1)S(1)}, u32[]{:S(2)}, u32[]{:S(2)}) collective-permute-start(bf16[5,96,128]{2,1,0:T(8,128)(2,1)S(1)} %get-tuple-element.27), channel_id=1, source_target_pairs={{0,1},{1,0},{2,3},{3,2},{4,5},{5,4},{6,7},{7,6},{8,9},{9,8},{10,11... | collective-permute-start | bytes 368648 | tf_op jit(solution)/shard_map/ppermute | solution.py:519
  5.0 0.7 collective-permute-start.1
  5.7 2.0 %collective-permute-done.y_near_ref = bf16[5,96,128]{2,1,0:T(8,128)(2,1)S(1)} collective-permute-done((bf16[5,96,128]{2,1,0:T(8,128)(2,1)S(1)}, bf16[5,96,128]{2,1,0:T(8,128)(2,1)S(1)}, u32[]{:S(2)}, u32[]{:S(2)}) %collective-permute-start) | collective-permute-done | bytes 122912 | tf_op jit(solution)/shard_map/ppermute | solution.py:519
  7.7 0.7 x_faces.1
  8.4 1.7 %collective-permute-start.2 = (bf16[5,6,40,128]{3,2,1,0:T(8,128)(2,1)S(1)}, bf16[5,6,40,128]{3,2,1,0:T(8,128)(2,1)S(1)}, u32[]{:S(2)}, u32[]{:S(2)}) collective-permute-start(bf16[5,6,40,128]{3,2,1,0:T(8,128)(2,1)S(1)} %get-tuple-element.29), channel_id=1, source_target_pairs={{0,8},{8,0},{16,24},{24,16},{32,40},{40,32},{48,56},{56,48},{64,72... | collective-permute-start | bytes 921608 | tf_op jit(solution)/shard_map/ppermute | solution.py:519
  10.1 3.6 %collective-permute-start.3 = (bf16[5,6,40,128]{3,2,1,0:T(8,128)(2,1)S(1)}, bf16[5,6,40,128]{3,2,1,0:T(8,128)(2,1)S(1)}, u32[]{:S(2)}, u32[]{:S(2)}) collective-permute-start(bf16[5,6,40,128]{3,2,1,0:T(8,128)(2,1)S(1)} %get-tuple-element.30), channel_id=1, source_target_pairs={{8,16},{16,8},{24,32},{32,24},{40,48},{48,40},{56,64},{64,56},{72,... | collective-permute-start | bytes 921608 | tf_op jit(solution)/shard_map/ppermute | solution.py:519
  13.8 0.1 broadcast_in_dim_reshape.6.own_row_ref
  14.1 0.4 slots.1
  14.4 7.9 %collective-permute-done.3.x_far_ref = bf16[5,6,40,128]{3,2,1,0:T(8,128)(2,1)S(1)} collective-permute-done((bf16[5,6,40,128]{3,2,1,0:T(8,128)(2,1)S(1)}, bf16[5,6,40,128]{3,2,1,0:T(8,128)(2,1)S(1)}, u32[]{:S(2)}, u32[]{:S(2)}) %collective-permute-start.3) | collective-permute-done | bytes 307232 | tf_op jit(solution)/shard_map/ppermute | solution.py:519
  22.4 14.4 %window.1 = (f32[5,16,32,128]{3,2,1,0:T(8,128)}, bf16[1280,128]{1,0:T(8,128)(2,1)S(1)}, bf16[1280,128]{1,0:T(8,128)(2,1)}, bf16[1024,512]{1,0:T(8,128)(2,1)}) custom-call(s32[6]{0:T(128)S(1)} %convert_element_type.8.edge_ref, f32[5,16,32,128]{3,2,1,0:T(8,128)} %f_ref.5, bf16[5,6,40,128]{3,2,1,0:T(8,128)(2,1)S(1)} %collective-permute-done.2.x_near_ref, ...), custom_call_target="tpu_custom_call" | custom-call | tf_op jit(solution)/shard_map/window/pallas_call | solution.py:606
  36.8 14.9 %all-to-all-start = ((bf16[128,8,512]{2,1,0:T(8,128)(2,1)}), bf16[128,8,512]{2,1,0:T(8,128)(2,1)S(1)}, u32[]{:S(2)}, u32[]{:S(2)}) async-start(bf16[128,8,512]{2,1,0:T(8,128)(2,1)} %bitcast.8), calls=%async_computation | async-start | bytes 2097152 | tf_op jit(solution)/shard_map/all_to_all | solution.py:648
  51.8 1.3 collective-permute-start.4
  53.1 17.8 %all-to-all-done = bf16[128,8,512]{2,1,0:T(8,128)(2,1)S(1)} async-done(((bf16[128,8,512]{2,1,0:T(8,128)(2,1)}), bf16[128,8,512]{2,1,0:T(8,128)(2,1)S(1)}, u32[]{:S(2)}, u32[]{:S(2)}) %all-to-all-start) | async-done | bytes 1048608 | tf_op jit(solution)/shard_map/all_to_all | solution.py:648
  70.9 9.1 %trainer.1 = (bf16[512,512]{1,0:T(8,128)(2,1)S(1)}, bf16[512,2048]{1,0:T(8,128)(2,1)}, bf16[512,512]{1,0:T(8,128)(2,1)S(1)}, bf16[512,2048]{1,0:T(8,128)(2,1)}, ...) custom-call(bf16[1024,512]{1,0:T(8,128)(2,1)S(1)} %bitcast.25, bf16[512,2048]{1,0:T(8,128)(2,1)} %bitcast.30, ...), custom_call_target="tpu_custom_call" | custom-call | tf_op jit(solution)/shard_map/trainer/pallas_call | solution.py:652
  80.0 4.7 %all-to-all-start.1 = ((bf16[128,8,256]{2,1,0:T(8,128)(2,1)}), bf16[128,8,256]{2,1,0:T(8,128)(2,1)S(1)}, u32[]{:S(2)}, u32[]{:S(2)}) async-start(bf16[128,8,256]{2,1,0:T(8,128)(2,1)} %bitcast.12), calls=%async_computation.1 | async-start | bytes 1048576 | tf_op jit(solution)/shard_map/all_to_all | solution.py:672
  84.7 5.0 %fusion = f32[512,2048]{1,0:T(8,128)} fusion(bf16[512,512]{1,0:T(8,128)(2,1)S(1)} %get-tuple-element.39, bf16[512,2048]{1,0:T(8,128)(2,1)} %get-tuple-element.40), kind=kOutput, calls=%fused_computation | convolution fusion | flops 1073741824 | bytes 6815744 | tf_op jit(solution)/shard_map/dot_general | solution.py:523
  89.8 3.3 %fusion.1 = f32[2048,512]{1,0:T(8,128)} fusion(bf16[512,2048]{1,0:T(8,128)(2,1)S(1)} %copy-done.3, bf16[512,512]{1,0:T(8,128)(2,1)S(1)} %get-tuple-element.42), kind=kOutput, calls=%fused_computation.1 | convolution fusion | flops 1073741824 | bytes 6815744 | tf_op jit(solution)/shard_map/dot_general | solution.py:523
  93.1 5.6 %all-to-all-done.1 = bf16[128,8,256]{2,1,0:T(8,128)(2,1)S(1)} async-done(((bf16[128,8,256]{2,1,0:T(8,128)(2,1)}), bf16[128,8,256]{2,1,0:T(8,128)(2,1)S(1)}, u32[]{:S(2)}, u32[]{:S(2)}) %all-to-all-start.1) | async-done | bytes 524320 | tf_op jit(solution)/shard_map/all_to_all | solution.py:672
  98.7 0.3 gather.1.own_grad_ref
  99.0 1.1 collective-permute-start.5
  100.1 1.0 collective-permute-done.5.other_grad_ref
  101.1 1.1 part.1
  102.2 23.5 %all_to_all.20.parts_ref = bf16[64,40,256]{2,1,0:T(8,128)(2,1)S(1)} all-to-all(bf16[64,40,256]{2,1,0:T(8,128)(2,1)S(1)} %bitcast.22), channel_id=1, replica_groups={{0,1,2,3,4,5,6,7,16,17,18,19,20,21,22,23,32,33,34,35,36,37,38,39,48,49,..., dimensions={0} | all-to-all | bytes 2621440 | tf_op jit(solution)/shard_map/all_to_all | solution.py:699
  125.7 0.2 total.1
  126.0 24.3 %all_to_all.21 = bf16[64,40,256]{2,1,0:T(8,128)(2,1)S(1)} all-to-all(bf16[64,40,256]{2,1,0:T(8,128)(2,1)S(1)} %total.1), channel_id=1, replica_groups={{0,1,2,3,4,5,6,7,16,17,18,19,20,21,22,23,32,33,34,35,36,37,38,39,48,49,..., dimensions={0} | all-to-all | bytes 2621440 | tf_op jit(solution)/shard_map/all_to_all | solution.py:710
  150.3 3.4 %collective-permute-start.6 = (bf16[2560,256]{1,0:T(8,128)(2,1)S(1)}, bf16[2560,256]{1,0:T(8,128)(2,1)S(1)}, u32[]{:S(2)}, u32[]{:S(2)}) collective-permute-start(bf16[2560,256]{1,0:T(8,128)(2,1)S(1)} %bitcast.23), channel_id=1, source_target_pairs={{0,8},{8,0},{16,24},{24,16},{32,40},{40,32},{48,56},{56,48},{64,72... | collective-permute-start | bytes 3932168 | tf_op jit(solution)/shard_map/ppermute | solution.py:712
  153.7 2.1 %spread_own.1.rest_0_ = f32[2560,512]{1,0:T(8,128)} custom-call(s32[6]{0:T(128)S(1)} %convert_element_type.8.edge_ref, bf16[2560,256]{1,0:T(8,128)(2,1)S(1)} %bitcast.24), custom_call_target="tpu_custom_call" | custom-call | tf_op jit(solution)/shard_map/spread_own/pallas_call | solution.py:715
  155.8 0.6 collective-permute-done.6.half_ref
  156.3 2.1 %spread_other.1 = f32[2560,512]{1,0:T(8,128)} custom-call(s32[6]{0:T(128)S(1)} %convert_element_type.8.edge_ref, bf16[2560,256]{1,0:T(8,128)(2,1)S(1)} %collective-permute-done.6.half_ref, f32[2560,512]{1,0:T(8,128)} %spread_own.1.rest_0_), custom_call_target="tpu_custom_call", output_to_operand_aliasing={{}: (2, {})} | custom-call | tf_op jit(solution)/shard_map/spread_other/pallas_call | solution.py:715
  (18 shorter events, 0.2 us)
Async XLA Ops:
  0.6 13.1 %copy-start.5 = (s32[64,1]{0,1:T(1,128)S(1)}, s32[64,1]{0,1:T(1,128)}, u32[]{:S(2)}) copy-start(s32[64,1]{0,1:T(1,128)} %param.10) | copy-start | bytes 772
  0.6 13.4 %copy-start.4 = (s32[2,4,16]{2,1,0:T(4,128)S(1)}, s32[2,4,16]{2,1,0:T(4,128)}, u32[]{:S(2)}) copy-start(s32[2,4,16]{2,1,0:T(4,128)} %param.11) | copy-start | bytes 1540
  0.8 1.3 copy-start
  2.8 4.8 %collective-permute-start = (bf16[5,96,128]{2,1,0:T(8,128)(2,1)S(1)}, bf16[5,96,128]{2,1,0:T(8,128)(2,1)S(1)}, u32[]{:S(2)}, u32[]{:S(2)}) collective-permute-start(bf16[5,96,128]{2,1,0:T(8,128)(2,1)S(1)} %get-tuple-element.27), channel_id=1, source_target_pairs={{0,1},{1,0},{2,3},{3,2},{4,5},{5,4},{6,7},{7,6},{8,9},{9,8},{10,11... | collective-permute-start | bytes 368648 | tf_op jit(solution)/shard_map/ppermute | solution.py:519
  5.0 2.6 %collective-permute-start.1 = (bf16[5,96,128]{2,1,0:T(8,128)(2,1)S(1)}, bf16[5,96,128]{2,1,0:T(8,128)(2,1)S(1)}, u32[]{:S(2)}, u32[]{:S(2)}) collective-permute-start(bf16[5,96,128]{2,1,0:T(8,128)(2,1)S(1)} %get-tuple-element.28), channel_id=1, source_target_pairs={{1,2},{2,1},{3,4},{4,3},{5,6},{6,5},{9,10},{10,9},{11,12},{12,11},... | collective-permute-start | bytes 368648 | tf_op jit(solution)/shard_map/ppermute | solution.py:519
  8.4 6.0 %collective-permute-start.2 = (bf16[5,6,40,128]{3,2,1,0:T(8,128)(2,1)S(1)}, bf16[5,6,40,128]{3,2,1,0:T(8,128)(2,1)S(1)}, u32[]{:S(2)}, u32[]{:S(2)}) collective-permute-start(bf16[5,6,40,128]{3,2,1,0:T(8,128)(2,1)S(1)} %get-tuple-element.29), channel_id=1, source_target_pairs={{0,8},{8,0},{16,24},{24,16},{32,40},{40,32},{48,56},{56,48},{64,72... | collective-permute-start | bytes 921608 | tf_op jit(solution)/shard_map/ppermute | solution.py:519
  10.1 12.2 %collective-permute-start.3 = (bf16[5,6,40,128]{3,2,1,0:T(8,128)(2,1)S(1)}, bf16[5,6,40,128]{3,2,1,0:T(8,128)(2,1)S(1)}, u32[]{:S(2)}, u32[]{:S(2)}) collective-permute-start(bf16[5,6,40,128]{3,2,1,0:T(8,128)(2,1)S(1)} %get-tuple-element.30), channel_id=1, source_target_pairs={{8,16},{16,8},{24,32},{32,24},{40,48},{48,40},{56,64},{64,56},{72,... | collective-permute-start | bytes 921608 | tf_op jit(solution)/shard_map/ppermute | solution.py:519
  36.8 34.1 %copy-start.1 = (f32[1,2048]{1,0:T(1,128)S(1)}, f32[1,2048]{1,0:T(1,128)}, u32[]{:S(2)}) copy-start(f32[1,2048]{1,0:T(1,128)} %b_in_ref.1) | copy-start | bytes 24580
  36.8 34.1 %copy-start.2 = (f32[1,512]{1,0:T(1,128)S(1)}, f32[1,512]{1,0:T(1,128)}, u32[]{:S(2)}) copy-start(f32[1,512]{1,0:T(1,128)} %b_out_ref.1) | copy-start | bytes 6148
  36.8 34.1 %all-to-all-start = ((bf16[128,8,512]{2,1,0:T(8,128)(2,1)}), bf16[128,8,512]{2,1,0:T(8,128)(2,1)S(1)}, u32[]{:S(2)}, u32[]{:S(2)}) async-start(bf16[128,8,512]{2,1,0:T(8,128)(2,1)} %bitcast.8), calls=%async_computation | async-start | bytes 2097152 | tf_op jit(solution)/shard_map/all_to_all | solution.py:648
  51.8 48.3 %collective-permute-start.4 = (bf16[1280,128]{1,0:T(8,128)(2,1)}, bf16[1280,128]{1,0:T(8,128)(2,1)S(1)}, u32[]{:S(2)}, u32[]{:S(2)}) collective-permute-start(bf16[1280,128]{1,0:T(8,128)(2,1)} %get-tuple-element.36), channel_id=1, source_target_pairs={{0,8},{8,0},{16,24},{24,16},{32,40},{40,32},{48,56},{56,48},{64,72... | collective-permute-start | bytes 983048 | tf_op jit(solution)/shard_map/ppermute | solution.py:647
  80.0 18.7 %all-to-all-start.1 = ((bf16[128,8,256]{2,1,0:T(8,128)(2,1)}), bf16[128,8,256]{2,1,0:T(8,128)(2,1)S(1)}, u32[]{:S(2)}, u32[]{:S(2)}) async-start(bf16[128,8,256]{2,1,0:T(8,128)(2,1)} %bitcast.12), calls=%async_computation.1 | async-start | bytes 1048576 | tf_op jit(solution)/shard_map/all_to_all | solution.py:672
  84.7 5.0 %copy-start.3 = (bf16[512,2048]{1,0:T(8,128)(2,1)S(1)}, bf16[512,2048]{1,0:T(8,128)(2,1)}, u32[]{:S(2)}) copy-start(bf16[512,2048]{1,0:T(8,128)(2,1)} %get-tuple-element.41) | copy-start | bytes 6291460
  99.0 2.1 %collective-permute-start.5 = (bf16[128,512]{1,0:T(8,128)(2,1)S(1)}, bf16[128,512]{1,0:T(8,128)(2,1)S(1)}, u32[]{:S(2)}, u32[]{:S(2)}) collective-permute-start(bf16[128,512]{1,0:T(8,128)(2,1)S(1)} %gather.1.own_grad_ref), channel_id=1, source_target_pairs={{0,8},{8,0},{16,24},{24,16},{32,40},{40,32},{48,56},{56,48},{64,72... | collective-permute-start | bytes 393224 | tf_op jit(solution)/shard_map/ppermute | solution.py:684
  150.3 6.1 %collective-permute-start.6 = (bf16[2560,256]{1,0:T(8,128)(2,1)S(1)}, bf16[2560,256]{1,0:T(8,128)(2,1)S(1)}, u32[]{:S(2)}, u32[]{:S(2)}) collective-permute-start(bf16[2560,256]{1,0:T(8,128)(2,1)S(1)} %bitcast.23), channel_id=1, source_target_pairs={{0,8},{8,0},{16,24},{24,16},{32,40},{40,32},{48,56},{56,48},{64,72... | collective-permute-start | bytes 3932168 | tf_op jit(solution)/shard_map/ppermute | solution.py:712

commit v9 on v8

--- a/solution.py
+++ b/solution.py
@@ -121,18 +121,25 @@
         act(near_ref, far_ref)
 
 
-def y_faces_kernel(edge_ref, f_ref, near_ref, far_ref, lines_ref):
-    wide_x, wide_y = f_ref.shape[1], f_ref.shape[2]
+def y_faces_kernel(edge_ref, f_hbm, near_ref, far_ref, tiles_ref, loaded):
+    wide_x, wide_y = f_hbm.shape[1], f_hbm.shape[2]
+    loads = []
+    for end, at in enumerate((0, wide_y - LIFT)):
+        load = pltpu.make_async_copy(
+            f_hbm.at[:, :, at : at + LIFT, :], tiles_ref.at[end], loaded.at[end]
+        )
+        load.start()
+        loads.append(load)
+    for load in loads:
+        load.wait()
 
     def write(first_ref, last_ref):
-        for at, out_ref in ((0, first_ref), (wide_y - LIFT, last_ref)):
+        for end, out_ref in enumerate((first_ref, last_ref)):
             for field in range(FIELDS):
-                for row in range(wide_x):
-                    lines_ref[row * LIFT : (row + 1) * LIFT] = f_ref[field, row, at : at + LIFT]
                 for layer in range(REACH):
-                    line = layer if at == 0 else LIFT - 1 - layer
-                    out_ref[field, layer * wide_x : (layer + 1) * wide_x] = lines_ref[
-                        pl.ds(line, wide_x, stride=LIFT), :
+                    line = layer if end == 0 else LIFT - 1 - layer
+                    out_ref[field, layer * wide_x : (layer + 1) * wide_x] = tiles_ref[
+                        end, field, :, line, :
                     ].astype(jnp.bfloat16)
 
     by_parity(edge_ref[5], write, near_ref, far_ref)
@@ -494,7 +501,7 @@
     half, width = wide_ref.shape[0], half_ref.shape[1]
     core = 1 - edge_ref[4] if other else edge_ref[4]
     begin = core * half
-    pieces = 4
+    pieces = 8
     stores = []
     for piece in range(pieces):
         lines = slice(piece * half // pieces, (piece + 1) * half // pieces)
@@ -570,10 +577,13 @@
     y_near, y_far = pl.pallas_call(
         y_faces_kernel,
         out_shape=(shape((FIELDS, REACH * wide_x, wide_z), jnp.bfloat16),) * 2,
-        in_specs=[smem, vmem],
+        in_specs=[smem, hbm],
         out_specs=(vmem,) * 2,
-        scratch_shapes=[pltpu.VMEM((wide_x * LIFT, wide_z), jnp.float32)],
-        compiler_params=grant(8),
+        scratch_shapes=[
+            pltpu.VMEM((2, FIELDS, wide_x, LIFT, wide_z), jnp.float32),
+            pltpu.SemaphoreType.DMA((2,)),
+        ],
+        compiler_params=grant(61),
         name="y_faces",
     )(edges, fields)
     y_near, y_far = swapped(y_near, y_far, "gy")
@@ -719,7 +729,7 @@
             out_specs=hbm,
             scratch_shapes=[
                 pltpu.VMEM((features // 2, EMBED), jnp.float32),
-                pltpu.SemaphoreType.DMA((4,)),
+                pltpu.SemaphoreType.DMA((8,)),
             ],
             input_output_aliases={2: 0} if other else {},
             compiler_params=grant(8),

time: 159 us -> 161 us (1.013)
  Pallas kernels: 31.2 us -> 33.6 us
    pallas_call x1, Pallas kernels: 0.72 us -> 3.07 us  [per_device(): pl.pallas_call(y_faces_kernel, out_shape=(shape((FIELDS, REACH * wide_x,...]
  transfers between devices with their start and end apart: 9 -> 9, of which waited for: 6 -> 6; matrix products, arithmetic and copies ran while one was open for 5% -> 5% of each run, Pallas kernels for 8% -> 7%
where the time goes in v9:
time: 161 us
  blocking collectives  47.8 us (30%)
  waiting for transfers between devices  34.4 us (21%)
  starting transfers between devices  34 us (21%)
  Pallas kernels  33.6 us (21%)
  matrix products  8.36 us (5%)
    all_to_all x1, blocking collectives, per_device(): lax.all_to_all(copies, axes, 0, 0, axis_index_groups=groups, tiled=True)  24.3 us
    all_to_all x1, blocking collectives, per_device(): lax.all_to_all(parts.reshape(members, piece, width), axes, 0, 0, axis_ind...  23.6 us
    all_to_all x1, waiting for transfers between devices, per_device(): lax.all_to_all(send.reshape(devices, 2 * per, EMBED), axes, 0, 0, tiled=T...  17.8 us
    all_to_all x1, starting transfers between devices, per_device(): lax.all_to_all(send.reshape(devices, 2 * per, EMBED), axes, 0, 0, tiled=T...  15.3 us
    pallas_call x1, Pallas kernels, per_device(): pl.pallas_call(functools.partial(window_kernel, (wide_x, wide_y, wide_z),...  14.4 us
    pallas_call x1, Pallas kernels, per_device(): pl.pallas_call(functools.partial(trainer_kernel, per), out_shape=(shape((...  9.09 us
    dot_general x2, matrix products, contract_rows(): lax.dot_general(left, right, (((0,), (0,)), ((), ())), preferred_element_...  8.36 us
    ppermute x2, waiting for transfers between devices, swapped(): lax.ppermute(far_piece, axis, far)  7.35 us
  transfers between devices with their start and end apart: 9, of which 6 were waited for; matrix products, arithmetic and copies ran while one was open for 5% of the time, Pallas kernels for 7%

profile of v9, /device:TPU:1, one launch (start us, length us, event | category | flops | bytes accessed | tf_op | source)
XLA Modules:
  0.0 160.8 jit_solution(14375099981389702316)
XLA Ops:
  0.8 0.5 convert_element_type.8.edge_ref
  1.3 3.1 %y_faces.1 = (bf16[5,96,128]{2,1,0:T(8,128)(2,1)}, bf16[5,96,128]{2,1,0:T(8,128)(2,1)}) custom-call(s32[6]{0:T(128)} %convert_element_type.8.edge_ref, f32[5,16,32,128]{3,2,1,0:T(8,128)} %f_ref.3), custom_call_target="tpu_custom_call" | custom-call | tf_op jit(solution)/shard_map/y_faces/pallas_call | solution.py:577
  4.4 2.2 %collective-permute-start = (bf16[5,96,128]{2,1,0:T(8,128)(2,1)}, bf16[5,96,128]{2,1,0:T(8,128)(2,1)S(1)}, u32[]{:S(2)}, u32[]{:S(2)}) collective-permute-start(bf16[5,96,128]{2,1,0:T(8,128)(2,1)} %get-tuple-element.27), channel_id=1, source_target_pairs={{0,1},{1,0},{2,3},{3,2},{4,5},{5,4},{6,7},{7,6},{8,9},{9,8},{10,11... | collective-permute-start | bytes 368648 | tf_op jit(solution)/shard_map/ppermute | solution.py:526
  6.6 0.7 collective-permute-start.1
  7.3 2.2 %collective-permute-done.y_near_ref = bf16[5,96,128]{2,1,0:T(8,128)(2,1)S(1)} collective-permute-done((bf16[5,96,128]{2,1,0:T(8,128)(2,1)}, bf16[5,96,128]{2,1,0:T(8,128)(2,1)S(1)}, u32[]{:S(2)}, u32[]{:S(2)}) %collective-permute-start) | collective-permute-done | bytes 122912 | tf_op jit(solution)/shard_map/ppermute | solution.py:526
  9.5 0.7 copy-done.1
  10.1 0.7 x_faces.1
  10.8 1.7 %collective-permute-start.2 = (bf16[5,6,40,128]{3,2,1,0:T(8,128)(2,1)S(1)}, bf16[5,6,40,128]{3,2,1,0:T(8,128)(2,1)S(1)}, u32[]{:S(2)}, u32[]{:S(2)}) collective-permute-start(bf16[5,6,40,128]{3,2,1,0:T(8,128)(2,1)S(1)} %get-tuple-element.29), channel_id=1, source_target_pairs={{0,8},{8,0},{16,24},{24,16},{32,40},{40,32},{48,56},{56,48},{64,72... | collective-permute-start | bytes 921608 | tf_op jit(solution)/shard_map/ppermute | solution.py:526
  12.6 3.6 %collective-permute-start.3 = (bf16[5,6,40,128]{3,2,1,0:T(8,128)(2,1)S(1)}, bf16[5,6,40,128]{3,2,1,0:T(8,128)(2,1)S(1)}, u32[]{:S(2)}, u32[]{:S(2)}) collective-permute-start(bf16[5,6,40,128]{3,2,1,0:T(8,128)(2,1)S(1)} %get-tuple-element.30), channel_id=1, source_target_pairs={{8,16},{16,8},{24,32},{32,24},{40,48},{48,40},{56,64},{64,56},{72,... | collective-permute-start | bytes 921608 | tf_op jit(solution)/shard_map/ppermute | solution.py:526
  16.3 0.1 broadcast_in_dim_reshape.6.own_row_ref
  16.5 0.4 slots.1
  16.9 7.3 %collective-permute-done.3.x_far_ref = bf16[5,6,40,128]{3,2,1,0:T(8,128)(2,1)S(1)} collective-permute-done((bf16[5,6,40,128]{3,2,1,0:T(8,128)(2,1)S(1)}, bf16[5,6,40,128]{3,2,1,0:T(8,128)(2,1)S(1)}, u32[]{:S(2)}, u32[]{:S(2)}) %collective-permute-start.3) | collective-permute-done | bytes 307232 | tf_op jit(solution)/shard_map/ppermute | solution.py:526
  24.2 14.4 %window.1 = (f32[5,16,32,128]{3,2,1,0:T(8,128)}, bf16[1280,128]{1,0:T(8,128)(2,1)S(1)}, bf16[1280,128]{1,0:T(8,128)(2,1)}, bf16[1024,512]{1,0:T(8,128)(2,1)}) custom-call(s32[6]{0:T(128)S(1)} %copy-done.2, f32[5,16,32,128]{3,2,1,0:T(8,128)} %f_ref.3, bf16[5,6,40,128]{3,2,1,0:T(8,128)(2,1)S(1)} %collective-permute-done.2.x_near_ref, ...), custom_call_target="tpu_custom_call" | custom-call | tf_op jit(solution)/shard_map/window/pallas_call | solution.py:616
  38.7 15.3 %all-to-all-start = ((bf16[128,8,512]{2,1,0:T(8,128)(2,1)}), bf16[128,8,512]{2,1,0:T(8,128)(2,1)S(1)}, u32[]{:S(2)}, u32[]{:S(2)}) async-start(bf16[128,8,512]{2,1,0:T(8,128)(2,1)} %bitcast.8), calls=%async_computation | async-start | bytes 2097152 | tf_op jit(solution)/shard_map/all_to_all | solution.py:658
  54.0 1.3 collective-permute-start.4
  55.3 17.8 %all-to-all-done = bf16[128,8,512]{2,1,0:T(8,128)(2,1)S(1)} async-done(((bf16[128,8,512]{2,1,0:T(8,128)(2,1)}), bf16[128,8,512]{2,1,0:T(8,128)(2,1)S(1)}, u32[]{:S(2)}, u32[]{:S(2)}) %all-to-all-start) | async-done | bytes 1048608 | tf_op jit(solution)/shard_map/all_to_all | solution.py:658
  73.1 9.1 %trainer.1 = (bf16[512,512]{1,0:T(8,128)(2,1)S(1)}, bf16[512,2048]{1,0:T(8,128)(2,1)}, bf16[512,512]{1,0:T(8,128)(2,1)S(1)}, bf16[512,2048]{1,0:T(8,128)(2,1)}, ...) custom-call(bf16[1024,512]{1,0:T(8,128)(2,1)S(1)} %bitcast.25, bf16[512,2048]{1,0:T(8,128)(2,1)} %bitcast.30, ...), custom_call_target="tpu_custom_call" | custom-call | tf_op jit(solution)/shard_map/trainer/pallas_call | solution.py:662
  82.2 4.7 %all-to-all-start.1 = ((bf16[128,8,256]{2,1,0:T(8,128)(2,1)}), bf16[128,8,256]{2,1,0:T(8,128)(2,1)S(1)}, u32[]{:S(2)}, u32[]{:S(2)}) async-start(bf16[128,8,256]{2,1,0:T(8,128)(2,1)} %bitcast.12), calls=%async_computation.1 | async-start | bytes 1048576 | tf_op jit(solution)/shard_map/all_to_all | solution.py:682
  86.9 5.0 %fusion = f32[512,2048]{1,0:T(8,128)} fusion(bf16[512,512]{1,0:T(8,128)(2,1)S(1)} %get-tuple-element.39, bf16[512,2048]{1,0:T(8,128)(2,1)} %get-tuple-element.40), kind=kOutput, calls=%fused_computation | convolution fusion | flops 1073741824 | bytes 6815744 | tf_op jit(solution)/shard_map/dot_general | solution.py:530
  92.0 3.3 %fusion.1 = f32[2048,512]{1,0:T(8,128)} fusion(bf16[512,2048]{1,0:T(8,128)(2,1)S(1)} %copy-done.5, bf16[512,512]{1,0:T(8,128)(2,1)S(1)} %get-tuple-element.42), kind=kOutput, calls=%fused_computation.1 | convolution fusion | flops 1073741824 | bytes 6815744 | tf_op jit(solution)/shard_map/dot_general | solution.py:530
  95.3 5.6 %all-to-all-done.1 = bf16[128,8,256]{2,1,0:T(8,128)(2,1)S(1)} async-done(((bf16[128,8,256]{2,1,0:T(8,128)(2,1)}), bf16[128,8,256]{2,1,0:T(8,128)(2,1)S(1)}, u32[]{:S(2)}, u32[]{:S(2)}) %all-to-all-start.1) | async-done | bytes 524320 | tf_op jit(solution)/shard_map/all_to_all | solution.py:682
  100.9 0.3 gather.1.own_grad_ref
  101.2 1.1 collective-permute-start.5
  102.3 1.0 collective-permute-done.5.other_grad_ref
  103.3 1.1 part.1
  104.4 23.6 %all_to_all.20.parts_ref = bf16[64,40,256]{2,1,0:T(8,128)(2,1)S(1)} all-to-all(bf16[64,40,256]{2,1,0:T(8,128)(2,1)S(1)} %bitcast.22), channel_id=1, replica_groups={{0,1,2,3,4,5,6,7,16,17,18,19,20,21,22,23,32,33,34,35,36,37,38,39,48,49,..., dimensions={0} | all-to-all | bytes 2621440 | tf_op jit(solution)/shard_map/all_to_all | solution.py:709
  127.9 0.2 total.1
  128.2 24.3 %all_to_all.21 = bf16[64,40,256]{2,1,0:T(8,128)(2,1)S(1)} all-to-all(bf16[64,40,256]{2,1,0:T(8,128)(2,1)S(1)} %total.1), channel_id=1, replica_groups={{0,1,2,3,4,5,6,7,16,17,18,19,20,21,22,23,32,33,34,35,36,37,38,39,48,49,..., dimensions={0} | all-to-all | bytes 2621440 | tf_op jit(solution)/shard_map/all_to_all | solution.py:720
  152.5 3.4 %collective-permute-start.6 = (bf16[2560,256]{1,0:T(8,128)(2,1)S(1)}, bf16[2560,256]{1,0:T(8,128)(2,1)S(1)}, u32[]{:S(2)}, u32[]{:S(2)}) collective-permute-start(bf16[2560,256]{1,0:T(8,128)(2,1)S(1)} %bitcast.23), channel_id=1, source_target_pairs={{0,8},{8,0},{16,24},{24,16},{32,40},{40,32},{48,56},{56,48},{64,72... | collective-permute-start | bytes 3932168 | tf_op jit(solution)/shard_map/ppermute | solution.py:722
  155.9 2.1 %spread_own.1.rest_0_ = f32[2560,512]{1,0:T(8,128)} custom-call(s32[6]{0:T(128)S(1)} %copy-done.2, bf16[2560,256]{1,0:T(8,128)(2,1)S(1)} %bitcast.24), custom_call_target="tpu_custom_call" | custom-call | tf_op jit(solution)/shard_map/spread_own/pallas_call | solution.py:725
  158.0 0.5 collective-permute-done.6.half_ref
  158.5 2.1 %spread_other.1 = f32[2560,512]{1,0:T(8,128)} custom-call(s32[6]{0:T(128)S(1)} %copy-done.2, bf16[2560,256]{1,0:T(8,128)(2,1)S(1)} %collective-permute-done.6.half_ref, f32[2560,512]{1,0:T(8,128)} %spread_own.1.rest_0_), custom_call_target="tpu_custom_call", output_to_operand_aliasing={{}: (2, {})} | custom-call | tf_op jit(solution)/shard_map/spread_other/pallas_call | solution.py:725
  (22 shorter events, 0.3 us)
Async XLA Ops:
  0.6 8.8 %copy-start = (f32[5,16,32,128]{3,2,1,0:T(8,128)S(1)}, f32[5,16,32,128]{3,2,1,0:T(8,128)}, u32[]{:S(2)}) copy-start(f32[5,16,32,128]{3,2,1,0:T(8,128)} %f_ref.3) | copy-start | bytes 3932164
  0.6 15.5 %copy-start.7 = (s32[64,1]{0,1:T(1,128)S(1)}, s32[64,1]{0,1:T(1,128)}, u32[]{:S(2)}) copy-start(s32[64,1]{0,1:T(1,128)} %param.10) | copy-start | bytes 772
  0.7 15.8 %copy-start.6 = (s32[2,4,16]{2,1,0:T(4,128)S(1)}, s32[2,4,16]{2,1,0:T(4,128)}, u32[]{:S(2)}) copy-start(s32[2,4,16]{2,1,0:T(4,128)} %param.11) | copy-start | bytes 1540
  1.3 22.9 %copy-start.2 = (s32[6]{0:T(128)S(1)}, s32[6]{0:T(128)}, u32[]{:S(2)}) copy-start(s32[6]{0:T(128)} %convert_element_type.8.edge_ref) | copy-start | bytes 76
  4.4 5.1 %collective-permute-start = (bf16[5,96,128]{2,1,0:T(8,128)(2,1)}, bf16[5,96,128]{2,1,0:T(8,128)(2,1)S(1)}, u32[]{:S(2)}, u32[]{:S(2)}) collective-permute-start(bf16[5,96,128]{2,1,0:T(8,128)(2,1)} %get-tuple-element.27), channel_id=1, source_target_pairs={{0,1},{1,0},{2,3},{3,2},{4,5},{5,4},{6,7},{7,6},{8,9},{9,8},{10,11... | collective-permute-start | bytes 368648 | tf_op jit(solution)/shard_map/ppermute | solution.py:526
  6.6 2.8 %collective-permute-start.1 = (bf16[5,96,128]{2,1,0:T(8,128)(2,1)}, bf16[5,96,128]{2,1,0:T(8,128)(2,1)S(1)}, u32[]{:S(2)}, u32[]{:S(2)}) collective-permute-start(bf16[5,96,128]{2,1,0:T(8,128)(2,1)} %get-tuple-element.28), channel_id=1, source_target_pairs={{1,2},{2,1},{3,4},{4,3},{5,6},{6,5},{9,10},{10,9},{11,12},{12,11},... | collective-permute-start | bytes 368648 | tf_op jit(solution)/shard_map/ppermute | solution.py:526
  9.5 0.7 copy-start.1
  10.8 6.0 %collective-permute-start.2 = (bf16[5,6,40,128]{3,2,1,0:T(8,128)(2,1)S(1)}, bf16[5,6,40,128]{3,2,1,0:T(8,128)(2,1)S(1)}, u32[]{:S(2)}, u32[]{:S(2)}) collective-permute-start(bf16[5,6,40,128]{3,2,1,0:T(8,128)(2,1)S(1)} %get-tuple-element.29), channel_id=1, source_target_pairs={{0,8},{8,0},{16,24},{24,16},{32,40},{40,32},{48,56},{56,48},{64,72... | collective-permute-start | bytes 921608 | tf_op jit(solution)/shard_map/ppermute | solution.py:526
  12.6 11.7 %collective-permute-start.3 = (bf16[5,6,40,128]{3,2,1,0:T(8,128)(2,1)S(1)}, bf16[5,6,40,128]{3,2,1,0:T(8,128)(2,1)S(1)}, u32[]{:S(2)}, u32[]{:S(2)}) collective-permute-start(bf16[5,6,40,128]{3,2,1,0:T(8,128)(2,1)S(1)} %get-tuple-element.30), channel_id=1, source_target_pairs={{8,16},{16,8},{24,32},{32,24},{40,48},{48,40},{56,64},{64,56},{72,... | collective-permute-start | bytes 921608 | tf_op jit(solution)/shard_map/ppermute | solution.py:526
  38.7 34.4 %copy-start.3 = (f32[1,2048]{1,0:T(1,128)S(1)}, f32[1,2048]{1,0:T(1,128)}, u32[]{:S(2)}) copy-start(f32[1,2048]{1,0:T(1,128)} %b_in_ref.1) | copy-start | bytes 24580
  38.7 34.4 %copy-start.4 = (f32[1,512]{1,0:T(1,128)S(1)}, f32[1,512]{1,0:T(1,128)}, u32[]{:S(2)}) copy-start(f32[1,512]{1,0:T(1,128)} %b_out_ref.1) | copy-start | bytes 6148
  38.7 34.4 %all-to-all-start = ((bf16[128,8,512]{2,1,0:T(8,128)(2,1)}), bf16[128,8,512]{2,1,0:T(8,128)(2,1)S(1)}, u32[]{:S(2)}, u32[]{:S(2)}) async-start(bf16[128,8,512]{2,1,0:T(8,128)(2,1)} %bitcast.8), calls=%async_computation | async-start | bytes 2097152 | tf_op jit(solution)/shard_map/all_to_all | solution.py:658
  54.0 48.4 %collective-permute-start.4 = (bf16[1280,128]{1,0:T(8,128)(2,1)}, bf16[1280,128]{1,0:T(8,128)(2,1)S(1)}, u32[]{:S(2)}, u32[]{:S(2)}) collective-permute-start(bf16[1280,128]{1,0:T(8,128)(2,1)} %get-tuple-element.36), channel_id=1, source_target_pairs={{0,8},{8,0},{16,24},{24,16},{32,40},{40,32},{48,56},{56,48},{64,72... | collective-permute-start | bytes 983048 | tf_op jit(solution)/shard_map/ppermute | solution.py:657
  82.2 18.7 %all-to-all-start.1 = ((bf16[128,8,256]{2,1,0:T(8,128)(2,1)}), bf16[128,8,256]{2,1,0:T(8,128)(2,1)S(1)}, u32[]{:S(2)}, u32[]{:S(2)}) async-start(bf16[128,8,256]{2,1,0:T(8,128)(2,1)} %bitcast.12), calls=%async_computation.1 | async-start | bytes 1048576 | tf_op jit(solution)/shard_map/all_to_all | solution.py:682
  86.9 5.0 %copy-start.5 = (bf16[512,2048]{1,0:T(8,128)(2,1)S(1)}, bf16[512,2048]{1,0:T(8,128)(2,1)}, u32[]{:S(2)}) copy-start(bf16[512,2048]{1,0:T(8,128)(2,1)} %get-tuple-element.41) | copy-start | bytes 6291460
  101.2 2.1 %collective-permute-start.5 = (bf16[128,512]{1,0:T(8,128)(2,1)S(1)}, bf16[128,512]{1,0:T(8,128)(2,1)S(1)}, u32[]{:S(2)}, u32[]{:S(2)}) collective-permute-start(bf16[128,512]{1,0:T(8,128)(2,1)S(1)} %gather.1.own_grad_ref), channel_id=1, source_target_pairs={{0,8},{8,0},{16,24},{24,16},{32,40},{40,32},{48,56},{56,48},{64,72... | collective-permute-start | bytes 393224 | tf_op jit(solution)/shard_map/ppermute | solution.py:694
  152.5 6.1 %collective-permute-start.6 = (bf16[2560,256]{1,0:T(8,128)(2,1)S(1)}, bf16[2560,256]{1,0:T(8,128)(2,1)S(1)}, u32[]{:S(2)}, u32[]{:S(2)}) collective-permute-start(bf16[2560,256]{1,0:T(8,128)(2,1)S(1)} %bitcast.23), channel_id=1, source_target_pairs={{0,8},{8,0},{16,24},{24,16},{32,40},{40,32},{48,56},{56,48},{64,72... | collective-permute-start | bytes 3932168 | tf_op jit(solution)/shard_map/ppermute | solution.py:722

commit v10 on v8

--- a/solution.py
+++ b/solution.py
@@ -259,7 +259,7 @@
                 dst[field, row, begin:end] = done[field]
             return carry
 
-        lax.fori_loop(least, full_x - least, body, 0, unroll=4)
+        lax.fori_loop(least, full_x - least, body, 0, unroll=8 if least == 2 else 4)
         clear(dst, least)
 
     def last_step(src):
@@ -269,7 +269,7 @@
                 new_ref[field, row - REACH] = done[field]
             return carry
 
-        lax.fori_loop(REACH, top_x, body, 0, unroll=4)
+        lax.fori_loop(REACH, top_x, body, 0, unroll=8)
 
     z_count = wide_z // PATCH
     lane_r = lax.broadcasted_iota(jnp.int32, (wide_z, wide_z), 0)

time: 159 us -> 159 us (level)
  no operation moved by 1% of the time
where the time goes in v10:
time: 159 us; the launch traced here: 158 us
  blocking collectives  47.8 us (30%)
  waiting for transfers between devices  34.8 us (22%)
  starting transfers between devices  33.7 us (21%)
  Pallas kernels  30.8 us (19%)
  matrix products  8.36 us (5%)
  local copies, waits for them, and re-layouts  1.74 us (1%)
    all_to_all x1, blocking collectives, per_device(): lax.all_to_all(copies, axes, 0, 0, axis_index_groups=groups, tiled=True)  24.3 us
    all_to_all x1, blocking collectives, per_device(): lax.all_to_all(parts.reshape(members, piece, width), axes, 0, 0, axis_ind...  23.5 us
    all_to_all x1, waiting for transfers between devices, per_device(): lax.all_to_all(send.reshape(devices, 2 * per, EMBED), axes, 0, 0, tiled=T...  17.8 us
    all_to_all x1, starting transfers between devices, per_device(): lax.all_to_all(send.reshape(devices, 2 * per, EMBED), axes, 0, 0, tiled=T...  14.9 us
    pallas_call x1, Pallas kernels, per_device(): pl.pallas_call(functools.partial(window_kernel, (wide_x, wide_y, wide_z),...  14 us
    pallas_call x1, Pallas kernels, per_device(): pl.pallas_call(functools.partial(trainer_kernel, per), out_shape=(shape((...  9.1 us
    dot_general x2, matrix products, contract_rows(): lax.dot_general(left, right, (((0,), (0,)), ((), ())), preferred_element_...  8.36 us
    ppermute x2, waiting for transfers between devices, swapped(): lax.ppermute(far_piece, axis, far)  7.91 us
  transfers between devices with their start and end apart: 9, of which 6 were waited for; matrix products, arithmetic and copies ran while one was open for 5% of the time, Pallas kernels for 8%

profile of v10, /device:TPU:1, one launch (start us, length us, event | category | flops | bytes accessed | tf_op | source)
XLA Modules:
  0.0 158.2 jit_solution(15236937622564124420)
XLA Ops:
  0.7 0.1 stack.27
  0.8 1.3 copy-done
  2.1 0.7 y_faces.1
  2.8 2.2 %collective-permute-start = (bf16[5,96,128]{2,1,0:T(8,128)(2,1)S(1)}, bf16[5,96,128]{2,1,0:T(8,128)(2,1)S(1)}, u32[]{:S(2)}, u32[]{:S(2)}) collective-permute-start(bf16[5,96,128]{2,1,0:T(8,128)(2,1)S(1)} %get-tuple-element.27), channel_id=1, source_target_pairs={{0,1},{1,0},{2,3},{3,2},{4,5},{5,4},{6,7},{7,6},{8,9},{9,8},{10,11... | collective-permute-start | bytes 368648 | tf_op jit(solution)/shard_map/ppermute | solution.py:519
  5.0 0.7 collective-permute-start.1
  5.7 2.0 %collective-permute-done.y_near_ref = bf16[5,96,128]{2,1,0:T(8,128)(2,1)S(1)} collective-permute-done((bf16[5,96,128]{2,1,0:T(8,128)(2,1)S(1)}, bf16[5,96,128]{2,1,0:T(8,128)(2,1)S(1)}, u32[]{:S(2)}, u32[]{:S(2)}) %collective-permute-start) | collective-permute-done | bytes 122912 | tf_op jit(solution)/shard_map/ppermute | solution.py:519
  7.7 0.7 x_faces.1
  8.4 1.7 %collective-permute-start.2 = (bf16[5,6,40,128]{3,2,1,0:T(8,128)(2,1)S(1)}, bf16[5,6,40,128]{3,2,1,0:T(8,128)(2,1)S(1)}, u32[]{:S(2)}, u32[]{:S(2)}) collective-permute-start(bf16[5,6,40,128]{3,2,1,0:T(8,128)(2,1)S(1)} %get-tuple-element.29), channel_id=1, source_target_pairs={{0,8},{8,0},{16,24},{24,16},{32,40},{40,32},{48,56},{56,48},{64,72... | collective-permute-start | bytes 921608 | tf_op jit(solution)/shard_map/ppermute | solution.py:519
  10.1 3.6 %collective-permute-start.3 = (bf16[5,6,40,128]{3,2,1,0:T(8,128)(2,1)S(1)}, bf16[5,6,40,128]{3,2,1,0:T(8,128)(2,1)S(1)}, u32[]{:S(2)}, u32[]{:S(2)}) collective-permute-start(bf16[5,6,40,128]{3,2,1,0:T(8,128)(2,1)S(1)} %get-tuple-element.30), channel_id=1, source_target_pairs={{8,16},{16,8},{24,32},{32,24},{40,48},{48,40},{56,64},{64,56},{72,... | collective-permute-start | bytes 921608 | tf_op jit(solution)/shard_map/ppermute | solution.py:519
  13.8 0.1 broadcast_in_dim_reshape.6.own_row_ref
  14.1 0.4 slots.1
  14.4 7.9 %collective-permute-done.3.x_far_ref = bf16[5,6,40,128]{3,2,1,0:T(8,128)(2,1)S(1)} collective-permute-done((bf16[5,6,40,128]{3,2,1,0:T(8,128)(2,1)S(1)}, bf16[5,6,40,128]{3,2,1,0:T(8,128)(2,1)S(1)}, u32[]{:S(2)}, u32[]{:S(2)}) %collective-permute-start.3) | collective-permute-done | bytes 307232 | tf_op jit(solution)/shard_map/ppermute | solution.py:519
  22.4 14.0 %window.1 = (f32[5,16,32,128]{3,2,1,0:T(8,128)}, bf16[1280,128]{1,0:T(8,128)(2,1)S(1)}, bf16[1280,128]{1,0:T(8,128)(2,1)}, bf16[1024,512]{1,0:T(8,128)(2,1)}) custom-call(s32[6]{0:T(128)S(1)} %convert_element_type.8.edge_ref, f32[5,16,32,128]{3,2,1,0:T(8,128)} %f_ref.5, bf16[5,6,40,128]{3,2,1,0:T(8,128)(2,1)S(1)} %collective-permute-done.2.x_near_ref, ...), custom_call_target="tpu_custom_call" | custom-call | tf_op jit(solution)/shard_map/window/pallas_call | solution.py:606
  36.4 14.9 %all-to-all-start = ((bf16[128,8,512]{2,1,0:T(8,128)(2,1)}), bf16[128,8,512]{2,1,0:T(8,128)(2,1)S(1)}, u32[]{:S(2)}, u32[]{:S(2)}) async-start(bf16[128,8,512]{2,1,0:T(8,128)(2,1)} %bitcast.8), calls=%async_computation | async-start | bytes 2097152 | tf_op jit(solution)/shard_map/all_to_all | solution.py:648
  51.3 1.3 collective-permute-start.4
  52.7 17.8 %all-to-all-done = bf16[128,8,512]{2,1,0:T(8,128)(2,1)S(1)} async-done(((bf16[128,8,512]{2,1,0:T(8,128)(2,1)}), bf16[128,8,512]{2,1,0:T(8,128)(2,1)S(1)}, u32[]{:S(2)}, u32[]{:S(2)}) %all-to-all-start) | async-done | bytes 1048608 | tf_op jit(solution)/shard_map/all_to_all | solution.py:648
  70.5 9.1 %trainer.1 = (bf16[512,512]{1,0:T(8,128)(2,1)S(1)}, bf16[512,2048]{1,0:T(8,128)(2,1)}, bf16[512,512]{1,0:T(8,128)(2,1)S(1)}, bf16[512,2048]{1,0:T(8,128)(2,1)}, ...) custom-call(bf16[1024,512]{1,0:T(8,128)(2,1)S(1)} %bitcast.25, bf16[512,2048]{1,0:T(8,128)(2,1)} %bitcast.30, ...), custom_call_target="tpu_custom_call" | custom-call | tf_op jit(solution)/shard_map/trainer/pallas_call | solution.py:652
  79.6 4.7 %all-to-all-start.1 = ((bf16[128,8,256]{2,1,0:T(8,128)(2,1)}), bf16[128,8,256]{2,1,0:T(8,128)(2,1)S(1)}, u32[]{:S(2)}, u32[]{:S(2)}) async-start(bf16[128,8,256]{2,1,0:T(8,128)(2,1)} %bitcast.12), calls=%async_computation.1 | async-start | bytes 1048576 | tf_op jit(solution)/shard_map/all_to_all | solution.py:672
  84.3 5.0 %fusion = f32[512,2048]{1,0:T(8,128)} fusion(bf16[512,512]{1,0:T(8,128)(2,1)S(1)} %get-tuple-element.39, bf16[512,2048]{1,0:T(8,128)(2,1)} %get-tuple-element.40), kind=kOutput, calls=%fused_computation | convolution fusion | flops 1073741824 | bytes 6815744 | tf_op jit(solution)/shard_map/dot_general | solution.py:523
  89.3 3.3 %fusion.1 = f32[2048,512]{1,0:T(8,128)} fusion(bf16[512,2048]{1,0:T(8,128)(2,1)S(1)} %copy-done.3, bf16[512,512]{1,0:T(8,128)(2,1)S(1)} %get-tuple-element.42), kind=kOutput, calls=%fused_computation.1 | convolution fusion | flops 1073741824 | bytes 6815744 | tf_op jit(solution)/shard_map/dot_general | solution.py:523
  92.7 5.6 %all-to-all-done.1 = bf16[128,8,256]{2,1,0:T(8,128)(2,1)S(1)} async-done(((bf16[128,8,256]{2,1,0:T(8,128)(2,1)}), bf16[128,8,256]{2,1,0:T(8,128)(2,1)S(1)}, u32[]{:S(2)}, u32[]{:S(2)}) %all-to-all-start.1) | async-done | bytes 524320 | tf_op jit(solution)/shard_map/all_to_all | solution.py:672
  98.2 0.3 gather.1.own_grad_ref
  98.6 1.1 collective-permute-start.5
  99.7 1.0 collective-permute-done.5.other_grad_ref
  100.7 1.1 part.1
  101.8 23.5 %all_to_all.20.parts_ref = bf16[64,40,256]{2,1,0:T(8,128)(2,1)S(1)} all-to-all(bf16[64,40,256]{2,1,0:T(8,128)(2,1)S(1)} %bitcast.22), channel_id=1, replica_groups={{0,1,2,3,4,5,6,7,16,17,18,19,20,21,22,23,32,33,34,35,36,37,38,39,48,49,..., dimensions={0} | all-to-all | bytes 2621440 | tf_op jit(solution)/shard_map/all_to_all | solution.py:699
  125.3 0.2 total.1
  125.5 24.3 %all_to_all.21 = bf16[64,40,256]{2,1,0:T(8,128)(2,1)S(1)} all-to-all(bf16[64,40,256]{2,1,0:T(8,128)(2,1)S(1)} %total.1), channel_id=1, replica_groups={{0,1,2,3,4,5,6,7,16,17,18,19,20,21,22,23,32,33,34,35,36,37,38,39,48,49,..., dimensions={0} | all-to-all | bytes 2621440 | tf_op jit(solution)/shard_map/all_to_all | solution.py:710
  149.8 3.4 %collective-permute-start.6 = (bf16[2560,256]{1,0:T(8,128)(2,1)S(1)}, bf16[2560,256]{1,0:T(8,128)(2,1)S(1)}, u32[]{:S(2)}, u32[]{:S(2)}) collective-permute-start(bf16[2560,256]{1,0:T(8,128)(2,1)S(1)} %bitcast.23), channel_id=1, source_target_pairs={{0,8},{8,0},{16,24},{24,16},{32,40},{40,32},{48,56},{56,48},{64,72... | collective-permute-start | bytes 3932168 | tf_op jit(solution)/shard_map/ppermute | solution.py:712
  153.2 2.1 %spread_own.1.rest_0_ = f32[2560,512]{1,0:T(8,128)} custom-call(s32[6]{0:T(128)S(1)} %convert_element_type.8.edge_ref, bf16[2560,256]{1,0:T(8,128)(2,1)S(1)} %bitcast.24), custom_call_target="tpu_custom_call" | custom-call | tf_op jit(solution)/shard_map/spread_own/pallas_call | solution.py:715
  155.3 0.6 collective-permute-done.6.half_ref
  155.9 2.1 %spread_other.1 = f32[2560,512]{1,0:T(8,128)} custom-call(s32[6]{0:T(128)S(1)} %convert_element_type.8.edge_ref, bf16[2560,256]{1,0:T(8,128)(2,1)S(1)} %collective-permute-done.6.half_ref, f32[2560,512]{1,0:T(8,128)} %spread_own.1.rest_0_), custom_call_target="tpu_custom_call", output_to_operand_aliasing={{}: (2, {})} | custom-call | tf_op jit(solution)/shard_map/spread_other/pallas_call | solution.py:715
  (18 shorter events, 0.2 us)
Async XLA Ops:
  0.6 13.1 %copy-start.5 = (s32[64,1]{0,1:T(1,128)S(1)}, s32[64,1]{0,1:T(1,128)}, u32[]{:S(2)}) copy-start(s32[64,1]{0,1:T(1,128)} %param.10) | copy-start | bytes 772
  0.6 13.4 %copy-start.4 = (s32[2,4,16]{2,1,0:T(4,128)S(1)}, s32[2,4,16]{2,1,0:T(4,128)}, u32[]{:S(2)}) copy-start(s32[2,4,16]{2,1,0:T(4,128)} %param.11) | copy-start | bytes 1540
  0.8 1.3 copy-start
  2.8 4.8 %collective-permute-start = (bf16[5,96,128]{2,1,0:T(8,128)(2,1)S(1)}, bf16[5,96,128]{2,1,0:T(8,128)(2,1)S(1)}, u32[]{:S(2)}, u32[]{:S(2)}) collective-permute-start(bf16[5,96,128]{2,1,0:T(8,128)(2,1)S(1)} %get-tuple-element.27), channel_id=1, source_target_pairs={{0,1},{1,0},{2,3},{3,2},{4,5},{5,4},{6,7},{7,6},{8,9},{9,8},{10,11... | collective-permute-start | bytes 368648 | tf_op jit(solution)/shard_map/ppermute | solution.py:519
  5.0 2.6 %collective-permute-start.1 = (bf16[5,96,128]{2,1,0:T(8,128)(2,1)S(1)}, bf16[5,96,128]{2,1,0:T(8,128)(2,1)S(1)}, u32[]{:S(2)}, u32[]{:S(2)}) collective-permute-start(bf16[5,96,128]{2,1,0:T(8,128)(2,1)S(1)} %get-tuple-element.28), channel_id=1, source_target_pairs={{1,2},{2,1},{3,4},{4,3},{5,6},{6,5},{9,10},{10,9},{11,12},{12,11},... | collective-permute-start | bytes 368648 | tf_op jit(solution)/shard_map/ppermute | solution.py:519
  8.4 6.0 %collective-permute-start.2 = (bf16[5,6,40,128]{3,2,1,0:T(8,128)(2,1)S(1)}, bf16[5,6,40,128]{3,2,1,0:T(8,128)(2,1)S(1)}, u32[]{:S(2)}, u32[]{:S(2)}) collective-permute-start(bf16[5,6,40,128]{3,2,1,0:T(8,128)(2,1)S(1)} %get-tuple-element.29), channel_id=1, source_target_pairs={{0,8},{8,0},{16,24},{24,16},{32,40},{40,32},{48,56},{56,48},{64,72... | collective-permute-start | bytes 921608 | tf_op jit(solution)/shard_map/ppermute | solution.py:519
  10.1 12.2 %collective-permute-start.3 = (bf16[5,6,40,128]{3,2,1,0:T(8,128)(2,1)S(1)}, bf16[5,6,40,128]{3,2,1,0:T(8,128)(2,1)S(1)}, u32[]{:S(2)}, u32[]{:S(2)}) collective-permute-start(bf16[5,6,40,128]{3,2,1,0:T(8,128)(2,1)S(1)} %get-tuple-element.30), channel_id=1, source_target_pairs={{8,16},{16,8},{24,32},{32,24},{40,48},{48,40},{56,64},{64,56},{72,... | collective-permute-start | bytes 921608 | tf_op jit(solution)/shard_map/ppermute | solution.py:519
  36.4 34.1 %copy-start.1 = (f32[1,2048]{1,0:T(1,128)S(1)}, f32[1,2048]{1,0:T(1,128)}, u32[]{:S(2)}) copy-start(f32[1,2048]{1,0:T(1,128)} %b_in_ref.1) | copy-start | bytes 24580
  36.4 34.1 %copy-start.2 = (f32[1,512]{1,0:T(1,128)S(1)}, f32[1,512]{1,0:T(1,128)}, u32[]{:S(2)}) copy-start(f32[1,512]{1,0:T(1,128)} %b_out_ref.1) | copy-start | bytes 6148
  36.4 34.1 %all-to-all-start = ((bf16[128,8,512]{2,1,0:T(8,128)(2,1)}), bf16[128,8,512]{2,1,0:T(8,128)(2,1)S(1)}, u32[]{:S(2)}, u32[]{:S(2)}) async-start(bf16[128,8,512]{2,1,0:T(8,128)(2,1)} %bitcast.8), calls=%async_computation | async-start | bytes 2097152 | tf_op jit(solution)/shard_map/all_to_all | solution.py:648
  51.3 48.3 %collective-permute-start.4 = (bf16[1280,128]{1,0:T(8,128)(2,1)}, bf16[1280,128]{1,0:T(8,128)(2,1)S(1)}, u32[]{:S(2)}, u32[]{:S(2)}) collective-permute-start(bf16[1280,128]{1,0:T(8,128)(2,1)} %get-tuple-element.36), channel_id=1, source_target_pairs={{0,8},{8,0},{16,24},{24,16},{32,40},{40,32},{48,56},{56,48},{64,72... | collective-permute-start | bytes 983048 | tf_op jit(solution)/shard_map/ppermute | solution.py:647
  79.6 18.6 %all-to-all-start.1 = ((bf16[128,8,256]{2,1,0:T(8,128)(2,1)}), bf16[128,8,256]{2,1,0:T(8,128)(2,1)S(1)}, u32[]{:S(2)}, u32[]{:S(2)}) async-start(bf16[128,8,256]{2,1,0:T(8,128)(2,1)} %bitcast.12), calls=%async_computation.1 | async-start | bytes 1048576 | tf_op jit(solution)/shard_map/all_to_all | solution.py:672
  84.3 5.0 %copy-start.3 = (bf16[512,2048]{1,0:T(8,128)(2,1)S(1)}, bf16[512,2048]{1,0:T(8,128)(2,1)}, u32[]{:S(2)}) copy-start(bf16[512,2048]{1,0:T(8,128)(2,1)} %get-tuple-element.41) | copy-start | bytes 6291460
  98.6 2.1 %collective-permute-start.5 = (bf16[128,512]{1,0:T(8,128)(2,1)S(1)}, bf16[128,512]{1,0:T(8,128)(2,1)S(1)}, u32[]{:S(2)}, u32[]{:S(2)}) collective-permute-start(bf16[128,512]{1,0:T(8,128)(2,1)S(1)} %gather.1.own_grad_ref), channel_id=1, source_target_pairs={{0,8},{8,0},{16,24},{24,16},{32,40},{40,32},{48,56},{56,48},{64,72... | collective-permute-start | bytes 393224 | tf_op jit(solution)/shard_map/ppermute | solution.py:684
  149.8 6.1 %collective-permute-start.6 = (bf16[2560,256]{1,0:T(8,128)(2,1)S(1)}, bf16[2560,256]{1,0:T(8,128)(2,1)S(1)}, u32[]{:S(2)}, u32[]{:S(2)}) collective-permute-start(bf16[2560,256]{1,0:T(8,128)(2,1)S(1)} %bitcast.23), channel_id=1, source_target_pairs={{0,8},{8,0},{16,24},{24,16},{32,40},{40,32},{48,56},{56,48},{64,72... | collective-permute-start | bytes 3932168 | tf_op jit(solution)/shard_map/ppermute | solution.py:712
